TPU v7x, 32 devices: a whole 2x2x4 slice. The times are simulated.
32 devices in a mesh: dp: 16 (over z, x, core), tensor: 2 (over y).
Axes of the slice: x: 2, y: 2, z: 4, core: 2. Of those that a mesh axis runs over, the one named last changes fastest.
Arguments:
- hidden: bfloat16 [2, 16384, 768], P(None, ('dp', 'tensor')), may hold values from -6 to 6
- lengths: int32 [2, 16], P(None, 'dp'), may hold values from 256 to 1024, as said below
- cotangent: bfloat16 [2, 16384, 768], P(None, ('dp', 'tensor')), may hold values from -6 to 6
- w_query: bfloat16 [768, 768], P('dp', 'tensor'), may hold values from -0.21875 to 0.21875
- w_key: bfloat16 [768, 768], P('dp', 'tensor'), may hold values from -0.21875 to 0.21875
- w_value: bfloat16 [768, 768], P('dp', 'tensor'), may hold values from -0.21875 to 0.21875
- w_out: bfloat16 [768, 768], P('dp', 'tensor'), may hold values from -1.5 to 1.5
- w_in: bfloat16 [768, 3072], P('dp', 'tensor'), may hold values from -0.21875 to 0.21875
- w_back: bfloat16 [768, 3072], P('dp', 'tensor'), may hold values from -0.109375 to 0.109375
- b_query: float32 [768], replicated, may hold values from -1.75 to 1.75
- b_value: float32 [768], replicated, may hold values from -0.3125 to 0.3125
- b_out: float32 [768], replicated, may hold values from -1.75 to 1.75
- b_in: float32 [3072], replicated, may hold values from -1.75 to 1.75
- b_back: float32 [768], replicated, may hold values from -1.75 to 1.75
- gain_one: float32 [768], replicated, may hold values from 0.5 to 1.5
- shift_one: float32 [768], replicated, may hold values from -1.75 to 1.75
- gain_two: float32 [768], replicated, may hold values from 0.5 to 1.5
- shift_two: float32 [768], replicated, may hold values from -1.75 to 1.75
Outputs:
- output: bfloat16 [2, 16384, 768], P(None, ('dp', 'tensor'))
- grad_hidden: bfloat16 [2, 16384, 768], P(None, ('dp', 'tensor'))
- grad_w_query: float32 [768, 768], P('dp', 'tensor')
- grad_w_key: float32 [768, 768], P('dp', 'tensor')
- grad_w_value: float32 [768, 768], P('dp', 'tensor')
- grad_w_out: float32 [768, 768], P('dp', 'tensor')
- grad_w_in: float32 [768, 3072], P('dp', 'tensor')
- grad_w_back: float32 [768, 3072], P('dp', 'tensor')
- grad_b_query: float32 [768], replicated
- grad_b_value: float32 [768], replicated
- grad_b_out: float32 [768], replicated
- grad_b_in: float32 [3072], replicated
- grad_b_back: float32 [768], replicated
- grad_gain_one: float32 [768], replicated
- grad_shift_one: float32 [768], replicated
- grad_gain_two: float32 [768], replicated
- grad_shift_two: float32 [768], replicated
Inputs may be any that keep to these rules, and one draw needn't show every extreme that they name: `lengths`: the count of real tokens of each sequence; its other slots of 1024 are padding. Some sequence has exactly 1024 and some exactly 256.
All inputs are finite; a program needn't handle non-finite values.
Results may differ from a plain program's by a relative error of at most 0.017.
Values may be sent and summed in bfloat16 or wider, within the bound.
A program may use at most 192 MiB of HBM per device.

v0:
```python
import math

import jax
import jax.numpy as jnp
from jax import lax
from jax.sharding import PartitionSpec as P

DH = 64


def layer_norm(values, gain_vec, shift_vec):
    center = values - jnp.mean(values, axis=-1, keepdims=True)
    spread = jnp.mean(center * center, axis=-1, keepdims=True)
    return center * lax.rsqrt(spread + 1e-05) * gain_vec + shift_vec


def gelu_exact(values):
    return jax.nn.gelu(values, approximate=False)


def product(left_side, right_side):
    return jnp.dot(left_side, right_side, preferred_element_type=jnp.float32)


def contract_last(left_side, right_side):
    return lax.dot_general(
        left_side, right_side, (((1,), (1,)), ((), ())), preferred_element_type=jnp.float32
    )


def contract_first(left_side, right_side):
    return lax.dot_general(
        left_side, right_side, (((0,), (0,)), ((), ())), preferred_element_type=jnp.float32
    )


def fetch_weights(w_query, w_key, w_value, w_out, w_in, w_back):
    return (
        lax.all_gather(w_query, "dp", axis=0, tiled=True),
        lax.all_gather(w_key, "dp", axis=0, tiled=True),
        lax.all_gather(w_value, "dp", axis=0, tiled=True),
        lax.all_gather(w_out, "dp", axis=0, tiled=True),
        lax.all_gather(w_in, "dp", axis=0, tiled=True),
        lax.all_gather(w_back, "dp", axis=0, tiled=True),
    )


def reduce_weights(grad_query, grad_key, grad_value, grad_out, grad_in, grad_back):
    return (
        lax.psum_scatter(grad_query, "dp", scatter_dimension=0, tiled=True),
        lax.psum_scatter(grad_key, "dp", scatter_dimension=0, tiled=True),
        lax.psum_scatter(grad_value, "dp", scatter_dimension=0, tiled=True),
        lax.psum_scatter(grad_out, "dp", scatter_dimension=0, tiled=True),
        lax.psum_scatter(grad_in, "dp", scatter_dimension=0, tiled=True),
        lax.psum_scatter(grad_back, "dp", scatter_dimension=0, tiled=True),
    )


def head_slice(matrix, head_index):
    return lax.dynamic_slice_in_dim(matrix, head_index * DH, DH, 1)


def side_by_side(stacked):
    return jnp.transpose(stacked, (1, 0, 2)).reshape(
        stacked.shape[1], stacked.shape[0] * stacked.shape[2]
    )


def attend_forward(query_rows, key_rows, value_rows, key_live, block_rows):
    seq_len = query_rows.shape[0]
    head_count = query_rows.shape[1] // DH
    scaling = 1.0 / math.sqrt(DH)

    def one_head(head_index):
        query_head = head_slice(query_rows, head_index)
        key_head = head_slice(key_rows, head_index)
        value_head = head_slice(value_rows, head_index)
        outputs = []
        log_parts = []
        for row_first in range(0, seq_len, block_rows):
            query_block = query_head[row_first : row_first + block_rows]
            scores = jnp.where(
                key_live[None, :], contract_last(query_block, key_head) * scaling, -1000000000.0
            )
            row_max = jnp.max(scores, axis=1, keepdims=True)
            exponent = jnp.exp(scores - row_max)
            row_total = jnp.sum(exponent, axis=1, keepdims=True)
            probs_low = (exponent / row_total).astype(jnp.bfloat16)
            outputs.append(product(probs_low, value_head))
            log_parts.append((row_max + jnp.log(row_total))[:, 0])
        return (jnp.concatenate(outputs, 0), jnp.concatenate(log_parts, 0))

    attended, log_sums = lax.map(one_head, jnp.arange(head_count, dtype=jnp.int32))
    return (side_by_side(attended).astype(jnp.bfloat16), log_sums)


def attend_backward(
    query_rows, key_rows, value_rows, log_sums, grad_attended, key_live, block_rows
):
    seq_len = query_rows.shape[0]
    head_count = query_rows.shape[1] // DH
    scaling = 1.0 / math.sqrt(DH)

    def one_head(head_index):
        query_head = head_slice(query_rows, head_index)
        key_head = head_slice(key_rows, head_index)
        value_head = head_slice(value_rows, head_index)
        grad_head = head_slice(grad_attended, head_index)
        log_head = log_sums[head_index]
        grad_keys = jnp.zeros(key_head.shape, jnp.float32)
        grad_values = jnp.zeros(value_head.shape, jnp.float32)
        grad_queries = []
        for row_first in range(0, seq_len, block_rows):
            query_block = query_head[row_first : row_first + block_rows]
            grad_block = grad_head[row_first : row_first + block_rows]
            log_block = log_head[row_first : row_first + block_rows]
            scores = jnp.where(
                key_live[None, :], contract_last(query_block, key_head) * scaling, -1000000000.0
            )
            soft_weights = jnp.exp(scores - log_block[:, None])
            probs_low = soft_weights.astype(jnp.bfloat16)
            grad_probs = contract_last(grad_block, value_head)
            weighted = jnp.sum(soft_weights * grad_probs, axis=1, keepdims=True)
            grad_scores = (soft_weights * (grad_probs - weighted)).astype(jnp.bfloat16)
            grad_queries.append((product(grad_scores, key_head) * scaling).astype(jnp.bfloat16))
            grad_keys = grad_keys + contract_first(grad_scores, query_block) * scaling
            grad_values = grad_values + contract_first(probs_low, grad_block)
        return (
            jnp.concatenate(grad_queries, 0),
            grad_keys.astype(jnp.bfloat16),
            grad_values.astype(jnp.bfloat16),
        )

    grad_query, grad_key, grad_value = lax.map(one_head, jnp.arange(head_count, dtype=jnp.int32))
    return (side_by_side(grad_query), side_by_side(grad_key), side_by_side(grad_value))


def widen_vector(vector, full_size, tensor_index):
    empty_vector = jnp.zeros((full_size,), jnp.float32)
    return lax.dynamic_update_slice(empty_vector, vector, (tensor_index * vector.shape[0],))


def per_device(
    hidden,
    lengths,
    cotangent,
    w_query,
    w_key,
    w_value,
    w_out,
    w_in,
    w_back,
    b_query,
    b_value,
    b_out,
    b_in,
    b_back,
    gain_one,
    shift_one,
    gain_two,
    shift_two,
):
    micro_count = hidden.shape[0]
    local_rows = hidden.shape[1]
    tensor_index = lax.axis_index("tensor")
    model_width = b_query.shape[0]
    inner_width = b_in.shape[0]
    seq_len = local_rows * lax.axis_size("tensor")
    block_rows = min(512, seq_len)
    half_width = w_query.shape[1]
    half_inner = w_in.shape[1]
    query_bias = lax.dynamic_slice_in_dim(b_query, tensor_index * half_width, half_width)
    value_bias = lax.dynamic_slice_in_dim(b_value, tensor_index * half_width, half_width)
    inner_bias = lax.dynamic_slice_in_dim(b_in, tensor_index * half_inner, half_inner)
    row_place = tensor_index * local_rows + jnp.arange(local_rows, dtype=jnp.int32)
    key_place = jnp.arange(seq_len, dtype=jnp.int32)
    outputs = []
    grad_rows = []
    owned_grads = None
    small_sums = None
    for micro_index in range(micro_count):
        gathered = fetch_weights(w_query, w_key, w_value, w_out, w_in, w_back)
        full_query, full_key, full_value, full_out, full_in, full_back = gathered
        length = lengths[micro_index, 0]
        key_live = key_place < length
        rows_in = hidden[micro_index]
        rows_f32 = rows_in.astype(jnp.float32)
        full_rows = lax.all_gather(rows_in, "tensor", axis=0, tiled=True)
        query_rows = (product(full_rows, full_query) + query_bias).astype(jnp.bfloat16)
        key_rows = product(full_rows, full_key).astype(jnp.bfloat16)
        value_rows = (product(full_rows, full_value) + value_bias).astype(jnp.bfloat16)
        attended, log_sums = attend_forward(query_rows, key_rows, value_rows, key_live, block_rows)
        branch_one = lax.psum_scatter(
            contract_last(
                lax.slice_in_dim(attended, 0, local_rows * lax.axis_size("tensor"), axis=0),
                full_out,
            ),
            "tensor",
            scatter_dimension=0,
            tiled=True,
        )
        sum_one = rows_f32 + branch_one + b_out
        normed_one, pull_one = jax.vjp(layer_norm, sum_one, gain_one, shift_one)
        mid_rows = lax.all_gather(normed_one.astype(jnp.bfloat16), "tensor", axis=0, tiled=True)
        hidden_pre = product(mid_rows, full_in) + inner_bias
        active_f32, pull_gelu = jax.vjp(gelu_exact, hidden_pre)
        active = active_f32.astype(jnp.bfloat16)
        branch_two = lax.psum_scatter(
            contract_last(active, full_back).astype(jnp.bfloat16),
            "tensor",
            scatter_dimension=0,
            tiled=True,
        ).astype(jnp.float32)
        sum_two = normed_one + branch_two + b_back
        result, pull_two = jax.vjp(layer_norm, sum_two, gain_two, shift_two)
        outputs.append(result.astype(jnp.bfloat16))
        row_live = (row_place < length).astype(jnp.float32)
        grad_out = cotangent[micro_index].astype(jnp.float32) * row_live[:, None]
        grad_two, grad_gain_two, grad_shift_two = pull_two(grad_out)
        back_rows = lax.all_gather(grad_two.astype(jnp.bfloat16), "tensor", axis=0, tiled=True)
        grad_w_back = contract_first(back_rows, active)
        grad_active = product(back_rows, full_back)
        grad_pre = pull_gelu(grad_active)[0].astype(jnp.bfloat16)
        grad_w_in = contract_first(mid_rows, grad_pre)
        grad_normed = (
            lax.psum_scatter(
                contract_last(grad_pre, full_in).astype(jnp.bfloat16),
                "tensor",
                scatter_dimension=0,
                tiled=True,
            ).astype(jnp.float32)
            + grad_two
        )
        grad_one, grad_gain_one, grad_shift_one = pull_one(grad_normed)
        attn_rows = lax.all_gather(grad_one.astype(jnp.bfloat16), "tensor", axis=0, tiled=True)
        grad_w_out = contract_first(attn_rows, attended)
        grad_attended = product(attn_rows, full_out).astype(jnp.bfloat16)
        grad_query, grad_key, grad_value = attend_backward(
            query_rows, key_rows, value_rows, log_sums, grad_attended, key_live, block_rows
        )
        grad_w_query = contract_first(full_rows, grad_query)
        grad_w_key = contract_first(full_rows, grad_key)
        grad_w_value = contract_first(full_rows, grad_value)
        total_term = contract_last(
            lax.slice_in_dim(grad_query, 0, local_rows * lax.axis_size("tensor"), axis=0),
            full_query,
        )
        total_term = total_term + contract_last(
            lax.slice_in_dim(grad_key, 0, local_rows * lax.axis_size("tensor"), axis=0), full_key
        )
        grad_input = (
            lax.psum_scatter(
                (
                    total_term
                    + contract_last(
                        lax.slice_in_dim(
                            grad_value, 0, local_rows * lax.axis_size("tensor"), axis=0
                        ),
                        full_value,
                    )
                ).astype(jnp.bfloat16),
                "tensor",
                scatter_dimension=0,
                tiled=True,
            ).astype(jnp.float32)
            + grad_one
        )
        grad_rows.append(grad_input.astype(jnp.bfloat16))
        summed = reduce_weights(
            grad_w_query, grad_w_key, grad_w_value, grad_w_out, grad_w_in, grad_w_back
        )
        owned_grads = summed if owned_grads is None else jax.tree.map(jnp.add, owned_grads, summed)
        vectors = (
            jnp.sum(grad_query.astype(jnp.float32), axis=0),
            jnp.sum(grad_value.astype(jnp.float32), axis=0),
            jnp.sum(grad_one, axis=0),
            jnp.sum(grad_pre.astype(jnp.float32), axis=0),
            jnp.sum(grad_two, axis=0),
            grad_gain_one,
            grad_shift_one,
            grad_gain_two,
            grad_shift_two,
        )
        small_sums = vectors if small_sums is None else jax.tree.map(jnp.add, small_sums, vectors)
    output_rows = jnp.stack(outputs, 0)
    grad_hidden_rows = jnp.stack(grad_rows, 0)
    small_vectors = (
        widen_vector(small_sums[0], model_width, tensor_index),
        widen_vector(small_sums[1], model_width, tensor_index),
        small_sums[2],
        widen_vector(small_sums[3], inner_width, tensor_index),
        small_sums[4],
        small_sums[5],
        small_sums[6],
        small_sums[7],
        small_sums[8],
    )
    totals = lax.psum(
        (
            small_vectors[0],
            small_vectors[1],
            small_vectors[2],
            small_vectors[3],
            small_vectors[4],
            small_vectors[5],
            small_vectors[6],
            small_vectors[7],
            small_vectors[8],
        ),
        ("dp", "tensor"),
    )
    return (
        output_rows,
        grad_hidden_rows,
        owned_grads[0],
        owned_grads[1],
        owned_grads[2],
        owned_grads[3],
        owned_grads[4],
        owned_grads[5],
        totals[0],
        totals[1],
        totals[2],
        totals[3],
        totals[4],
        totals[5],
        totals[6],
        totals[7],
        totals[8],
    )


def solution(mesh):
    return jax.shard_map(
        per_device,
        mesh=mesh,
        in_specs=(
            P(None, ("dp", "tensor"), None),
            P(None, "dp"),
            P(None, ("dp", "tensor"), None),
            P("dp", "tensor"),
            P("dp", "tensor"),
            P("dp", "tensor"),
            P("dp", "tensor"),
            P("dp", "tensor"),
            P("dp", "tensor"),
            P(),
            P(),
            P(),
            P(),
            P(),
            P(),
            P(),
            P(),
            P(),
        ),
        out_specs=(
            P(None, ("dp", "tensor"), None),
            P(None, ("dp", "tensor"), None),
            P("dp", "tensor"),
            P("dp", "tensor"),
            P("dp", "tensor"),
            P("dp", "tensor"),
            P("dp", "tensor"),
            P("dp", "tensor"),
            P(),
            P(),
            P(),
            P(),
            P(),
            P(),
            P(),
            P(),
            P(),
        ),
        check_vma=False,
    )
```

profile of v0, /device:TPU:0, one launch (start us, length us, event | category | flops | bytes accessed | tf_op | source)
XLA Modules:
  0.0 1236.3 jit_solution(3482107749326957179)
XLA Ops:
  12.3 24.8 %all_gather.49 = bf16[768,384]{1,0:T(8,128)(2,1)S(1)} all-gather(bf16[48,384]{1,0:T(8,128)(2,1)S(1)} %copy-done.51), channel_id=1, replica_groups=mesh['dp'=16,'tensor'=2] {'dp'}, dimensions={0}, use_global_device_ids=true | all-gather | bytes 626688 | tf_op jit(solution)/shard_map/all_gather | solution.py:39
  37.1 19.0 %all_gather.50 = bf16[768,384]{1,0:T(8,128)(2,1)S(1)} all-gather(bf16[48,384]{1,0:T(8,128)(2,1)S(1)} %copy-done.52), channel_id=1, replica_groups=mesh['dp'=16,'tensor'=2] {'dp'}, dimensions={0}, use_global_device_ids=true | all-gather | bytes 626688 | tf_op jit(solution)/shard_map/all_gather | solution.py:40
  56.2 20.4 %all_gather.51 = bf16[768,384]{1,0:T(8,128)(2,1)S(1)} all-gather(bf16[48,384]{1,0:T(8,128)(2,1)S(1)} %copy-done.53), channel_id=1, replica_groups=mesh['dp'=16,'tensor'=2] {'dp'}, dimensions={0}, use_global_device_ids=true | all-gather | bytes 626688 | tf_op jit(solution)/shard_map/all_gather | solution.py:41
  76.6 20.4 %all_gather.52 = bf16[768,384]{1,0:T(8,128)(2,1)} all-gather(bf16[48,384]{1,0:T(8,128)(2,1)S(1)} %copy-done.54), channel_id=1, replica_groups=mesh['dp'=16,'tensor'=2] {'dp'}, dimensions={0}, use_global_device_ids=true | all-gather | bytes 626688 | tf_op jit(solution)/shard_map/all_gather | solution.py:42
  103.2 60.0 %while.56 = (s32[]{:T(128)}, bf16[6,1024,64]{1,2,0:T(8,128)(2,1)}, f32[6,1024]{1,0:T(8,128)}, s32[6]{0:T(128)S(1)}, bf16[1024,384]{1,0:T(8,128)(2,1)S(1)}, /*ind...) while((s32[]{:T(128)}, bf16[6,1024,64]{1,2,0:T(8,128)(2,1)}, ...), condition=%wide.region_5.6_spmd.clone, body=%wide.region_0.5_spmd.clone.sunk | while | flops 281281536 | bytes 14344927 | solution.py:93
  173.7 35.8 %while.57 = (s32[]{:T(128)}, bf16[6,1024,64]{1,2,0:T(8,128)(2,1)S(1)}, f32[6,1024]{1,0:T(8,128)S(1)}, s32[6]{0:T(128)S(1)}, bf16[1024,384]{1,0:T(8,128)(2,1)S(1)...) while((s32[]{:T(128)}, ...), condition=%wide.region_17.18_spmd.clone, body=%wide.region_12.0_spmd.clone.sunk | while | flops 281281536 | bytes 14344927 | solution.py:93
  214.5 41.4 %reduce-scatter.25.cloned.1.call-done = f32[512,768]{1,0:T(8,128)} async-done(((f32[1024,768]{1,0:T(8,128)}), f32[512,768]{1,0:T(8,128)}) %reduce-scatter.25.cloned.1.call-update) | async-done | bytes 1572880 | tf_op jit(solution)/shard_map/reduce_scatter | solution.py:193
  263.3 25.5 %all-gather.19.cloned.1.call-done = bf16[1024,768]{1,0:T(8,128)(2,1)} async-done(((bf16[512,768]{1,0:T(8,128)(2,1)}), bf16[1024,768]{1,0:T(8,128)(2,1)}) %all-gather.19.cloned.1.call-update) | async-done | bytes 1572880 | tf_op jit(solution)/shard_map/all_gather | solution.py:204
  296.2 21.7 %all-gather.13.cloned.1.call-done = bf16[1024,768]{1,0:T(8,128)(2,1)} async-done(((bf16[512,768]{1,0:T(8,128)(2,1)}), bf16[1024,768]{1,0:T(8,128)(2,1)}) %all-gather.13.cloned.1.call-update) | async-done | bytes 1572880 | tf_op jit(solution)/shard_map/all_gather | solution.py:204
  317.9 32.9 %multiply_convert_fusion.5 = (bf16[1024,1536]{1,0:T(8,128)(2,1)}, f32[1024,1536]{1,0:T(8,128)}, bf16[1024,1536]{1,0:T(8,128)(2,1)}, f32[1024,1536]{1,0:T(8,128)}, f32[1024,1536]{1,0:T(8,128)}) fusion(f32[1536]{0:T(1024)S(1)} %dynamic_slice.72, f32[1024,1536]{1,0:T(8,128)} %fusion.246, bf16[1024,768]{1,0:T(8,128)(2,1)} %all-gather.13.cloned.1.call-done, ...), kind=kOutput, calls=%fused_computation.195 | convolution fusion | flops 2623537152 | bytes 35395584 | tf_op jit(solution)/shard_map/dot_general | solution.py:22
  393.8 28.9 %reduce-scatter.27.cloned.1.call-done = bf16[512,768]{1,0:T(8,128)(2,1)} async-done(((bf16[1024,768]{1,0:T(8,128)(2,1)}), bf16[512,768]{1,0:T(8,128)(2,1)}) %reduce-scatter.27.cloned.1.call-update) | async-done | bytes 786448 | tf_op jit(solution)/shard_map/reduce_scatter | solution.py:208
  436.4 24.8 %all-gather.25.cloned.1.call-done = bf16[1024,768]{1,0:T(8,128)(2,1)} async-done(((bf16[512,768]{1,0:T(8,128)(2,1)}), bf16[1024,768]{1,0:T(8,128)(2,1)}) %all-gather.25.cloned.1.call-update) | async-done | bytes 1572880 | tf_op jit(solution)/shard_map/all_gather | solution.py:220
  468.6 21.2 %all-gather.21.cloned.1.call-done = bf16[1024,768]{1,0:T(8,128)(2,1)} async-done(((bf16[512,768]{1,0:T(8,128)(2,1)}), bf16[1024,768]{1,0:T(8,128)(2,1)}) %all-gather.21.cloned.1.call-update) | async-done | bytes 1572880 | tf_op jit(solution)/shard_map/all_gather | solution.py:220
  519.4 19.4 %reduce-scatter.33.cloned.1.call-done = bf16[512,768]{1,0:T(8,128)(2,1)} async-done(((bf16[1024,768]{1,0:T(8,128)(2,1)}), bf16[512,768]{1,0:T(8,128)(2,1)}) %reduce-scatter.33.cloned.1.call-update) | async-done | bytes 786448 | tf_op jit(solution)/shard_map/reduce_scatter | solution.py:226
  538.8 28.8 %reduce-scatter.29.cloned.1.call-done = bf16[512,768]{1,0:T(8,128)(2,1)} async-done(((bf16[1024,768]{1,0:T(8,128)(2,1)}), bf16[512,768]{1,0:T(8,128)(2,1)}) %reduce-scatter.29.cloned.1.call-update) | async-done | bytes 786448 | tf_op jit(solution)/shard_map/reduce_scatter | solution.py:226
  577.9 26.1 %all-gather.23.cloned.1.call-done = bf16[1024,768]{1,0:T(8,128)(2,1)} async-done(((bf16[512,768]{1,0:T(8,128)(2,1)}), bf16[1024,768]{1,0:T(8,128)(2,1)}) %all-gather.23.cloned.1.call-update) | async-done | bytes 1572880 | tf_op jit(solution)/shard_map/all_gather | solution.py:235
  608.9 82.4 %while.58 = (s32[]{:T(128)}, bf16[6,1024,64]{1,2,0:T(8,128)(2,1)S(1)}, bf16[6,1024,64]{1,2,0:T(8,128)(2,1)}, bf16[6,1024,64]{1,2,0:T(8,128)(2,1)S(1)}, s32[6]{0:...) while((s32[]{:T(128)}, ...), condition=%wide.region_32.33_spmd.clone, body=%wide.region_29.32_spmd.clone.sunk | while | flops 681246720 | bytes 38957408 | solution.py:134
  703.9 88.5 %while.59 = (s32[]{:T(128)}, bf16[6,1024,64]{1,2,0:T(8,128)(2,1)}, bf16[6,1024,64]{1,2,0:T(8,128)(2,1)}, bf16[6,1024,64]{1,2,0:T(8,128)(2,1)}, s32[6]{0:T(128)S(...) while((s32[]{:T(128)}, bf16[6,1024,64]{1,2,0:T(8,128)(2,1)}, ...), condition=%wide.region_42.43_spmd.clone, body=%wide.region_39.42_spmd.clone.sunk | while | flops 681246720 | bytes 38957408 | solution.py:134
  851.0 40.5 %all-reduce = (f32[768]{0:T(1024)}, f32[768]{0:T(1024)}, f32[768]{0:T(1024)}, f32[3072]{0:T(1024)}, f32[768]{0:T(1024)}, /*index=5*/f32[768]{0:T(1024)}, f32[768]{0:T(1024)}, f32[768]{0:T(1024)}, f32[768]{0:T(1024)}) all-reduce(f32[768]{0:T(1024)S(1)} %dynamic_update_slice.42, ...), channel_id=1, replica_groups=mesh['dp'=16,'tensor'=2] {'dp','tensor'}, use_global_device_ids=true, to_apply=%region_58.59 | all-reduce | flops 9216 | bytes 73728 | tf_op jit(solution)/shard_map/psum | solution.py:298
  896.5 51.9 %reduce-scatter.47.cloned.1.call-done = f32[48,384]{1,0:T(8,128)} async-done(((f32[768,384]{1,0:T(8,128)}), f32[48,384]{1,0:T(8,128)}) %reduce-scatter.47.cloned.1.call-update) | async-done | bytes 73744
  948.4 61.1 %reduce-scatter.43.cloned.1.call-done = f32[48,384]{1,0:T(8,128)} async-done(((f32[768,384]{1,0:T(8,128)}), f32[48,384]{1,0:T(8,128)}) %reduce-scatter.43.cloned.1.call-update) | async-done | bytes 73744
  1009.6 61.1 %reduce-scatter.45.cloned.1.call-done = f32[48,384]{1,0:T(8,128)} async-done(((f32[768,384]{1,0:T(8,128)}), f32[48,384]{1,0:T(8,128)}) %reduce-scatter.45.cloned.1.call-update) | async-done | bytes 73744
  1070.7 79.0 %reduce-scatter.41.cloned.1.call-done = f32[48,1536]{1,0:T(8,128)} async-done(((f32[768,1536]{1,0:T(8,128)}), f32[48,1536]{1,0:T(8,128)}) %reduce-scatter.41.cloned.1.call-update) | async-done | bytes 294928 | tf_op jit(solution)/shard_map/reduce_scatter | solution.py:55
  1149.7 79.4 %reduce-scatter.39.cloned.1.call-done = f32[48,1536]{1,0:T(8,128)} async-done(((f32[768,1536]{1,0:T(8,128)}), f32[48,1536]{1,0:T(8,128)}) %reduce-scatter.39.cloned.1.call-update) | async-done | bytes 294928 | tf_op jit(solution)/shard_map/reduce_scatter | solution.py:54
  (696 shorter events, 449.7 us)
Async XLA Ops:
  8.1 89.0 %all-gather.29.cloned.1.call-start = ((), (), s32[]{:S(2)}) async-start(), calls=%async_computation.30 | async-start | bytes 2359296 | tf_op jit(solution)/shard_map/all_gather | solution.py:188
  10.8 157.5 %all-gather.31.cloned.1.call-start = ((), (), s32[]{:S(2)}) async-start(), calls=%async_computation.31 | async-start | bytes 2359296 | tf_op jit(solution)/shard_map/all_gather | solution.py:188
  11.5 203.0 %reduce-scatter.21.cloned.1.call-start = ((), (), s32[]{:S(2)}) async-start(), calls=%async_computation.14 | async-start | bytes 4718592 | tf_op jit(solution)/shard_map/reduce_scatter | solution.py:193
  168.1 87.9 %reduce-scatter.25.cloned.1.call-start = ((), (), s32[]{:S(2)}) async-start(), calls=%async_computation.19 | async-start | bytes 4718592 | tf_op jit(solution)/shard_map/reduce_scatter | solution.py:193
  213.9 49.5 %all-gather.15.cloned.1.call-start = ((), (), s32[]{:S(2)}) async-start(), calls=%async_computation.16 | async-start | bytes 2506752 | tf_op jit(solution)/shard_map/all_gather | solution.py:43
  214.4 74.3 %all-gather.19.cloned.1.call-start = ((), (), s32[]{:S(2)}) async-start(), calls=%async_computation.20 | async-start | bytes 2359296 | tf_op jit(solution)/shard_map/all_gather | solution.py:204
  261.7 56.2 %all-gather.13.cloned.1.call-start = ((), (), s32[]{:S(2)}) async-start(), calls=%async_computation.15 | async-start | bytes 2359296 | tf_op jit(solution)/shard_map/all_gather | solution.py:204
  262.2 100.6 %all-gather.17.cloned.1.call-start = ((), (), s32[]{:S(2)}) async-start(), calls=%async_computation.17 | async-start | bytes 2506752 | tf_op jit(solution)/shard_map/all_gather | solution.py:44
  263.0 130.8 %reduce-scatter.23.cloned.1.call-start = ((), (), s32[]{:S(2)}) async-start(), calls=%async_computation.18 | async-start | bytes 2359296 | tf_op jit(solution)/shard_map/reduce_scatter | solution.py:208
  369.2 53.5 %reduce-scatter.27.cloned.1.call-start = ((), (), s32[]{:S(2)}) async-start(), calls=%async_computation.21 | async-start | bytes 2359296 | tf_op jit(solution)/shard_map/reduce_scatter | solution.py:208
  375.7 85.5 %all-gather.25.cloned.1.call-start = ((), (), s32[]{:S(2)}) async-start(), calls=%async_computation.26 | async-start | bytes 2359296 | tf_op jit(solution)/shard_map/all_gather | solution.py:220
  433.8 56.0 %all-gather.21.cloned.1.call-start = ((), (), s32[]{:S(2)}) async-start(), calls=%async_computation.22 | async-start | bytes 2359296 | tf_op jit(solution)/shard_map/all_gather | solution.py:220
  436.4 102.4 %reduce-scatter.33.cloned.1.call-start = ((), (), s32[]{:S(2)}) async-start(), calls=%async_computation.27 | async-start | bytes 2359296 | tf_op jit(solution)/shard_map/reduce_scatter | solution.py:226
  512.7 54.9 %reduce-scatter.29.cloned.1.call-start = ((), (), s32[]{:S(2)}) async-start(), calls=%async_computation.23 | async-start | bytes 2359296 | tf_op jit(solution)/shard_map/reduce_scatter | solution.py:226
  519.2 84.8 %all-gather.23.cloned.1.call-start = ((), (), s32[]{:S(2)}) async-start(), calls=%async_computation.24 | async-start | bytes 2359296 | tf_op jit(solution)/shard_map/all_gather | solution.py:235
  576.6 121.0 %all-gather.27.cloned.1.call-start = ((), (), s32[]{:S(2)}) async-start(), calls=%async_computation.28 | async-start | bytes 2359296 | tf_op jit(solution)/shard_map/all_gather | solution.py:235
  577.8 313.7 %reduce-scatter.31.cloned.1.call-start = ((), (), s32[]{:S(2)}) async-start(), calls=%async_computation.25 | async-start | bytes 2359296 | tf_op jit(solution)/shard_map/reduce_scatter | solution.py:252
  697.3 196.4 %reduce-scatter.35.cloned.1.call-start = ((), (), s32[]{:S(2)}) async-start(), calls=%async_computation.29 | async-start | bytes 2359296 | tf_op jit(solution)/shard_map/reduce_scatter | solution.py:252
  798.4 98.1 %reduce-scatter.37.cloned.1.call-start = ((), (), s32[]{:S(2)}) async-start(), calls=%async_computation.32 | async-start | bytes 1253376 | tf_op jit(solution)/shard_map/reduce_scatter | solution.py:53
  803.2 145.2 %reduce-scatter.47.cloned.1.call-start = ((), (), s32[]{:S(2)}) async-start(), calls=%async_computation.37 | async-start | bytes 1253376
  811.0 198.5 %reduce-scatter.43.cloned.1.call-start = ((), (), s32[]{:S(2)}) async-start(), calls=%async_computation.35 | async-start | bytes 1253376
  818.1 252.6 %reduce-scatter.45.cloned.1.call-start = ((), (), s32[]{:S(2)}) async-start(), calls=%async_computation.36 | async-start | bytes 1253376
  825.2 324.4 %reduce-scatter.41.cloned.1.call-start = ((), (), s32[]{:S(2)}) async-start(), calls=%async_computation.34 | async-start | bytes 5013504 | tf_op jit(solution)/shard_map/reduce_scatter | solution.py:55
  834.7 394.3 %reduce-scatter.39.cloned.1.call-start = ((), (), s32[]{:S(2)}) async-start(), calls=%async_computation.33 | async-start | bytes 5013504 | tf_op jit(solution)/shard_map/reduce_scatter | solution.py:54
  (101 other events, 1187.4 us)
Sparse Core Ops, SparseCore 0:
  11.0 29.8 all-gather.28
  43.1 27.2 all-gather.30
  168.2 41.9 reduce-scatter.20
  214.0 41.9 reduce-scatter.24
  434.0 27.2 all-gather.24
  462.6 27.1 all-gather.20
  576.8 27.1 all-gather.22
  606.1 27.2 all-gather.26
  697.4 26.0 reduce-scatter.30
  798.6 26.0 reduce-scatter.34
  828.9 58.2 reduce-scatter.36
  891.3 57.1 reduce-scatter.46
  952.6 56.9 reduce-scatter.42
  1013.6 57.0 reduce-scatter.44
  1075.0 74.6 reduce-scatter.40
  1154.4 74.5 reduce-scatter.38
Sparse Core Ops, SparseCore 1:
  216.6 41.0 all-gather.14
  261.7 27.0 all-gather.18
  290.8 27.0 all-gather.12
  320.2 42.6 all-gather.16
  369.3 24.4 reduce-scatter.22
  396.7 25.9 reduce-scatter.26
  512.7 25.9 reduce-scatter.32
  541.5 25.9 reduce-scatter.28
where the time goes:
time: 1250 us; the launch traced here: 1240 us
  waiting for transfers between devices  601 us (48%)
  matrix products  309 us (25%)
  blocking collectives  125 us (10%)
  other arithmetic  78.2 us (6%)
  local copies, waits for them, and re-layouts  61.1 us (5%)
  loops' own time  41.5 us (3%)
  between operations  16.8 us (1%)
    unnamed x27, waiting for transfers between devices  177 us
    dot_general x60, matrix products, product(): return jnp.dot(left_side, right_side, preferred_element_type=jnp.float32)  121 us
    dot_general x84, matrix products, contract_last(): lax.dot_general(left_side, right_side, (((1,), (1,)), ((), ())), preferre...  120 us
    reduce_scatter x1, waiting for transfers between devices, reduce_weights(): lax.psum_scatter(grad_in, 'dp', scatter_dimension=0, tiled=True)  79.4 us
    reduce_scatter x1, waiting for transfers between devices, reduce_weights(): lax.psum_scatter(grad_back, 'dp', scatter_dimension=0, tiled=True)  79 us
    dot_general x60, matrix products, contract_first(): lax.dot_general(left_side, right_side, (((0,), (0,)), ((), ())), preferre...  68.3 us
    reduce_scatter x2, waiting for transfers between devices, per_device(): lax.psum_scatter(contract_last(grad_pre, full_in).astype(jnp.bfloat16), '...  48.1 us
    all_gather x2, waiting for transfers between devices, per_device(): lax.all_gather(normed_one.astype(jnp.bfloat16), 'tensor', axis=0, tiled=T...  47.1 us
  transfers between devices with their start and end apart: 24, of which 16 were waited for; matrix products, arithmetic and copies ran while one was open for 32% of the time, Pallas kernels for 0%

commit v1 on v0

v1 whole, which is shorter than its diff:
```python
import functools
import math

import jax
import jax.numpy as jnp
from jax import lax
from jax.experimental import pallas as pl
from jax.experimental.pallas import tpu as pltpu
from jax.sharding import PartitionSpec as P

F32, BF16 = jnp.float32, jnp.bfloat16
DH = 64

def nt(a, b): return lax.dot_general(a, b, (((1,), (1,)), ((), ())), preferred_element_type=F32)
def nn(a, b): return lax.dot_general(a, b, (((1,), (0,)), ((), ())), preferred_element_type=F32)
def tn(a, b): return lax.dot_general(a, b, (((0,), (0,)), ((), ())), preferred_element_type=F32)

def split3(v):
    hi = v.astype(BF16).astype(F32); r = v - hi
    mid = r.astype(BF16).astype(F32)
    return hi, mid, r - mid

def fwd_kernel(bq, len_ref, q_ref, k_ref, v_ref, o_ref, lse_ref):
    rows = q_ref.shape[0]
    n = len_ref[0]
    lane = lax.broadcasted_iota(jnp.int32, (1, 128), 1)
    krow = lax.broadcasted_iota(jnp.int32, (rows, 1), 0)
    kbias = jnp.where((krow + len_ref[1]) % rows < n, 0.0, -1e9)
    k = k_ref[...].astype(F32)
    v = v_ref[...]
    kas = []
    for h in range(2):
        own = lane // DH == h
        kas.append(jnp.where(own, k, jnp.where(lane == DH * (1 - h), kbias, 0.0)).astype(BF16))
    for qb in range(0, rows, bq):
        q = q_ref[qb : qb + bq].astype(F32)
        os_, ls = [], []
        for h in range(2):
            own = lane // DH == h
            qa = jnp.where(own, q, jnp.where(lane == DH * (1 - h), 1.0, 0.0)).astype(BF16)
            s = nt(qa, kas[h])
            m = jnp.max(s, axis=1, keepdims=True)
            p = jnp.exp(s - m)
            l = jnp.sum(p, axis=1, keepdims=True)
            os_.append(nn(p.astype(BF16), v) * (1.0 / l))
            ls.append(m + jnp.log(l))
        first = lane < DH
        o_ref[qb : qb + bq] = jnp.where(first, os_[0], os_[1]).astype(BF16)
        lse_ref[qb : qb + bq] = jnp.where(first, ls[1], ls[0])

def attend_forward(length, q, k, v, bq=256):
    rows, width = q.shape
    spec = pl.BlockSpec((rows, 128), lambda i: (0, i))
    return pl.pallas_call(functools.partial(fwd_kernel, bq), grid=(width // 128,),
        in_specs=[pl.BlockSpec(memory_space=pltpu.SMEM), spec, spec, spec], out_specs=[spec, spec],
        out_shape=[jax.ShapeDtypeStruct((rows, width), BF16), jax.ShapeDtypeStruct((rows, width), F32)],
        compiler_params=pltpu.CompilerParams(vmem_limit_bytes=56 << 20), name="attend_forward")(length, q, k, v)

def bwd_kernel(bk, mode, len_ref, q_ref, k_ref, v_ref, d_ref, o_ref, lse_ref, dq_ref, dk_ref, dv_ref, qa_s, ka_s, va_s, da_s, acc):
    rows = q_ref.shape[0]
    n = len_ref[0]
    lane = lax.broadcasted_iota(jnp.int32, (1, 128), 1)
    krow = lax.broadcasted_iota(jnp.int32, (rows, 1), 0)
    kbias = jnp.where((krow + len_ref[1]) % rows < n, 0.0, -1e9)
    d = d_ref[...].astype(F32)
    prod = d * o_ref[...].astype(F32)
    nl = -lse_ref[...]
    hi, mid, lo = split3(nl)
    for h in range(2):
        own = lane // DH == h
        sp = DH * (1 - h)
        pick = lambda a, b, c, e: jnp.where(lane == sp, a, jnp.where(lane == sp + 1, b, jnp.where(lane == sp + 2, c, jnp.where(lane == sp + 3, e, 0.0))))
        dlt = -jnp.sum(jnp.where(own, prod, 0.0), axis=1, keepdims=True)
        dh, dm, dl = split3(dlt)
        qa_s[h] = jnp.where(own, q_ref[...].astype(F32), pick(hi, mid, lo, 1.0)).astype(BF16)
        ka_s[h] = jnp.where(own, k_ref[...].astype(F32), pick(1.0, 1.0, 1.0, kbias)).astype(BF16)
        da_s[h] = jnp.where(own, d, pick(dh, dm, dl, 0.0)).astype(BF16)
        va_s[h] = jnp.where(own, v_ref[...].astype(F32), pick(1.0, 1.0, 1.0, 0.0)).astype(BF16)
    first = lane < DH
    for kb in range(0, rows, bk):
        dks, dvs, dqs = [], [], []
        for h in range(2):
            sT = nt(ka_s[h, kb : kb + bk], qa_s[h])
            p = jnp.exp(sT)
            dpT = nt(va_s[h, kb : kb + bk], da_s[h])
            ds = (p * dpT).astype(BF16)
            dvs.append(nn(p.astype(BF16), d_ref[...]))
            dks.append(nn(ds, q_ref[...]))
            if mode == 0:
                dqs.append(tn(ds, k_ref[kb : kb + bk]))
            else:
                dqs.append(tn(k_ref[kb : kb + bk], ds))
        dk_ref[kb : kb + bk] = jnp.where(first, dks[0], dks[1]).astype(BF16)
        dv_ref[kb : kb + bk] = jnp.where(first, dvs[0], dvs[1]).astype(BF16)
        if mode == 0:
            dq = jnp.where(first, dqs[0], dqs[1])
            if kb == 0: acc[...] = dq
            else: acc[...] += dq
        else:
            row = lax.broadcasted_iota(jnp.int32, (128, 1), 0)
            dq = jnp.where(row < DH, dqs[0], dqs[1])
            if kb == 0: acc[...] = dq
            else: acc[...] += dq
    dqv = acc[...] if mode == 0 else acc[...].T
    dq_ref[...] = (dqv * 0.125).astype(BF16)

def attend_backward(length, q, k, v, d, o, lse, bk=256, mode=0):
    rows, width = q.shape
    spec = pl.BlockSpec((rows, 128), lambda i: (0, i))
    aug = pltpu.VMEM((2, rows, 128), BF16)
    return pl.pallas_call(functools.partial(bwd_kernel, bk, mode), grid=(width // 128,),
        in_specs=[pl.BlockSpec(memory_space=pltpu.SMEM)] + [spec] * 6, out_specs=[spec] * 3,
        out_shape=[jax.ShapeDtypeStruct((rows, width), BF16)] * 3,
        scratch_shapes=[aug, aug, aug, aug, pltpu.VMEM((rows, 128) if mode == 0 else (128, rows), F32)],
        compiler_params=pltpu.CompilerParams(vmem_limit_bytes=56 << 20), name=f"attend_backward_{mode}_{bk}")(length, q, k, v, d, o, lse)

def norm_parts(v):
    c = v - jnp.mean(v, axis=-1, keepdims=True)
    r = lax.rsqrt(jnp.mean(c * c, axis=-1, keepdims=True) + 1e-5)
    return c * r, r

def norm_back(n, r, dyg):
    return r * (dyg - jnp.mean(dyg, axis=-1, keepdims=True) - n * jnp.mean(dyg * n, axis=-1, keepdims=True))

def colsum(v): return jnp.sum(v, axis=0, keepdims=True)

def mlp_kernel(chunk, len_ref, a_ref, h_ref, c_ref, wo_ref, wi_ref, wb_ref, vec_ref, bi_ref,
               out_ref, g1_ref, ga_ref, gwo_ref, gwi_ref, gwb_ref, small_ref, gbi_ref,
               acc_o, acc_i, acc_b, act, gp, b2, gn, btT, midT):
    step = pl.program_id(0)
    rows, inner = a_ref.shape[0], wi_ref.shape[1]
    b_out, b_back, gain_one, shift_one, gain_two, shift_two = [vec_ref[i : i + 1] for i in range(6)]
    @pl.when(step == 0)
    def _():
        acc_o[...] = jnp.zeros_like(acc_o); acc_i[...] = jnp.zeros_like(acc_i); acc_b[...] = jnp.zeros_like(acc_b)
        small_ref[...] = jnp.zeros_like(small_ref); gbi_ref[...] = jnp.zeros_like(gbi_ref)
    v1 = h_ref[...].astype(F32) + nt(a_ref[...], wo_ref[...]) + b_out
    n1, r1 = norm_parts(v1)
    normed = n1 * gain_one + shift_one
    mid = normed.astype(BF16)
    midT[...] = mid.T
    b2[...] = jnp.zeros_like(b2)
    def up(i, _):
        cols = pl.ds(pl.multiple_of(i * chunk, chunk), chunk)
        hp = nn(mid, wi_ref[:, cols]) + bi_ref[:, cols]
        half = 0.5 + 0.5 * lax.erf(hp * math.sqrt(0.5))
        a = (hp * half).astype(BF16)
        act[:, cols] = a
        gp[:, cols] = (half + hp * (jnp.exp(hp * hp * -0.5) * (1.0 / math.sqrt(2 * math.pi)))).astype(BF16)
        b2[...] += nt(a, wb_ref[:, cols])
        return 0
    lax.fori_loop(0, inner // chunk, up, 0)
    n2, r2 = norm_parts(normed + b2[...] + b_back)
    out_ref[...] = (n2 * gain_two + shift_two).astype(BF16)
    place = (step * rows + lax.broadcasted_iota(jnp.int32, (rows, 1), 0) + len_ref[1]) % (rows * pl.num_programs(0))
    go = c_ref[...].astype(F32) * jnp.where(place < len_ref[0], 1.0, 0.0)
    grad_two = norm_back(n2, r2, go * gain_two)
    back = grad_two.astype(BF16)
    btT[...] = back.T
    small_ref[1:2] += colsum(grad_two)
    small_ref[4:5] += colsum(go * n2)
    small_ref[5:6] += colsum(go)
    gn[...] = grad_two
    def down(i, _):
        cols = pl.ds(pl.multiple_of(i * chunk, chunk), chunk)
        gpre = nn(back, wb_ref[:, cols]) * gp[:, cols].astype(F32)
        gb = gpre.astype(BF16)
        gbi_ref[:, cols] += colsum(gb.astype(F32))
        acc_b[:, cols] += nn(btT[...], act[:, cols])
        acc_i[:, cols] += nn(midT[...], gb)
        gn[...] += nt(gb, wi_ref[:, cols])
        return 0
    lax.fori_loop(0, inner // chunk, down, 0)
    g = gn[...]
    grad_one = norm_back(n1, r1, g * gain_one)
    bo = grad_one.astype(BF16)
    small_ref[0:1] += colsum(grad_one)
    small_ref[2:3] += colsum(g * n1)
    small_ref[3:4] += colsum(g)
    g1_ref[...] = grad_one
    acc_o[...] += tn(bo, a_ref[...])
    ga_ref[...] = nn(bo, wo_ref[...]).astype(BF16)
    @pl.when(step == pl.num_programs(0) - 1)
    def _():
        gwo_ref[...] = acc_o[...].astype(BF16)
        gwi_ref[...] = acc_i[...].astype(BF16)
        gwb_ref[...] = acc_b[...].astype(BF16)

def mlp(length, a, h, c, wo, wi, wb, vec, bi, rows=256, chunk=1024):
    total, width = a.shape
    inner = wi.shape[1]
    row = pl.BlockSpec((rows, width), lambda i: (i, 0))
    def whole(s, **kw): return pl.BlockSpec(s, lambda i: (0, 0), pipeline_mode=pl.Buffered(1))
    S = jax.ShapeDtypeStruct
    V = pltpu.VMEM
    return pl.pallas_call(functools.partial(mlp_kernel, chunk), grid=(total // rows,),
        in_specs=[pl.BlockSpec(memory_space=pltpu.SMEM), row, row, row, whole((width, width)), whole((width, inner)), whole((width, inner)), whole((8, width)), whole((1, inner))],
        out_specs=[row, row, row, whole((width, width)), whole((width, inner)), whole((width, inner)), whole((8, width)), whole((1, inner))],
        out_shape=[S((total, width), BF16), S((total, width), F32), S((total, width), BF16), S((width, width), BF16), S((width, inner), BF16), S((width, inner), BF16), S((8, width), F32), S((1, inner), F32)],
        scratch_shapes=[V((width, width), F32), V((width, inner), F32), V((width, inner), F32), V((rows, inner), BF16), V((rows, inner), BF16), V((rows, width), F32), V((rows, width), F32), V((width, rows), BF16), V((width, rows), BF16)],
        compiler_params=pltpu.CompilerParams(vmem_limit_bytes=62 << 20), name=f"mlp_{rows}_{chunk}")(length, a, h, c, wo, wi, wb, vec, bi)


def per_device(
    hidden, lengths, cotangent, w_query, w_key, w_value, w_out, w_in, w_back,
    b_query, b_value, b_out, b_in, b_back, gain_one, shift_one, gain_two, shift_two,
):
    t = lax.axis_index("tensor")
    local = hidden.shape[1]
    width = b_query.shape[0]
    swap = [(0, 1), (1, 0)]

    def mine(a):
        return lax.dynamic_index_in_dim(a, t, 0, keepdims=False)

    def other(a):
        return lax.dynamic_index_in_dim(a, 1 - t, 0, keepdims=False)

    def gather(w):
        w = lax.all_gather(w, "dp", axis=0, tiled=True)
        return lax.all_gather(w, "tensor", axis=1, tiled=True)

    length = jnp.stack([mine(lengths)[0], t * local]).astype(jnp.int32)
    rows = jnp.concatenate([mine(hidden), lax.ppermute(other(hidden), "tensor", swap)], 0)
    cot = jnp.concatenate([mine(cotangent), lax.ppermute(other(cotangent), "tensor", swap)], 0)
    full_query, full_key, full_value, full_out, full_in, full_back = [gather(w) for w in (w_query, w_key, w_value, w_out, w_in, w_back)]
    query = ((nn(rows, full_query) + b_query) * 0.125).astype(BF16)
    key = nn(rows, full_key).astype(BF16)
    value = (nn(rows, full_value) + b_value).astype(BF16)
    attended, lse = attend_forward(length, query, key, value)
    vec = jnp.stack([b_out, b_back, gain_one, shift_one, gain_two, shift_two, b_out, b_out])
    out, grad_one, grad_attended, g_out, g_in, g_back, small, g_b_in = mlp(
        length, attended, rows, cot, full_out, full_in, full_back, vec, b_in[None]
    )
    d_query, d_key, d_value = attend_backward(length, query, key, value, grad_attended, attended, lse)
    grad_rows = (grad_one + nt(d_query, full_query) + nt(d_key, full_key) + nt(d_value, full_value)).astype(BF16)
    g_query, g_key, g_value = [tn(rows, d).astype(BF16) for d in (d_query, d_key, d_value)]

    def scatter(g):
        g = lax.psum_scatter(g, "dp", scatter_dimension=0, tiled=True)
        return lax.psum_scatter(g, "tensor", scatter_dimension=1, tiled=True).astype(F32)

    owned = [scatter(g) for g in (g_query, g_key, g_value, g_out, g_in, g_back)]
    sums = lax.psum(
        (jnp.sum(d_query.astype(F32), 0), jnp.sum(d_value.astype(F32), 0), small, g_b_in[0]), ("dp", "tensor")
    )

    def give(a):
        got = lax.ppermute(a[local:], "tensor", swap)
        first = t == 0
        return jnp.stack([jnp.where(first, a[:local], got), jnp.where(first, got, a[:local])], 0)

    s = sums[2]
    return (give(out), give(grad_rows), *owned, sums[0], sums[1], s[0], sums[3], s[1], s[2], s[3], s[4], s[5])


def solution(mesh):
    rows = P(None, ("dp", "tensor"), None)
    weight = P("dp", "tensor")
    return jax.shard_map(
        per_device, mesh=mesh,
        in_specs=(rows, P(None, "dp"), rows) + (weight,) * 6 + (P(),) * 9,
        out_specs=(rows, rows) + (weight,) * 6 + (P(),) * 9,
        check_vma=False,
    )
```

time: 1250 us -> 905 us (0.72)
  matrix products: 309 us -> 36.6 us
  Pallas kernels: 0 us -> 133 us
  waiting for transfers between devices: 601 us -> 533 us
  other arithmetic: 78.2 us -> 23.2 us
  local copies, waits for them, and re-layouts: 61.1 us -> 17.4 us
  loops' own time: 41.5 us -> 0 us
    dot_general x204 -> x9, matrix products: 309 us -> 36.6 us  [the longest x3 13.4 us: nt(): lax.dot_general(a, b, (((1,), (1,)), ((), ())), preferred_element_type=F32)]
    pallas_call x0 -> x3, Pallas kernels: none -> 133 us  [the longest x1 62.9 us: mlp(): pl.pallas_call(functools.partial(mlp_kernel, chunk), grid=(total // rows,...]
    unnamed x27 -> x24, waiting for transfers between devices: 177 us -> 47.3 us
    ppermute x0 -> x4, waiting for transfers between devices: none -> 44.8 us  [the longest x1 25.8 us: per_device(): lax.ppermute(other(cotangent), 'tensor', swap)]
    another operation x4 -> x0, loops' own time: 41.5 us -> none  [the longest x2 33.2 us: attend_backward(): lax.map(one_head, jnp.arange(head_count, dtype=jnp.int32))]
    reduce_sum x27 -> x1, other arithmetic: 29.1 us -> 1.9 us  [per_device(): jnp.sum(d_value.astype(F32), 0)]
    lt x24 -> x0, other arithmetic: 16.5 us -> none  [per_device(): key_live = key_place < length]
    all_gather x10 -> x8, waiting for transfers between devices: 131 us -> 147 us  [the longest x6 145 us: gather(): return lax.all_gather(w, 'tensor', axis=1, tiled=True)]
  transfers between devices with their start and end apart: 24 -> 24, of which waited for: 16 -> 19; matrix products, arithmetic and copies ran while one was open for 32% -> 8% of each run, Pallas kernels for 0% -> 8%
where the time goes in v1:
time: 905 us; the launch traced here: 897 us
  waiting for transfers between devices  533 us (59%)
  blocking collectives  134 us (15%)
  Pallas kernels  133 us (15%)
  matrix products  36.6 us (4%)
  other arithmetic  23.2 us (3%)
  local copies, waits for them, and re-layouts  17.4 us (2%)
  between operations  15.1 us (2%)
    reduce_scatter x6, waiting for transfers between devices, scatter(): g = lax.psum_scatter(g, 'dp', scatter_dimension=0, tiled=True)  269 us
    all_gather x6, waiting for transfers between devices, gather(): return lax.all_gather(w, 'tensor', axis=1, tiled=True)  145 us
    all_gather x4, blocking collectives, gather(): w = lax.all_gather(w, 'dp', axis=0, tiled=True)  92.7 us
    pallas_call x1, Pallas kernels, mlp(): pl.pallas_call(functools.partial(mlp_kernel, chunk), grid=(total // rows,...  62.9 us
    unnamed x24, waiting for transfers between devices  47.3 us
    pallas_call x1, Pallas kernels, attend_backward(): pl.pallas_call(functools.partial(bwd_kernel, bk, mode), grid=(width // 12...  41.3 us
    psum x1, blocking collectives, per_device(): lax.psum((jnp.sum(d_query.astype(F32), 0), jnp.sum(d_value.astype(F32), 0...  40.8 us
    pallas_call x1, Pallas kernels, attend_forward(): pl.pallas_call(functools.partial(fwd_kernel, bq), grid=(width // 128,), i...  28.4 us
  transfers between devices with their start and end apart: 24, of which 19 were waited for; matrix products, arithmetic and copies ran while one was open for 8% of the time, Pallas kernels for 8%

profile of v1, /device:TPU:0, one launch (start us, length us, event | category | flops | bytes accessed | tf_op | source)
XLA Modules:
  0.0 896.8 jit_solution(14444913461947831245)
XLA Ops:
  8.7 26.8 %all_gather.38 = bf16[768,384]{1,0:T(8,128)(2,1)} all-gather(bf16[48,384]{1,0:T(8,128)(2,1)} %param.22), channel_id=1, replica_groups=mesh['dp'=16,'tensor'=2] {'dp'}, dimensions={0}, use_global_device_ids=true | all-gather | bytes 626688 | tf_op jit(solution)/shard_map/all_gather | solution.py:220
  35.7 22.2 %all_gather.36 = bf16[768,384]{1,0:T(8,128)(2,1)} all-gather(bf16[48,384]{1,0:T(8,128)(2,1)} %param.21), channel_id=1, replica_groups=mesh['dp'=16,'tensor'=2] {'dp'}, dimensions={0}, use_global_device_ids=true | all-gather | bytes 626688 | tf_op jit(solution)/shard_map/all_gather | solution.py:220
  58.0 21.6 %all_gather.40 = bf16[768,384]{1,0:T(8,128)(2,1)} all-gather(bf16[48,384]{1,0:T(8,128)(2,1)S(1)} %copy-done.7), channel_id=1, replica_groups=mesh['dp'=16,'tensor'=2] {'dp'}, dimensions={0}, use_global_device_ids=true | all-gather | bytes 626688 | tf_op jit(solution)/shard_map/all_gather | solution.py:220
  79.6 22.1 %all_gather.42 = bf16[768,384]{1,0:T(8,128)(2,1)} all-gather(bf16[48,384]{1,0:T(8,128)(2,1)S(1)} %copy-done.8), channel_id=1, replica_groups=mesh['dp'=16,'tensor'=2] {'dp'}, dimensions={0}, use_global_device_ids=true | all-gather | bytes 626688 | tf_op jit(solution)/shard_map/all_gather | solution.py:220
  111.6 25.8 %collective-permute-done.1 = bf16[512,768]{1,0:T(8,128)(2,1)} collective-permute-done((bf16[512,768]{1,0:T(8,128)(2,1)}, bf16[512,768]{1,0:T(8,128)(2,1)}, u32[]{:S(2)}, u32[]{:S(2)}) %collective-permute-start.1) | collective-permute-done | bytes 786464 | tf_op jit(solution)/shard_map/ppermute | solution.py:225
  139.8 19.0 %collective-permute-done = bf16[512,768]{1,0:T(8,128)(2,1)S(1)} collective-permute-done((bf16[512,768]{1,0:T(8,128)(2,1)}, bf16[512,768]{1,0:T(8,128)(2,1)S(1)}, u32[]{:S(2)}, u32[]{:S(2)}) %collective-permute-start) | collective-permute-done | bytes 786464 | tf_op jit(solution)/shard_map/ppermute | solution.py:224
  172.1 19.9 %all-gather.13.cloned.1.call-done = bf16[768,768]{1,0:T(8,128)(2,1)} async-done(((bf16[768,384]{1,0:T(8,128)(2,1)}), bf16[768,768]{1,0:T(8,128)(2,1)}) %all-gather.13.cloned.1.call-update) | async-done | bytes 1179664 | tf_op jit(solution)/shard_map/all_gather | solution.py:221
  196.0 28.4 %attend_forward.1 = (bf16[1024,768]{1,0:T(8,128)(2,1)}, f32[1024,768]{1,0:T(8,128)}) custom-call(s32[2]{0:T(128)} %pad_add_fusion.len_ref, bf16[1024,768]{1,0:T(8,128)(2,1)} %multiply_convert_fusion.q_ref, bf16[1024,768]{1,0:T(8,128)(2,1)} %convolution_convert_fusion.k_ref, bf16[1024,768]{1,0:T(8,128)(2,1)} %add_convert_fusion.1.v_ref), custom_call_target="tpu_custom_call" | custom-call | tf_op jit(solution)/shard_map/attend_forward/pallas_call | solution.py:54
  224.4 56.1 %all-gather.19.cloned.1.call-done.wi_ref = bf16[768,3072]{1,0:T(8,128)(2,1)} async-done(((bf16[768,1536]{1,0:T(8,128)(2,1)}), bf16[768,3072]{1,0:T(8,128)(2,1)}) %all-gather.19.cloned.1.call-update) | async-done | bytes 4718608 | tf_op jit(solution)/shard_map/all_gather | solution.py:221
  280.5 64.2 %all-gather.23.cloned.1.call-done.wb_ref = bf16[768,3072]{1,0:T(8,128)(2,1)} async-done(((bf16[768,1536]{1,0:T(8,128)(2,1)}), bf16[768,3072]{1,0:T(8,128)(2,1)}) %all-gather.23.cloned.1.call-update) | async-done | bytes 4718608 | tf_op jit(solution)/shard_map/all_gather | solution.py:221
  344.7 62.9 %mlp_256_1024.1 = (bf16[1024,768]{1,0:T(8,128)(2,1)}, f32[1024,768]{1,0:T(8,128)}, bf16[1024,768]{1,0:T(8,128)(2,1)}, bf16[768,768]{1,0:T(8,128)(2,1)}, bf16[768...) custom-call(s32[2]{0:T(128)} %pad_add_fusion.len_ref, ...), custom_call_target="tpu_custom_call" | custom-call | tf_op jit(solution)/shard_map/mlp_256_1024/pallas_call | solution.py:196
  407.7 41.3 %attend_backward_0_256.1 = (bf16[1024,768]{1,0:T(8,128)(2,1)}, bf16[1024,768]{1,0:T(8,128)(2,1)}, bf16[1024,768]{1,0:T(8,128)(2,1)}) custom-call(s32[2]{0:T(128)} %pad_add_fusion.len_ref, bf16[1024,768]{1,0:T(8,128)(2,1)} %multiply_convert_fusion.q_ref, bf16[1024,768]{1,0:T(8,128)(2,1)} %convolution_convert_fusion.k_ref, ...), custom_call_target="tpu_custom_call" | custom-call | tf_op jit(solution)/shard_map/attend_backward_0_256/pallas_call | solution.py:111
  472.5 54.6 %reduce-scatter.23.cloned.1.call-done = bf16[48,768]{1,0:T(8,128)(2,1)} async-done(((bf16[768,768]{1,0:T(8,128)(2,1)}), bf16[48,768]{1,0:T(8,128)(2,1)}) %reduce-scatter.23.cloned.1.call-update) | async-done | bytes 73744 | tf_op jit(solution)/shard_map/reduce_scatter | solution.py:240
  533.3 55.1 %reduce-scatter.21.cloned.1.call-done = bf16[48,768]{1,0:T(8,128)(2,1)} async-done(((bf16[768,768]{1,0:T(8,128)(2,1)}), bf16[48,768]{1,0:T(8,128)(2,1)}) %reduce-scatter.21.cloned.1.call-update) | async-done | bytes 73744 | tf_op jit(solution)/shard_map/reduce_scatter | solution.py:240
  594.6 54.5 %reduce-scatter.25.cloned.1.call-done = bf16[48,768]{1,0:T(8,128)(2,1)} async-done(((bf16[768,768]{1,0:T(8,128)(2,1)}), bf16[48,768]{1,0:T(8,128)(2,1)}) %reduce-scatter.25.cloned.1.call-update) | async-done | bytes 73744 | tf_op jit(solution)/shard_map/reduce_scatter | solution.py:240
  658.5 69.0 %reduce-scatter.33.cloned.1.call-done = bf16[48,3072]{1,0:T(8,128)(2,1)} async-done(((bf16[768,3072]{1,0:T(8,128)(2,1)}), bf16[48,3072]{1,0:T(8,128)(2,1)}) %reduce-scatter.33.cloned.1.call-update) | async-done | bytes 294928 | tf_op jit(solution)/shard_map/reduce_scatter | solution.py:240
  729.5 40.8 %all-reduce = (f32[768]{0:T(1024)}, f32[768]{0:T(1024)}, f32[8,768]{1,0:T(8,128)S(1)}, f32[3072]{0:T(1024)}) all-reduce(f32[768]{0:T(1024)S(1)} %get-tuple-element.62, f32[768]{0:T(1024)S(1)} %get-tuple-element.61, f32[8,768]{1,0:T(8,128)S(1)} %copy-done.9, f32[3072]{0:T(1024)S(1)} %bitcast.49), channel_id=1, replica_groups=mesh['dp'=16,'tensor'=2] {'dp','tensor'}, use_global_device_ids=true, to_apply=%region_13.14 | all-reduce | flops 10752 | bytes 86016 | tf_op jit(solution)/shard_map/psum | solution.py:244
  772.4 34.5 %reduce-scatter.29.cloned.1.call-done = bf16[48,3072]{1,0:T(8,128)(2,1)} async-done(((bf16[768,3072]{1,0:T(8,128)(2,1)}), bf16[48,3072]{1,0:T(8,128)(2,1)}) %reduce-scatter.29.cloned.1.call-update) | async-done | bytes 294928 | tf_op jit(solution)/shard_map/reduce_scatter | solution.py:240
  810.8 8.3 reduce-scatter.43.cloned.1.call-done
  820.7 12.0 %reduce-scatter.39.cloned.1.call-done = bf16[384,48]{1,0:T(8,128)(2,1)} async-done(((bf16[768,48]{1,0:T(8,128)(2,1)}), bf16[384,48]{1,0:T(8,128)(2,1)}) %reduce-scatter.39.cloned.1.call-update) | async-done | bytes 36880
  834.3 12.0 %reduce-scatter.37.cloned.1.call-done = bf16[384,48]{1,0:T(8,128)(2,1)} async-done(((bf16[768,48]{1,0:T(8,128)(2,1)}), bf16[384,48]{1,0:T(8,128)(2,1)}) %reduce-scatter.37.cloned.1.call-update) | async-done | bytes 36880
  848.0 11.4 %reduce-scatter.41.cloned.1.call-done = bf16[384,48]{1,0:T(8,128)(2,1)} async-done(((bf16[768,48]{1,0:T(8,128)(2,1)}), bf16[384,48]{1,0:T(8,128)(2,1)}) %reduce-scatter.41.cloned.1.call-update) | async-done | bytes 36880
  861.0 12.7 %reduce-scatter.35.cloned.1.call-done = bf16[48,1536]{1,0:T(8,128)(2,1)} async-done(((bf16[48,3072]{1,0:T(8,128)(2,1)}), bf16[48,1536]{1,0:T(8,128)(2,1)}) %reduce-scatter.35.cloned.1.call-update) | async-done | bytes 147472 | tf_op jit(solution)/shard_map/reduce_scatter | solution.py:241
  875.4 12.5 %reduce-scatter.31.cloned.1.call-done = bf16[48,1536]{1,0:T(8,128)(2,1)} async-done(((bf16[48,3072]{1,0:T(8,128)(2,1)}), bf16[48,1536]{1,0:T(8,128)(2,1)}) %reduce-scatter.31.cloned.1.call-update) | async-done | bytes 147472 | tf_op jit(solution)/shard_map/reduce_scatter | solution.py:241
  (137 shorter events, 93.9 us)
Async XLA Ops:
  7.2 94.5 %all-gather.17.cloned.1.call-start = ((), (), s32[]{:S(2)}) async-start(), calls=%async_computation.16 | async-start | bytes 2506752 | tf_op jit(solution)/shard_map/all_gather | solution.py:220
  8.0 96.9 %all-gather.21.cloned.1.call-start = ((), (), s32[]{:S(2)}) async-start(), calls=%async_computation.18 | async-start | bytes 2506752 | tf_op jit(solution)/shard_map/all_gather | solution.py:220
  8.7 151.3 %all-gather.11.cloned.1.call-start = ((), (), s32[]{:S(2)}) async-start(), calls=%async_computation.13 | async-start | bytes 1769472 | tf_op jit(solution)/shard_map/all_gather | solution.py:221
  35.6 132.7 %all-gather.9.cloned.1.call-start = ((), (), s32[]{:S(2)}) async-start(), calls=%async_computation.12 | async-start | bytes 1769472 | tf_op jit(solution)/shard_map/all_gather | solution.py:221
  57.9 134.2 %all-gather.13.cloned.1.call-start = ((), (), s32[]{:S(2)}) async-start(), calls=%async_computation.14 | async-start | bytes 1769472 | tf_op jit(solution)/shard_map/all_gather | solution.py:221
  79.5 144.8 %all-gather.15.cloned.1.call-start = ((), (), s32[]{:S(2)}) async-start(), calls=%async_computation.15 | async-start | bytes 1769472 | tf_op jit(solution)/shard_map/all_gather | solution.py:221
  101.7 178.8 %all-gather.19.cloned.1.call-start = ((), (), s32[]{:S(2)}) async-start(), calls=%async_computation.17 | async-start | bytes 7077888 | tf_op jit(solution)/shard_map/all_gather | solution.py:221
  102.5 242.3 %all-gather.23.cloned.1.call-start = ((), (), s32[]{:S(2)}) async-start(), calls=%async_computation.19 | async-start | bytes 7077888 | tf_op jit(solution)/shard_map/all_gather | solution.py:221
  104.9 361.0 %reduce-scatter.27.cloned.1.call-start = ((), (), s32[]{:S(2)}) async-start(), calls=%async_computation.23 | async-start | bytes 1253376 | tf_op jit(solution)/shard_map/reduce_scatter | solution.py:240
  106.0 31.4 %collective-permute-start.1 = (bf16[512,768]{1,0:T(8,128)(2,1)}, bf16[512,768]{1,0:T(8,128)(2,1)}, u32[]{:S(2)}, u32[]{:S(2)}) collective-permute-start(bf16[512,768]{1,0:T(8,128)(2,1)} %get-tuple-element.58), channel_id=1, source_target_pairs={{0,1},{1,0},{2,3},{3,2},{4,5},{5,4},{6,7},{7,6},{8,9},{9,8},{10,11... | collective-permute-start | bytes 2359304 | tf_op jit(solution)/shard_map/ppermute | solution.py:225
  108.4 50.3 %collective-permute-start = (bf16[512,768]{1,0:T(8,128)(2,1)}, bf16[512,768]{1,0:T(8,128)(2,1)S(1)}, u32[]{:S(2)}, u32[]{:S(2)}) collective-permute-start(bf16[512,768]{1,0:T(8,128)(2,1)} %get-tuple-element.60), channel_id=1, source_target_pairs={{0,1},{1,0},{2,3},{3,2},{4,5},{5,4},{6,7},{7,6},{8,9},{9,8},{10,11... | collective-permute-start | bytes 2359304 | tf_op jit(solution)/shard_map/ppermute | solution.py:224
  407.7 119.4 %reduce-scatter.23.cloned.1.call-start = ((), (), s32[]{:S(2)}) async-start(), calls=%async_computation.21 | async-start | bytes 1253376 | tf_op jit(solution)/shard_map/reduce_scatter | solution.py:240
  452.9 135.5 %reduce-scatter.21.cloned.1.call-start = ((), (), s32[]{:S(2)}) async-start(), calls=%async_computation.20 | async-start | bytes 1253376 | tf_op jit(solution)/shard_map/reduce_scatter | solution.py:240
  456.9 192.1 %reduce-scatter.25.cloned.1.call-start = ((), (), s32[]{:S(2)}) async-start(), calls=%async_computation.22 | async-start | bytes 1253376 | tf_op jit(solution)/shard_map/reduce_scatter | solution.py:240
  460.9 266.6 %reduce-scatter.33.cloned.1.call-start = ((), (), s32[]{:S(2)}) async-start(), calls=%async_computation.26 | async-start | bytes 5013504 | tf_op jit(solution)/shard_map/reduce_scatter | solution.py:240
  461.6 345.3 %reduce-scatter.29.cloned.1.call-start = ((), (), s32[]{:S(2)}) async-start(), calls=%async_computation.24 | async-start | bytes 5013504 | tf_op jit(solution)/shard_map/reduce_scatter | solution.py:240
  462.2 356.8 %reduce-scatter.43.cloned.1.call-start = ((), (), s32[]{:S(2)}) async-start(), calls=%async_computation.31 | async-start | bytes 294912
  464.1 306.9 %collective-permute-start.2 = (bf16[512,768]{1,0:T(8,128)(2,1)}, bf16[512,768]{1,0:T(8,128)(2,1)}, u32[]{:S(2)}, u32[]{:S(2)}) collective-permute-start(bf16[512,768]{1,0:T(8,128)(2,1)} %slice.33), channel_id=1, source_target_pairs={{0,1},{1,0},{2,3},{3,2},{4,5},{5,4},{6,7},{7,6},{8,9},{9,8},{10,11... | collective-permute-start | bytes 2359304 | tf_op jit(solution)/shard_map/ppermute | solution.py:249
  467.6 365.1 %reduce-scatter.39.cloned.1.call-start = ((), (), s32[]{:S(2)}) async-start(), calls=%async_computation.29 | async-start | bytes 294912
  528.8 317.5 %reduce-scatter.37.cloned.1.call-start = ((), (), s32[]{:S(2)}) async-start(), calls=%async_computation.28 | async-start | bytes 294912
  590.2 269.3 %reduce-scatter.41.cloned.1.call-start = ((), (), s32[]{:S(2)}) async-start(), calls=%async_computation.30 | async-start | bytes 294912
  650.8 223.0 %reduce-scatter.35.cloned.1.call-start = ((), (), s32[]{:S(2)}) async-start(), calls=%async_computation.27 | async-start | bytes 442368 | tf_op jit(solution)/shard_map/reduce_scatter | solution.py:241
  657.0 151.2 %collective-permute-start.3 = (bf16[512,768]{1,0:T(8,128)(2,1)}, bf16[512,768]{1,0:T(8,128)(2,1)}, u32[]{:S(2)}, u32[]{:S(2)}) collective-permute-start(bf16[512,768]{1,0:T(8,128)(2,1)} %slice.43), channel_id=1, source_target_pairs={{0,1},{1,0},{2,3},{3,2},{4,5},{5,4},{6,7},{7,6},{8,9},{9,8},{10,11... | collective-permute-start | bytes 2359304 | tf_op jit(solution)/shard_map/ppermute | solution.py:249
  727.5 160.4 %reduce-scatter.31.cloned.1.call-start = ((), (), s32[]{:S(2)}) async-start(), calls=%async_computation.25 | async-start | bytes 442368 | tf_op jit(solution)/shard_map/reduce_scatter | solution.py:241
  (20 other events, 474.3 us)
Sparse Core Ops, SparseCore 0:
  10.3 46.8 all-gather.16
  59.5 45.2 all-gather.20
  106.4 35.0 all-gather.10
  142.9 25.3 all-gather.8
  169.7 22.3 all-gather.12
  193.5 22.7 all-gather.14
  217.8 62.6 all-gather.18
  282.1 62.6 all-gather.22
  407.8 58.0 reduce-scatter.26
  469.9 57.1 reduce-scatter.22
  531.3 57.1 reduce-scatter.20
  591.9 57.0 reduce-scatter.24
  652.9 74.5 reduce-scatter.32
  731.7 75.2 reduce-scatter.28
  809.0 9.9 reduce-scatter.42
  821.7 10.9 reduce-scatter.38
  835.4 10.9 reduce-scatter.36
  848.4 10.9 reduce-scatter.40
  861.6 12.0 reduce-scatter.34
  875.8 12.0 reduce-scatter.30

commit v2 on v1

v2 whole, which is shorter than its diff:
```python
import functools
import math

import jax
import jax.numpy as jnp
from jax import lax
from jax.experimental import pallas as pl
from jax.experimental.pallas import tpu as pltpu
from jax.sharding import PartitionSpec as P

F32, BF16 = jnp.float32, jnp.bfloat16
DH = 64
S = jax.ShapeDtypeStruct
HBM = pl.BlockSpec(memory_space=pl.ANY)
SMALL = pl.BlockSpec(memory_space=pltpu.SMEM)
DMA = pltpu.SemaphoreType.DMA


def nt(a, b):
    return lax.dot_general(a, b, (((1,), (1,)), ((), ())), preferred_element_type=F32)


def nn(a, b):
    return lax.dot_general(a, b, (((1,), (0,)), ((), ())), preferred_element_type=F32)


def tn(a, b):
    return lax.dot_general(a, b, (((0,), (0,)), ((), ())), preferred_element_type=F32)


def split3(v):
    hi = v.astype(BF16).astype(F32)
    rest = v - hi
    mid = rest.astype(BF16).astype(F32)
    return hi, mid, rest - mid


class Place:
    def __init__(self):
        dp, t = lax.axis_index("dp"), lax.axis_index("tensor")
        z, x, c = dp // 4, (dp // 2) % 2, dp % 2
        self.z, self.x, self.c, self.t = z, x, c, t
        self.above, self.below, self.far = (z + 1) % 4, (z + 3) % 4, (z + 2) % 4
        at = lambda z, x, c, t: ((z * 2 + x) * 2 + c, t)
        self.up, self.down = at(self.above, x, c, t), at(self.below, x, c, t)
        self.across, self.beside, self.twin = at(z, 1 - x, c, t), at(z, x, c, 1 - t), at(z, x, 1 - c, t)

    def greet(self):
        barrier = pltpu.get_barrier_semaphore()
        for peer in (self.up, self.down, self.across, self.beside, self.twin):
            pl.semaphore_signal(barrier, inc=1, device_id=peer, device_id_type=pl.DeviceIdType.MESH)
        pl.semaphore_wait(barrier, 5)


def remote(src, dst, send, recv, peer):
    return pltpu.make_async_remote_copy(src, dst, send, recv, device_id=peer, device_id_type=pl.DeviceIdType.MESH)


def gather_stages(place, order, shard, full, first, count, send, recv, local):
    z, x, c, t = place.z, place.x, place.c, place.t
    lanes = pl.ds(first, count)
    part = count // 256 * 128
    low, high = pl.ds(first, part), pl.ds(first + part, count - part)
    own = full.at[t, z, x, c, :, lanes]
    here = shard.at[:, lanes]
    def move(i, view, peer, src=None):
        return remote(view if src is None else src, view, send.at[i], recv.at[i], peer)
    keep = pltpu.make_async_copy(here, own, local)
    everything = move(6, full.at[:, :, :, c, :, lanes], place.twin)
    if order[0] == "z":
        first_up, first_down = move(0, own, place.up, here), move(1, own, place.down, here)
        next_up = move(2, full.at[t, place.below, x, c, :, low], place.up)
        next_down = move(3, full.at[t, place.above, x, c, :, high], place.down)
        if order == "zxy":
            four, five = move(4, full.at[t, :, x, c, :, lanes], place.across), move(5, full.at[t, :, :, c, :, lanes], place.beside)
        else:
            four, five = move(4, full.at[t, :, x, c, :, lanes], place.beside), move(5, full.at[:, :, x, c, :, lanes], place.across)
        copies = [first_up, first_down, next_up, next_down, four, five, everything]
        def s0(): keep.start(); first_up.start(); first_down.start()
        def s1(): first_up.wait_recv(); next_up.start(); first_down.wait_recv(); next_down.start()
        def s2(): next_up.wait_recv(); next_down.wait_recv(); keep.wait(); four.start()
        def s3(): four.wait_recv(); five.start()
        def s4(): five.wait_recv(); everything.start()
    else:
        if order == "xyz":
            one, two = move(0, own, place.across, here), move(1, full.at[t, z, :, c, :, lanes], place.beside)
        else:
            one, two = move(0, own, place.beside, here), move(1, full.at[:, z, x, c, :, lanes], place.across)
        first_up, first_down = move(2, full.at[:, z, :, c, :, lanes], place.up), move(3, full.at[:, z, :, c, :, lanes], place.down)
        next_up = move(4, full.at[0, place.below, :, c, :, lanes], place.up)
        next_down = move(5, full.at[1, place.above, :, c, :, lanes], place.down)
        copies = [one, two, first_up, first_down, next_up, next_down, everything]
        def s0(): keep.start(); one.start()
        def s1(): one.wait_recv(); keep.wait(); two.start()
        def s2(): two.wait_recv(); first_up.start(); first_down.start()
        def s3(): first_up.wait_recv(); next_up.start(); first_down.wait_recv(); next_down.start()
        def s4(): next_up.wait_recv(); next_down.wait_recv(); everything.start()
    def s5():
        everything.wait_recv()
        for copy in copies: copy.wait_send()
    return [s0, s1, s2, s3, s4, s5]


def add_blocks(count, dst, *srcs):
    def body(i, _):
        ref = dst(i)
        total = ref[...].astype(F32)
        for s in srcs: total = total + s(i)[...].astype(F32)
        ref[...] = total.astype(ref.dtype)
        return 0
    lax.fori_loop(0, count, body, 0)


def reduce_scratch(order, rows, lanes):
    V = lambda *s: pltpu.VMEM(s + (rows, lanes), BF16)
    base = [V(2, 4, 2), V(2, 4, 2)]
    if order == "yxz": base += [V(4, 2), V(4), V(), V(2)]
    elif order == "xyz": base += [V(2, 4), V(4), V(), V(2)]
    else: base += [V(2, 2), V(2, 2, 2), V(2), V()]
    return base + [pltpu.SemaphoreType.DMA((7,)), pltpu.SemaphoreType.DMA((7,)), pltpu.SemaphoreType.DMA]


def reduce_stages(place, order, grad, first, count, out, scratch):
    held, r0, r1, r2, r3, r4, send, recv, local = scratch
    z, x, c, t = place.z, place.x, place.c, place.t
    lanes = pl.ds(first, count)
    part = count // 256 * 128
    low, high = pl.ds(0, part), pl.ds(part, count - part)
    load = pltpu.make_async_copy(grad.at[:, :, :, c, :, lanes], held, local)
    def move(i, src, dst, peer):
        return remote(src, dst, send.at[i], recv.at[i], peer)
    c0 = move(0, grad.at[:, :, :, 1 - c, :, lanes], r0, place.twin)
    at3 = lambda ref: (lambda i: ref.at[i // 8, (i // 2) % 4, i % 2])
    def s0(): load.start(); c0.start()
    if order[0] != "z":
        if order == "yxz":
            c1, c2 = move(1, held.at[1 - t], r1, place.beside), move(2, held.at[t, :, 1 - x], r2, place.across)
            def add1(): add_blocks(8, lambda i: held.at[t, i // 2, i % 2], lambda i: r1.at[i // 2, i % 2])
        else:
            c1, c2 = move(1, held.at[:, :, 1 - x], r1, place.across), move(2, held.at[1 - t, :, x], r2, place.beside)
            def add1(): add_blocks(8, lambda i: held.at[i // 4, i % 4, x], lambda i: r1.at[i // 4, i % 4])
        mine = lambda k: held.at[t, k, x]
        c3 = move(3, held.at[t, place.far, x, :, low], r3.at[:, low], place.up)
        c4 = move(4, held.at[t, place.far, x, :, high], r3.at[:, high], place.down)
        c5, c6 = move(5, mine(place.above), r4.at[0], place.up), move(6, mine(place.below), r4.at[1], place.down)
        def s1(): load.wait(); c0.wait_recv(); add_blocks(16, at3(held), at3(r0)); c1.start()
        def s2(): c1.wait_recv(); add1(); c2.start()
        def s3(): c2.wait_recv(); add_blocks(4, mine, lambda k: r2.at[k]); c3.start(); c4.start()
        def s4():
            c3.wait_recv()
            v = held.at[t, place.above, x, :, low]; v[...] = (v[...].astype(F32) + r3[:, low].astype(F32)).astype(BF16)
            c5.start()
            c4.wait_recv()
            v = held.at[t, place.below, x, :, high]; v[...] = (v[...].astype(F32) + r3[:, high].astype(F32)).astype(BF16)
            c6.start()
        def s5():
            c5.wait_recv(); c6.wait_recv()
            out[:, lanes] = mine(z)[...].astype(F32) + r4[0].astype(F32) + r4[1].astype(F32)
            for copy in (c0, c1, c2, c3, c4, c5, c6): copy.wait_send()
    else:
        c1, c2 = move(1, held.at[0, place.far], r1.at[0], place.up), move(2, held.at[1, place.far], r1.at[1], place.down)
        c3, c4 = move(3, held.at[:, place.above], r2.at[0], place.up), move(4, held.at[:, place.below], r2.at[1], place.down)
        if order == "zyx":
            c5, c6 = move(5, held.at[1 - t, z], r3, place.beside), move(6, held.at[t, z, 1 - x], r4, place.across)
            def add5(): add_blocks(2, lambda k: held.at[t, z, k], lambda k: r3.at[k])
        else:
            c5, c6 = move(5, held.at[:, z, 1 - x], r3, place.across), move(6, held.at[1 - t, z, x], r4, place.beside)
            def add5(): add_blocks(2, lambda k: held.at[k, z, x], lambda k: r3.at[k])
        def s1(): load.wait(); c0.wait_recv(); add_blocks(16, at3(held), at3(r0)); c1.start(); c2.start()
        def s2():
            c1.wait_recv(); add_blocks(2, lambda k: held.at[0, place.above, k], lambda k: r1.at[0, k]); c3.start()
            c2.wait_recv(); add_blocks(2, lambda k: held.at[1, place.below, k], lambda k: r1.at[1, k]); c4.start()
        def s3():
            c3.wait_recv(); c4.wait_recv()
            add_blocks(4, lambda k: held.at[k // 2, z, k % 2], lambda k: r2.at[0, k // 2, k % 2], lambda k: r2.at[1, k // 2, k % 2])
            c5.start()
        def s4(): c5.wait_recv(); add5(); c6.start()
        def s5():
            c6.wait_recv()
            out[:, lanes] = held[t, z, x].astype(F32) + r4[...].astype(F32)
            for copy in (c0, c1, c2, c3, c4, c5, c6): copy.wait_send()
    return [s0, s1, s2, s3, s4, s5]


def fold_stages(place, part, got, send, recv):
    flip = place.z % 2
    near = jax.tree.map(lambda u, d: u + flip * (d - u), place.up, place.down)
    next_ = jax.tree.map(lambda u, d: d + flip * (u - d), place.up, place.down)
    peers = (place.twin, place.across, place.beside, near, next_)
    copies = [remote(part, got.at[i], send.at[i], recv.at[i], peer) for i, peer in enumerate(peers)]
    def stage(i):
        def run():
            if i > 0:
                copies[i - 1].wait()
                part[...] = part[...] + got[i - 1]
            if i < 5:
                copies[i].start()
        return run
    return [stage(i) for i in range(6)]


def gather_sems(count):
    return [s for _ in range(count) for s in (DMA((7,)), DMA((7,)), DMA)]


def gather_plans(place, items, shards, fulls, sems):
    return [
        gather_stages(place, order, shards[w], fulls[w], first, count, *sems[3 * i : 3 * i + 3])
        for i, (w, first, count, order) in enumerate(items)
    ]


def reduce_plans(place, items, grads, outs, scratch):
    return [
        reduce_stages(place, order, grads[w], first, count, outs[w], scratch[9 * i : 9 * i + 9])
        for i, (w, first, count, order) in enumerate(items)
    ]


def swap_in(place, pair, rows, sems):
    local = pair.shape[1]
    keep = pltpu.make_async_copy(pair.at[place.t], rows.at[pl.ds(0, local)], sems.at[0])
    give = remote(pair.at[1 - place.t], rows.at[pl.ds(local, local)], sems.at[1], sems.at[2], place.beside)
    return keep, give


def swap_out(place, rows, pair, sems):
    local = pair.shape[1]
    keep = pltpu.make_async_copy(rows.at[pl.ds(0, local)], pair.at[place.t], sems.at[0])
    give = remote(rows.at[pl.ds(local, local)], pair.at[place.t], sems.at[1], sems.at[2], place.beside)
    return keep, give


ENTER_ITEMS = ((0, 0, 1, "xyz"), (1, 0, 1, "zxy"), (2, 0, 1, "zyx"))
REST_ITEMS = ((0, 0, 1, "zxy"), (1, 0, 2, "xyz"), (1, 1, 2, "zxy"), (2, 0, 2, "yxz"), (2, 1, 2, "zyx"))


def items_for(table, widths):
    return [(w, widths[w] // parts * i, widths[w] // parts, order) for w, i, parts, order in table]


def enter(hidden, shards):
    items = items_for(ENTER_ITEMS, [s.shape[1] for s in shards])
    n = len(shards)

    def kernel(*refs):
        pair, given, rows, fulls = refs[0], refs[1 : 1 + n], refs[1 + n], refs[2 + n : 2 + 2 * n]
        sems, swap = refs[2 + 2 * n : -1], refs[-1]
        place = Place()
        place.greet()
        keep, give = swap_in(place, pair, rows, swap)
        plans = gather_plans(place, items, given, fulls, sems)
        keep.start()
        give.start()
        for s in range(6):
            for plan in plans:
                plan[s]()
        keep.wait()
        give.wait()

    return pl.pallas_call(
        kernel,
        in_specs=[HBM] * (1 + n),
        out_specs=[HBM] * (1 + n),
        out_shape=[S((2 * hidden.shape[1], hidden.shape[2]), BF16)] + [S((2, 4, 2, 2) + s.shape, BF16) for s in shards],
        scratch_shapes=gather_sems(len(items)) + [DMA((3,))],
        compiler_params=pltpu.CompilerParams(collective_id=1, has_side_effects=True),
        name="enter",
    )(hidden, *shards)


def forward_pair(bq, len_ref, q_ref, k_ref, v_ref, o_ref, lse_ref):
    rows = q_ref.shape[0]
    n = len_ref[0]
    lane = lax.broadcasted_iota(jnp.int32, (1, 128), 1)
    krow = lax.broadcasted_iota(jnp.int32, (rows, 1), 0)
    kbias = jnp.where((krow + len_ref[1]) % rows < n, 0.0, -1e9)
    k = k_ref[...].astype(F32)
    v = v_ref[...]
    kas = []
    for h in range(2):
        own = lane // DH == h
        kas.append(jnp.where(own, k, jnp.where(lane == DH * (1 - h), kbias, 0.0)).astype(BF16))
    first = lane < DH

    def block(i, _):
        place = pl.ds(pl.multiple_of(i * bq, bq), bq)
        q = q_ref[place].astype(F32)
        os_, ls = [], []
        for h in range(2):
            own = lane // DH == h
            qa = jnp.where(own, q, jnp.where(lane == DH * (1 - h), 1.0, 0.0)).astype(BF16)
            s = nt(qa, kas[h])
            m = jnp.max(s, axis=1, keepdims=True)
            p = jnp.exp(s - m)
            l = jnp.sum(p, axis=1, keepdims=True)
            os_.append(nn(p.astype(BF16), v) * (1.0 / l))
            ls.append(m + jnp.log(l))
        o_ref[place] = jnp.where(first, os_[0], os_[1]).astype(BF16)
        lse_ref[place] = jnp.where(first, ls[1], ls[0])
        return 0

    for i in range(rows // bq):
        block(i, 0)


def attend_forward(length, q, k, v, comm=None, bq=256):
    rows, width = q.shape
    spec = pl.BlockSpec((rows, 128), lambda i: (0, i))
    out_shape = [S((rows, width), BF16), S((rows, width), F32)]
    cost = pl.CostEstimate(flops=4 * rows * rows * width, bytes_accessed=12 * rows * width, transcendentals=rows * rows * width // DH)
    if comm is None:
        return pl.pallas_call(
            functools.partial(forward_pair, bq),
            grid=(width // 128,),
            in_specs=[SMALL, spec, spec, spec],
            out_specs=[spec, spec],
            out_shape=out_shape,
            cost_estimate=cost,
            compiler_params=pltpu.CompilerParams(vmem_limit_bytes=56 << 20),
            name="attend_forward",
        )(length, q, k, v)
    pair, shards = comm
    n = len(shards)
    items = items_for(REST_ITEMS, [s.shape[1] for s in shards])

    def kernel(*refs):
        len_ref, q_ref, k_ref, v_ref, pair_ref = refs[:5]
        given, (o_ref, lse_ref, rows_ref), fulls = refs[5 : 5 + n], refs[5 + n : 8 + n], refs[8 + n : 8 + 2 * n]
        sems, swap = refs[8 + 2 * n : -1], refs[-1]
        step = pl.program_id(0)
        place = Place()
        keep, give = swap_in(place, pair_ref, rows_ref, swap)
        plans = gather_plans(place, items, given, fulls, sems)
        for s in range(5):
            @pl.when(step == s)
            def _():
                if s == 0:
                    place.greet()
                    keep.start()
                for plan in plans:
                    plan[s]()
                if s == 1:
                    give.start()
        forward_pair(bq, len_ref, q_ref, k_ref, v_ref, o_ref, lse_ref)
        @pl.when(step == pl.num_programs(0) - 1)
        def _():
            for plan in plans:
                plan[5]()
            keep.wait()
            give.wait()

    return pl.pallas_call(
        kernel,
        grid=(width // 128,),
        in_specs=[SMALL, spec, spec, spec] + [HBM] * (1 + n),
        out_specs=[spec, spec] + [HBM] * (1 + n),
        out_shape=out_shape + [S((rows, width), BF16)] + [S((2, 4, 2, 2) + s.shape, BF16) for s in shards],
        scratch_shapes=gather_sems(len(items)) + [DMA((3,))],
        cost_estimate=cost,
        compiler_params=pltpu.CompilerParams(collective_id=2, has_side_effects=True, vmem_limit_bytes=56 << 20),
        name="attend_forward",
    )(length, q, k, v, pair, *shards)


def backward_pair(bk, len_ref, q_ref, k_ref, v_ref, d_ref, o_ref, lse_ref, dq_ref, dk_ref, dv_ref, qa_s, ka_s, va_s, da_s, acc):
    rows = q_ref.shape[0]
    n = len_ref[0]
    lane = lax.broadcasted_iota(jnp.int32, (1, 128), 1)
    krow = lax.broadcasted_iota(jnp.int32, (rows, 1), 0)
    kbias = jnp.where((krow + len_ref[1]) % rows < n, 0.0, -1e9)
    d = d_ref[...].astype(F32)
    prod = d * o_ref[...].astype(F32)
    hi, mid, lo = split3(-lse_ref[...])
    for h in range(2):
        own = lane // DH == h
        sp = DH * (1 - h)
        def pick(a, b, c, e):
            return jnp.where(lane == sp, a, jnp.where(lane == sp + 1, b, jnp.where(lane == sp + 2, c, jnp.where(lane == sp + 3, e, 0.0))))
        dh, dm, dl = split3(-jnp.sum(jnp.where(own, prod, 0.0), axis=1, keepdims=True))
        qa_s[h] = jnp.where(own, q_ref[...].astype(F32), pick(hi, mid, lo, 1.0)).astype(BF16)
        ka_s[h] = jnp.where(own, k_ref[...].astype(F32), pick(1.0, 1.0, 1.0, kbias)).astype(BF16)
        da_s[h] = jnp.where(own, d, pick(dh, dm, dl, 0.0)).astype(BF16)
        va_s[h] = jnp.where(own, v_ref[...].astype(F32), pick(1.0, 1.0, 1.0, 0.0)).astype(BF16)
    first = lane < DH
    upper = lax.broadcasted_iota(jnp.int32, (128, 1), 0) < DH
    for kb in range(0, rows, bk):
        dks, dvs, dqs = [], [], []
        for h in range(2):
            p = jnp.exp(nt(ka_s[h, kb : kb + bk], qa_s[h]))
            ds = (p * nt(va_s[h, kb : kb + bk], da_s[h])).astype(BF16)
            dvs.append(nn(p.astype(BF16), d_ref[...]))
            dks.append(nn(ds, q_ref[...]))
            dqs.append(tn(k_ref[kb : kb + bk], ds))
        dk_ref[kb : kb + bk] = jnp.where(first, dks[0], dks[1]).astype(BF16)
        dv_ref[kb : kb + bk] = jnp.where(first, dvs[0], dvs[1]).astype(BF16)
        dq = jnp.where(upper, dqs[0], dqs[1])
        if kb == 0:
            acc[...] = dq
        else:
            acc[...] += dq
    dq_ref[...] = (acc[...].T * 0.125).astype(BF16)


def attend_backward(length, q, k, v, d, o, lse, comm=None, bk=256):
    rows, width = q.shape
    spec = pl.BlockSpec((rows, 128), lambda i: (0, i))
    aug = pltpu.VMEM((2, rows, 128), BF16)
    base = [aug, aug, aug, aug, pltpu.VMEM((128, rows), F32)]
    out_shape = [S((rows, width), BF16)] * 3
    cost = pl.CostEstimate(flops=10 * rows * rows * width, bytes_accessed=20 * rows * width, transcendentals=rows * rows * width // DH)
    if comm is None:
        return pl.pallas_call(
            functools.partial(backward_pair, bk),
            grid=(width // 128,),
            in_specs=[SMALL] + [spec] * 6,
            out_specs=[spec] * 3,
            out_shape=out_shape,
            scratch_shapes=base,
            cost_estimate=cost,
            compiler_params=pltpu.CompilerParams(vmem_limit_bytes=56 << 20),
            name="attend_backward",
        )(length, q, k, v, d, o, lse)
    out_rows, grads = comm
    n = len(grads)
    shards = [g.shape[4:] for g in grads]
    items = items_for(REST_ITEMS, [s[1] for s in shards])

    def kernel(*refs):
        main_in, (rows_ref,), given = refs[:7], refs[7:8], refs[8 : 8 + n]
        rest = refs[8 + n :]
        main_out, (pair_ref,), outs = rest[:3], rest[3:4], rest[4 : 4 + n]
        main_scratch, scratch, swap = rest[4 + n : 9 + n], rest[9 + n : -1], rest[-1]
        step = pl.program_id(0)
        place = Place()
        keep, give = swap_out(place, rows_ref, pair_ref, swap)
        plans = reduce_plans(place, items, given, outs, scratch)
        for s in range(5):
            @pl.when(step == s)
            def _():
                if s == 0:
                    place.greet()
                    keep.start()
                for plan in plans:
                    plan[s]()
                if s == 2:
                    give.start()
        backward_pair(bk, *main_in, *main_out, *main_scratch)
        @pl.when(step == pl.num_programs(0) - 1)
        def _():
            for plan in plans:
                plan[5]()
            keep.wait()
            give.wait()

    vm = [pl.BlockSpec(s, lambda i: (0, 0), pipeline_mode=pl.Buffered(1)) for s in shards]
    return pl.pallas_call(
        kernel,
        grid=(width // 128,),
        in_specs=[SMALL] + [spec] * 6 + [HBM] * (1 + n),
        out_specs=[spec] * 3 + [HBM] + vm,
        out_shape=out_shape + [S((2, rows // 2, width), BF16)] + [S(s, F32) for s in shards],
        scratch_shapes=base + [s for w, f, c, o in items for s in reduce_scratch(o, shards[w][0], c)] + [DMA((3,))],
        cost_estimate=cost,
        compiler_params=pltpu.CompilerParams(collective_id=3, has_side_effects=True, vmem_limit_bytes=60 << 20),
        name="attend_backward",
    )(length, q, k, v, d, o, lse, out_rows, *grads)


def norm_parts(v):
    c = v - jnp.mean(v, axis=-1, keepdims=True)
    r = lax.rsqrt(jnp.mean(c * c, axis=-1, keepdims=True) + 1e-5)
    return c * r, r


def norm_back(n, r, dyg):
    return r * (dyg - jnp.mean(dyg, axis=-1, keepdims=True) - n * jnp.mean(dyg * n, axis=-1, keepdims=True))


def colsum(v):
    return jnp.sum(v, axis=0, keepdims=True)


def mlp_kernel(chunk, len_ref, a_ref, h_ref, c_ref, wo_ref, wi_ref, wb_ref, vec_ref, bi_ref,
               out_ref, g1_ref, ga_ref, gwo_ref, gwi_ref, gwb_ref, small_ref, gbi_ref,
               acc_o, acc_i, acc_b, act, gp, b2, gn, btT, midT):
    step = pl.program_id(0)
    rows = a_ref.shape[0]
    half, inner = wo_ref.shape[2], wi_ref.shape[2]
    b_out, b_back, gain_one, shift_one, gain_two, shift_two = [vec_ref[i : i + 1] for i in range(6)]

    @pl.when(step == 0)
    def _():
        for ref in (acc_o, acc_i, acc_b, small_ref, gbi_ref):
            ref[...] = jnp.zeros_like(ref)

    v1 = h_ref[...].astype(F32) + (nt(a_ref[:, :half], wo_ref[0]) + nt(a_ref[:, half:], wo_ref[1])) + b_out
    n1, r1 = norm_parts(v1)
    normed = n1 * gain_one + shift_one
    mid = normed.astype(BF16)
    midT[...] = mid.T
    b2[...] = jnp.zeros_like(b2)

    def up(i, _):
        t = i // (inner // chunk)
        cols = pl.ds(pl.multiple_of(i % (inner // chunk) * chunk, chunk), chunk)
        hp = nn(mid, wi_ref[t, :, cols]) + bi_ref[t, :, cols]
        half_up = 0.5 + 0.5 * lax.erf(hp * math.sqrt(0.5))
        a = (hp * half_up).astype(BF16)
        act[t, :, cols] = a
        gp[t, :, cols] = (half_up + hp * (jnp.exp(hp * hp * -0.5) * (1.0 / math.sqrt(2 * math.pi)))).astype(BF16)
        b2[...] += nt(a, wb_ref[t, :, cols])
        return 0

    lax.fori_loop(0, 2 * inner // chunk, up, 0)
    n2, r2 = norm_parts(normed + b2[...] + b_back)
    out_ref[...] = (n2 * gain_two + shift_two).astype(BF16)
    place = (step * rows + lax.broadcasted_iota(jnp.int32, (rows, 1), 0) + len_ref[1]) % (rows * pl.num_programs(0))
    go = c_ref[...].astype(F32) * jnp.where(place < len_ref[0], 1.0, 0.0)
    grad_two = norm_back(n2, r2, go * gain_two)
    back = grad_two.astype(BF16)
    btT[...] = back.T
    small_ref[1:2] += colsum(grad_two)
    small_ref[4:5] += colsum(go * n2)
    small_ref[5:6] += colsum(go)
    gn[...] = grad_two

    def down(i, _):
        t = i // (inner // chunk)
        cols = pl.ds(pl.multiple_of(i % (inner // chunk) * chunk, chunk), chunk)
        gb = (nn(back, wb_ref[t, :, cols]) * gp[t, :, cols].astype(F32)).astype(BF16)
        gbi_ref[t, :, cols] += colsum(gb.astype(F32))
        acc_b[t, :, cols] += nn(btT[...], act[t, :, cols])
        acc_i[t, :, cols] += nn(midT[...], gb)
        gn[...] += nt(gb, wi_ref[t, :, cols])
        return 0

    lax.fori_loop(0, 2 * inner // chunk, down, 0)
    g = gn[...]
    grad_one = norm_back(n1, r1, g * gain_one)
    bo = grad_one.astype(BF16)
    small_ref[0:1] += colsum(grad_one)
    small_ref[2:3] += colsum(g * n1)
    small_ref[3:4] += colsum(g)
    g1_ref[...] = grad_one
    for t in range(2):
        cols = slice(t * half, (t + 1) * half)
        acc_o[t] += tn(bo, a_ref[:, cols])
        ga_ref[:, cols] = nn(bo, wo_ref[t]).astype(BF16)

    @pl.when(step == pl.num_programs(0) - 1)
    def _():
        gwo_ref[...] = acc_o[...].astype(BF16)
        gwi_ref[...] = acc_i[...].astype(BF16)
        gwb_ref[...] = acc_b[...].astype(BF16)


def mlp(length, a, h, c, wo, wi, wb, vec, bi, rows=256, chunk=768):
    total, width = a.shape
    row = pl.BlockSpec((rows, width), lambda i: (i, 0))
    def whole(s):
        return pl.BlockSpec(s, lambda i: (0,) * len(s), pipeline_mode=pl.Buffered(1))
    V = pltpu.VMEM
    inner = wi.shape[2]
    return pl.pallas_call(
        functools.partial(mlp_kernel, chunk),
        grid=(total // rows,),
        in_specs=[SMALL, row, row, row] + [whole(s.shape) for s in (wo, wi, wb, vec, bi)],
        out_specs=[row, row, row] + [whole(s.shape) for s in (wo, wi, wb, vec, bi)],
        out_shape=[S((total, width), BF16), S((total, width), F32), S((total, width), BF16)]
        + [S(s.shape, BF16) for s in (wo, wi, wb)] + [S(vec.shape, F32), S(bi.shape, F32)],
        scratch_shapes=[V(s.shape, F32) for s in (wo, wi, wb)]
        + [V((2, rows, inner), BF16), V((2, rows, inner), BF16), V((rows, width), F32), V((rows, width), F32), V((width, rows), BF16), V((width, rows), BF16)],
        cost_estimate=pl.CostEstimate(flops=total * width * (24 * inner + 6 * width), bytes_accessed=60 << 20, transcendentals=4 * total * inner),
        compiler_params=pltpu.CompilerParams(vmem_limit_bytes=62 << 20),
        name="mlp",
    )(length, a, h, c, wo, wi, wb, vec, bi)


def leave(grad_rows, small, grads):
    n = len(grads)
    shards = [g.shape[4:] for g in grads]
    items = items_for(ENTER_ITEMS, [s[1] for s in shards])
    rows, width = grad_rows.shape

    def kernel(*refs):
        rows_ref, small_ref, given = refs[0], refs[1], refs[2 : 2 + n]
        rest = refs[2 + n :]
        pair_ref, sum_ref, outs = rest[0], rest[1], rest[2 : 2 + n]
        part, got, fold_send, fold_recv, swap, scratch = rest[2 + n], rest[3 + n], rest[4 + n], rest[5 + n], rest[6 + n], rest[7 + n :]
        place = Place()
        part[...] = small_ref[...]
        place.greet()
        keep, give = swap_out(place, rows_ref, pair_ref, swap)
        plans = reduce_plans(place, items, given, outs, scratch) + [fold_stages(place, part, got, fold_send, fold_recv)]
        keep.start()
        for s in range(6):
            for plan in plans:
                plan[s]()
            if s == 0:
                give.start()
        sum_ref[...] = part[...]
        keep.wait()
        give.wait()

    vmem = pl.BlockSpec(memory_space=pltpu.VMEM)
    return pl.pallas_call(
        kernel,
        in_specs=[HBM, vmem] + [HBM] * n,
        out_specs=[HBM, vmem] + [vmem] * n,
        out_shape=[S((2, rows // 2, width), BF16), S(small.shape, F32)] + [S(s, F32) for s in shards],
        scratch_shapes=[pltpu.VMEM(small.shape, F32), pltpu.VMEM((5,) + small.shape, F32), DMA((5,)), DMA((5,)), DMA((3,))]
        + [s for w, f, c, o in items for s in reduce_scratch(o, shards[w][0], c)],
        compiler_params=pltpu.CompilerParams(collective_id=4, has_side_effects=True, vmem_limit_bytes=56 << 20),
        name="leave",
    )(grad_rows, small, *grads)


def per_device(
    hidden, lengths, cotangent, w_query, w_key, w_value, w_out, w_in, w_back,
    b_query, b_value, b_out, b_in, b_back, gain_one, shift_one, gain_two, shift_two,
):
    t = lax.axis_index("tensor")
    local = hidden.shape[1]
    width = b_query.shape[0]
    inner = b_in.shape[0]
    own_kernels = lax.axis_size("dp") == 16 and lax.axis_size("tensor") == 2
    swap = [(0, 1), (1, 0)]

    def mine(a):
        return lax.dynamic_index_in_dim(a, t, 0, keepdims=False)

    def take(a):
        other = lax.dynamic_index_in_dim(a, 1 - t, 0, keepdims=False)
        return jnp.concatenate([mine(a), lax.ppermute(other, "tensor", swap)], 0)

    def give(a):
        got = lax.ppermute(a[local:], "tensor", swap)
        first = t == 0
        return jnp.stack([jnp.where(first, a[:local], got), jnp.where(first, got, a[:local])], 0)

    def gather(w):
        return lax.all_gather(lax.all_gather(w, "dp", axis=0, tiled=True), "tensor", axis=0)

    def scatter(g):
        g = lax.psum_scatter(g, "dp", scatter_dimension=1, tiled=True)
        return lax.psum_scatter(g, "tensor", scatter_dimension=0, tiled=False).astype(F32)

    def flat(w):
        return w.reshape(2, width, -1)

    length = jnp.stack([mine(lengths)[0], t * local]).astype(jnp.int32)
    if own_kernels:
        rows, *near = enter(hidden, (w_query, w_key, w_value))
        full_query, full_key, full_value = [flat(w) for w in near]
    else:
        rows = take(hidden)
        full_query, full_key, full_value = [gather(w) for w in (w_query, w_key, w_value)]

    def project(w):
        return jnp.concatenate([nn(rows, w[0]), nn(rows, w[1])], 1)

    query = ((project(full_query) + b_query) * 0.125).astype(BF16)
    key = project(full_key).astype(BF16)
    value = (project(full_value) + b_value).astype(BF16)
    if own_kernels:
        attended, lse, cot, *rest = attend_forward(length, query, key, value, (cotangent, (w_out, w_in, w_back)))
        full_out, full_in, full_back = [flat(w) for w in rest]
    else:
        attended, lse = attend_forward(length, query, key, value)
        cot = take(cotangent)
        full_out, full_in, full_back = [gather(w) for w in (w_out, w_in, w_back)]
    vec = jnp.stack([b_out, b_back, gain_one, shift_one, gain_two, shift_two, b_out, b_out])
    out, grad_one, grad_attended, g_out, g_in, g_back, small, g_b_in = mlp(
        length, attended, rows, cot, full_out, full_in, full_back, vec, b_in.reshape(2, 1, inner // 2)
    )
    def split(g):
        return g.reshape(2, 4, 2, 2, -1, g.shape[-1])
    if own_kernels:
        d_query, d_key, d_value, output, *owned_rest = attend_backward(
            length, query, key, value, grad_attended, attended, lse, (out, [split(g) for g in (g_out, g_in, g_back)])
        )
    else:
        d_query, d_key, d_value = attend_backward(length, query, key, value, grad_attended, attended, lse)
        output = give(out)
        owned_rest = [scatter(g) for g in (g_out, g_in, g_back)]
    total = grad_one
    grads = []
    for d, w in ((d_query, full_query), (d_key, full_key), (d_value, full_value)):
        total = total + nt(d, jnp.concatenate([w[0], w[1]], 1))
        g = tn(rows, d).astype(BF16)
        grads.append(jnp.stack([g[:, : width // 2], g[:, width // 2 :]]))
    grad_rows = total.astype(BF16)
    small = jnp.concatenate([
        small, g_b_in.reshape(-1, width),
        jnp.sum(d_query.astype(F32), 0)[None], jnp.sum(d_value.astype(F32), 0)[None],
        jnp.zeros((2, width), F32),
    ])
    if own_kernels:
        grad_hidden, small, *owned = leave(grad_rows, small, [split(g) for g in grads])
    else:
        grad_hidden = give(grad_rows)
        owned = [scatter(g) for g in grads]
        small = lax.psum(small, ("dp", "tensor"))
    vb = 8 + inner // width
    return (
        output, grad_hidden, *owned, *owned_rest,
        small[vb], small[vb + 1], small[0], small[8:vb].reshape(inner), small[1], small[2], small[3], small[4], small[5],
    )


def solution(mesh):
    rows = P(None, ("dp", "tensor"), None)
    weight = P("dp", "tensor")
    return jax.shard_map(
        per_device,
        mesh=mesh,
        in_specs=(rows, P(None, "dp"), rows) + (weight,) * 6 + (P(),) * 9,
        out_specs=(rows, rows) + (weight,) * 6 + (P(),) * 9,
        check_vma=False,
    )
```

time: 905 us -> 381 us (0.42)
  waiting for transfers between devices: 533 us -> 0 us
  Pallas kernels: 133 us -> 333 us
  blocking collectives: 134 us -> 0 us
  matrix products: 36.6 us -> 19 us
  between operations: 15.1 us -> 1.14 us
  other arithmetic: 23.2 us -> 9.42 us
    reduce_scatter x8 -> x0, waiting for transfers between devices: 294 us -> none  [the longest x6 269 us: scatter(): g = lax.psum_scatter(g, 'dp', scatter_dimension=0, tiled=True)]
    pallas_call x2 -> x4, Pallas kernels: 69.8 us -> 268 us  [the longest x1 95.2 us: attend_forward(): pl.pallas_call(kernel, grid=(width // 128,), in_specs=[SMALL, spec, spec,...]
    all_gather x8 -> x0, waiting for transfers between devices: 147 us -> none  [the longest x6 145 us: gather(): return lax.all_gather(w, 'tensor', axis=1, tiled=True)]
    all_gather x4 -> x0, blocking collectives: 92.7 us -> none  [gather(): w = lax.all_gather(w, 'dp', axis=0, tiled=True)]
    unnamed x24 -> x0, waiting for transfers between devices: 47.3 us -> none
    ppermute x4 -> x0, waiting for transfers between devices: 44.8 us -> none  [the longest x1 25.8 us: per_device(): lax.ppermute(other(cotangent), 'tensor', swap)]
    psum x1 -> x0, blocking collectives: 40.8 us -> none  [per_device(): lax.psum((jnp.sum(d_query.astype(F32), 0), jnp.sum(d_value.astype(F32), 0...]
  transfers between devices with their start and end apart: 24 -> 0, of which waited for: 19 -> 0; matrix products, arithmetic and copies ran while one was open for 8% -> 0% of each run, Pallas kernels for 8% -> 0%
where the time goes in v2:
time: 381 us
  Pallas kernels  333 us (87%)
  matrix products  19 us (5%)
  local copies, waits for them, and re-layouts  17.9 us (5%)
  other arithmetic  9.42 us (2%)
    pallas_call x1, Pallas kernels, attend_forward(): pl.pallas_call(kernel, grid=(width // 128,), in_specs=[SMALL, spec, spec,...  95.2 us
    pallas_call x1, Pallas kernels, attend_backward(): pl.pallas_call(kernel, grid=(width // 128,), in_specs=[SMALL] + [spec] *...  82.8 us
    pallas_call x1, Pallas kernels, mlp(): pl.pallas_call(functools.partial(mlp_kernel, chunk), grid=(total // rows,...  65 us
    pallas_call x1, Pallas kernels, enter(): pl.pallas_call(kernel, in_specs=[HBM] * (1 + n), out_specs=[HBM] * (1 + n...  50.6 us
    pallas_call x1, Pallas kernels, leave(): pl.pallas_call(kernel, in_specs=[HBM, vmem] + [HBM] * n, out_specs=[HBM,...  39.8 us
    unnamed x72, local copies, waits for them, and re-layouts  9.97 us

profile of v2, /device:TPU:0, one launch (start us, length us, event | category | flops | bytes accessed | tf_op | source)
XLA Modules:
  0.0 380.9 jit_solution(6600887475743462049)
XLA Ops:
  0.7 50.6 %enter.1 = (bf16[1024,768]{1,0:T(8,128)(2,1)}, bf16[2,4,2,2,48,384]{5,4,3,2,1,0:T(8,128)(2,1)}, bf16[2,4,2,2,48,384]{5,4,3,2,1,0:T(8,128)(2,1)}, bf16[2,4,2,2,48,384]{5,4,3,2,1,0:T(8,128)(2,1)}) custom-call(bf16[2,512,768]{2,1,0:T(8,128)(2,1)} %refs_0_.1, bf16[48,384]{1,0:T(8,128)(2,1)} %refs_1_.1, bf16[48,384]{1,0:T(8,128)(2,1)} %refs_2_.1, ...), custom_call_target="tpu_custom_call" | custom-call | tf_op jit(solution)/shard_map/enter/pallas_call | solution.py:261
  51.3 2.0 fusion.20
  55.4 1.4 fusion.2.refs_3_
  58.7 1.3 pad_maximum_fusion.refs_2_
  60.6 1.0 fusion.23
  62.6 1.4 fusion.1.refs_1_
  64.7 1.2 pad_add_fusion.refs_0_.len_ref
  65.9 95.2 %attend_forward.1 = (bf16[1024,768]{1,0:T(8,128)(2,1)}, f32[1024,768]{1,0:T(8,128)}, bf16[1024,768]{1,0:T(8,128)(2,1)}, bf16[2,4,2,2,48,384]{5,4,3,2,1,0:T(8,128...) custom-call(s32[2]{0:T(128)} %pad_add_fusion.refs_0_.len_ref, ...), custom_call_target="tpu_custom_call" | custom-call | flops 3221225472 | bytes 9437184 | tf_op jit(solution)/shard_map/attend_forward/pallas_call | solution.py:353
  161.9 65.0 %mlp.1 = (bf16[1024,768]{1,0:T(8,128)(2,1)}, f32[1024,768]{1,0:T(8,128)}, bf16[1024,768]{1,0:T(8,128)(2,1)}, bf16[2,768,384]{2,1,0:T(8,128)(2,1)}, bf16[2,768,15...) custom-call(s32[2]{0:T(128)} %pad_add_fusion.refs_0_.len_ref, ...), custom_call_target="tpu_custom_call" | custom-call | flops 32614907904 | bytes 62914560 | tf_op jit(solution)/shard_map/mlp/pallas_call | solution.py:565
  226.9 82.8 %attend_backward.1 = (bf16[1024,768]{1,0:T(8,128)(2,1)}, bf16[1024,768]{1,0:T(8,128)(2,1)}, bf16[1024,768]{1,0:T(8,128)(2,1)}, bf16[2,512,768]{2,1,0:T(8,128)(2,...) custom-call(s32[2]{0:T(128)} %pad_add_fusion.refs_0_.len_ref, bf16[1024,768]{1,0:T(8,128)(2,1)} %fusion.1.refs_1_, ...), custom_call_target="tpu_custom_call" | custom-call | flops 8053063680 | bytes 15728640 | tf_op jit(solution)/shard_map/attend_backward/pallas_call | solution.py:457
  309.7 2.9 convolution_convert_fusion
  312.7 1.2 pad_maximum_fusion.3.refs_4_
  314.5 1.4 convolution_convert_fusion.1
  316.1 1.2 pad_maximum_fusion.2.refs_3_
  317.9 1.4 convolution_convert_fusion.2
  319.5 1.1 pad_maximum_fusion.1.refs_2_
  321.7 1.2 concatenate.31.refs_1_
  323.0 3.3 fusion.3
  326.3 1.4 fusion.7
  328.2 2.7 add_convert_fusion.refs_0_
  330.9 39.8 %leave.1 = (bf16[2,512,768]{2,1,0:T(8,128)(2,1)}, f32[16,768]{1,0:T(8,128)}, f32[48,384]{1,0:T(8,128)}, f32[48,384]{1,0:T(8,128)}, f32[48,384]{1,0:T(8,128)}) custom-call(bf16[1024,768]{1,0:T(8,128)(2,1)} %add_convert_fusion.refs_0_, f32[16,768]{1,0:T(8,128)} %concatenate.31.refs_1_, bf16[2,4,2,2,48,384]{5,4,3,2,1,0:T(8,128)(2,1)} %pad_maximum_fusion.1.refs_2_, ...), custom_call_target="tpu_custom_call" | custom-call | tf_op jit(solution)/shard_map/leave/pallas_call | solution.py:607
  370.7 1.6 slice_reduce_fusion
  373.7 1.1 copy.55
  375.7 1.1 copy.56
  (96 shorter events, 16.3 us)
Async XLA Ops:
  0.7 63.4 %copy-start = (s32[2,1]{0,1:T(1,128)S(1)}, s32[2,1]{0,1:T(1,128)}, u32[]{:S(2)}) copy-start(s32[2,1]{0,1:T(1,128)} %param.19) | copy-start | bytes 28
  51.3 2.1 copy-start.28
  53.2 3.5 copy-start.8
  65.9 95.2 %copy-start.20 = (f32[768]{0:T(1024)S(1)}, f32[768]{0:T(1024)}, u32[]{:S(2)}) copy-start(f32[768]{0:T(1024)} %param.29) | copy-start | bytes 9220
  65.9 95.2 %copy-start.21 = (f32[768]{0:T(1024)S(1)}, f32[768]{0:T(1024)}, u32[]{:S(2)}) copy-start(f32[768]{0:T(1024)} %param.31) | copy-start | bytes 9220
  65.9 95.2 %copy-start.22 = (f32[768]{0:T(1024)S(1)}, f32[768]{0:T(1024)}, u32[]{:S(2)}) copy-start(f32[768]{0:T(1024)} %param.32) | copy-start | bytes 9220
  65.9 95.3 %copy-start.23 = (f32[768]{0:T(1024)S(1)}, f32[768]{0:T(1024)}, u32[]{:S(2)}) copy-start(f32[768]{0:T(1024)} %param.33) | copy-start | bytes 9220
  65.9 95.3 %copy-start.24 = (f32[768]{0:T(1024)S(1)}, f32[768]{0:T(1024)}, u32[]{:S(2)}) copy-start(f32[768]{0:T(1024)} %param.34) | copy-start | bytes 9220
  65.9 95.3 %copy-start.25 = (f32[768]{0:T(1024)S(1)}, f32[768]{0:T(1024)}, u32[]{:S(2)}) copy-start(f32[768]{0:T(1024)} %param.35) | copy-start | bytes 9220
  226.9 82.8 %copy-start.29 = (bf16[1024,768]{1,0:T(8,128)(2,1)S(1)}, bf16[1024,768]{1,0:T(8,128)(2,1)}, u32[]{:S(2)}) copy-start(bf16[1024,768]{1,0:T(8,128)(2,1)} %get-tuple-element.47.h_ref) | copy-start | bytes 4718596
  312.7 1.8 copy-start.30
  316.1 1.8 copy-start.5
  319.5 1.8 copy-start.2
  323.0 3.3 copy-start.9
  323.0 3.3 copy-start.31
  326.3 1.9 copy-start.3
  330.9 42.9 %copy-start.4 = (bf16[2,512,768]{2,1,0:T(8,128)(2,1)S(1)}, bf16[2,512,768]{2,1,0:T(8,128)(2,1)}, u32[]{:S(2)}) copy-start(bf16[2,512,768]{2,1,0:T(8,128)(2,1)} %get-tuple-element.116) | copy-start | bytes 4718596
  373.7 2.0 copy-start.6
  375.7 1.8 copy-start.16
  375.7 2.5 copy-start.15
  375.7 3.1 copy-start.14
  375.7 3.7 copy-start.13
  375.7 4.4 %copy-start.12 = (f32[48,1536]{1,0:T(8,128)S(1)}, f32[48,1536]{1,0:T(8,128)}, u32[]{:S(2)}) copy-start(f32[48,1536]{1,0:T(8,128)} %get-tuple-element.123) | copy-start | bytes 884740
  375.7 5.1 %copy-start.1 = (s32[2,1]{0,1:T(1,128)S(1)}, s32[2,1]{0,1:T(1,128)}, u32[]{:S(2)}) copy-start(s32[2,1]{0,1:T(1,128)} %param.19) | copy-start | bytes 28
  (8 other events, 9.0 us)

commit v3 on v2

v3 whole, which is shorter than its diff:
```python
import functools
import math

import jax
import jax.numpy as jnp
from jax import lax
from jax.experimental import pallas as pl
from jax.experimental.pallas import tpu as pltpu
from jax.sharding import PartitionSpec as P

F32, BF16 = jnp.float32, jnp.bfloat16
DH = 64
S = jax.ShapeDtypeStruct
HBM = pl.BlockSpec(memory_space=pl.ANY)
SMALL = pl.BlockSpec(memory_space=pltpu.SMEM)
DMA = pltpu.SemaphoreType.DMA


def nt(a, b):
    return lax.dot_general(a, b, (((1,), (1,)), ((), ())), preferred_element_type=F32)


def nn(a, b):
    return lax.dot_general(a, b, (((1,), (0,)), ((), ())), preferred_element_type=F32)


def tn(a, b):
    return lax.dot_general(a, b, (((0,), (0,)), ((), ())), preferred_element_type=F32)


def split3(v):
    hi = v.astype(BF16).astype(F32)
    rest = v - hi
    mid = rest.astype(BF16).astype(F32)
    return hi, mid, rest - mid


class Place:
    def __init__(self):
        dp, t = lax.axis_index("dp"), lax.axis_index("tensor")
        z, x, c = dp // 4, (dp // 2) % 2, dp % 2
        self.z, self.x, self.c, self.t = z, x, c, t
        self.above, self.below, self.far = (z + 1) % 4, (z + 3) % 4, (z + 2) % 4
        at = lambda z, x, c, t: ((z * 2 + x) * 2 + c, t)
        self.up, self.down = at(self.above, x, c, t), at(self.below, x, c, t)
        self.across, self.beside, self.twin = at(z, 1 - x, c, t), at(z, x, c, 1 - t), at(z, x, 1 - c, t)

    def greet(self):
        barrier = pltpu.get_barrier_semaphore()
        for peer in (self.up, self.down, self.across, self.beside, self.twin):
            pl.semaphore_signal(barrier, inc=1, device_id=peer, device_id_type=pl.DeviceIdType.MESH)
        pl.semaphore_wait(barrier, 5)


def remote(src, dst, send, recv, peer):
    return pltpu.make_async_remote_copy(src, dst, send, recv, device_id=peer, device_id_type=pl.DeviceIdType.MESH)


def gather_stages(place, order, shard, full, first, count, send, recv, local):
    z, x, c, t = place.z, place.x, place.c, place.t
    lanes = pl.ds(first, count)
    part = count // 256 * 128
    low, high = pl.ds(first, part), pl.ds(first + part, count - part)
    own = full.at[t, z, x, c, :, lanes]
    here = shard.at[:, lanes]
    def move(i, view, peer, src=None):
        return remote(view if src is None else src, view, send.at[i], recv.at[i], peer)
    keep = pltpu.make_async_copy(here, own, local)
    everything = move(6, full.at[:, :, :, c, :, lanes], place.twin)
    if order[0] == "z":
        first_up, first_down = move(0, own, place.up, here), move(1, own, place.down, here)
        next_up = move(2, full.at[t, place.below, x, c, :, low], place.up)
        next_down = move(3, full.at[t, place.above, x, c, :, high], place.down)
        if order == "zxy":
            four, five = move(4, full.at[t, :, x, c, :, lanes], place.across), move(5, full.at[t, :, :, c, :, lanes], place.beside)
        else:
            four, five = move(4, full.at[t, :, x, c, :, lanes], place.beside), move(5, full.at[:, :, x, c, :, lanes], place.across)
        copies = [first_up, first_down, next_up, next_down, four, five, everything]
        def s0(): keep.start(); first_up.start(); first_down.start()
        def s1(): first_up.wait_recv(); next_up.start(); first_down.wait_recv(); next_down.start()
        def s2(): next_up.wait_recv(); next_down.wait_recv(); keep.wait(); four.start()
        def s3(): four.wait_recv(); five.start()
        def s4(): five.wait_recv(); everything.start()
    else:
        if order == "xyz":
            one, two = move(0, own, place.across, here), move(1, full.at[t, z, :, c, :, lanes], place.beside)
        else:
            one, two = move(0, own, place.beside, here), move(1, full.at[:, z, x, c, :, lanes], place.across)
        first_up, first_down = move(2, full.at[:, z, :, c, :, lanes], place.up), move(3, full.at[:, z, :, c, :, lanes], place.down)
        next_up = move(4, full.at[0, place.below, :, c, :, lanes], place.up)
        next_down = move(5, full.at[1, place.above, :, c, :, lanes], place.down)
        copies = [one, two, first_up, first_down, next_up, next_down, everything]
        def s0(): keep.start(); one.start()
        def s1(): one.wait_recv(); keep.wait(); two.start()
        def s2(): two.wait_recv(); first_up.start(); first_down.start()
        def s3(): first_up.wait_recv(); next_up.start(); first_down.wait_recv(); next_down.start()
        def s4(): next_up.wait_recv(); next_down.wait_recv(); everything.start()
    def s5():
        everything.wait_recv()
        for copy in copies: copy.wait_send()
    return [s0, s1, s2, s3, s4, s5]


def add_blocks(count, dst, *srcs):
    def body(i, _):
        ref = dst(i)
        total = ref[...].astype(F32)
        for s in srcs: total = total + s(i)[...].astype(F32)
        ref[...] = total.astype(ref.dtype)
        return 0
    lax.fori_loop(0, count, body, 0)


def reduce_scratch(order, rows, lanes):
    V = lambda *s: pltpu.VMEM(s + (rows, lanes), BF16)
    base = [V(2, 4, 2), V(2, 4, 2)]
    if order == "yxz": base += [V(4, 2), V(4), V(), V(2)]
    elif order == "xyz": base += [V(2, 4), V(4), V(), V(2)]
    else: base += [V(2, 2), V(2, 2, 2), V(2), V()]
    return base + [pltpu.SemaphoreType.DMA((7,)), pltpu.SemaphoreType.DMA((7,)), pltpu.SemaphoreType.DMA]


def reduce_stages(place, order, grad, first, count, out, scratch):
    held, r0, r1, r2, r3, r4, send, recv, local = scratch
    z, x, c, t = place.z, place.x, place.c, place.t
    lanes = pl.ds(first, count)
    part = count // 256 * 128
    low, high = pl.ds(0, part), pl.ds(part, count - part)
    load = pltpu.make_async_copy(grad.at[:, :, :, c, :, lanes], held, local)
    def move(i, src, dst, peer):
        return remote(src, dst, send.at[i], recv.at[i], peer)
    c0 = move(0, grad.at[:, :, :, 1 - c, :, lanes], r0, place.twin)
    at3 = lambda ref: (lambda i: ref.at[i // 8, (i // 2) % 4, i % 2])
    def s0(): load.start(); c0.start()
    if order[0] != "z":
        if order == "yxz":
            c1, c2 = move(1, held.at[1 - t], r1, place.beside), move(2, held.at[t, :, 1 - x], r2, place.across)
            def add1(): add_blocks(8, lambda i: held.at[t, i // 2, i % 2], lambda i: r1.at[i // 2, i % 2])
        else:
            c1, c2 = move(1, held.at[:, :, 1 - x], r1, place.across), move(2, held.at[1 - t, :, x], r2, place.beside)
            def add1(): add_blocks(8, lambda i: held.at[i // 4, i % 4, x], lambda i: r1.at[i // 4, i % 4])
        mine = lambda k: held.at[t, k, x]
        c3 = move(3, held.at[t, place.far, x, :, low], r3.at[:, low], place.up)
        c4 = move(4, held.at[t, place.far, x, :, high], r3.at[:, high], place.down)
        c5, c6 = move(5, mine(place.above), r4.at[0], place.up), move(6, mine(place.below), r4.at[1], place.down)
        def s1(): load.wait(); c0.wait_recv(); add_blocks(16, at3(held), at3(r0)); c1.start()
        def s2(): c1.wait_recv(); add1(); c2.start()
        def s3(): c2.wait_recv(); add_blocks(4, mine, lambda k: r2.at[k]); c3.start(); c4.start()
        def s4():
            c3.wait_recv()
            v = held.at[t, place.above, x, :, low]; v[...] = (v[...].astype(F32) + r3[:, low].astype(F32)).astype(BF16)
            c5.start()
            c4.wait_recv()
            v = held.at[t, place.below, x, :, high]; v[...] = (v[...].astype(F32) + r3[:, high].astype(F32)).astype(BF16)
            c6.start()
        def s5():
            c5.wait_recv(); c6.wait_recv()
            out[:, lanes] = mine(z)[...].astype(F32) + r4[0].astype(F32) + r4[1].astype(F32)
            for copy in (c0, c1, c2, c3, c4, c5, c6): copy.wait_send()
    else:
        c1, c2 = move(1, held.at[0, place.far], r1.at[0], place.up), move(2, held.at[1, place.far], r1.at[1], place.down)
        c3, c4 = move(3, held.at[:, place.above], r2.at[0], place.up), move(4, held.at[:, place.below], r2.at[1], place.down)
        if order == "zyx":
            c5, c6 = move(5, held.at[1 - t, z], r3, place.beside), move(6, held.at[t, z, 1 - x], r4, place.across)
            def add5(): add_blocks(2, lambda k: held.at[t, z, k], lambda k: r3.at[k])
        else:
            c5, c6 = move(5, held.at[:, z, 1 - x], r3, place.across), move(6, held.at[1 - t, z, x], r4, place.beside)
            def add5(): add_blocks(2, lambda k: held.at[k, z, x], lambda k: r3.at[k])
        def s1(): load.wait(); c0.wait_recv(); add_blocks(16, at3(held), at3(r0)); c1.start(); c2.start()
        def s2():
            c1.wait_recv(); add_blocks(2, lambda k: held.at[0, place.above, k], lambda k: r1.at[0, k]); c3.start()
            c2.wait_recv(); add_blocks(2, lambda k: held.at[1, place.below, k], lambda k: r1.at[1, k]); c4.start()
        def s3():
            c3.wait_recv(); c4.wait_recv()
            add_blocks(4, lambda k: held.at[k // 2, z, k % 2], lambda k: r2.at[0, k // 2, k % 2], lambda k: r2.at[1, k // 2, k % 2])
            c5.start()
        def s4(): c5.wait_recv(); add5(); c6.start()
        def s5():
            c6.wait_recv()
            out[:, lanes] = held[t, z, x].astype(F32) + r4[...].astype(F32)
            for copy in (c0, c1, c2, c3, c4, c5, c6): copy.wait_send()
    return [s0, s1, s2, s3, s4, s5]


FRONT_ITEMS = {
    "q": (0, 0, 1, "zyx"),
    "k": (1, 0, 1, "zyx"),
    "v": (2, 0, 1, "yxz"),
    "o0": (3, 0, 1, "xyz"),
    "i0": (4, 0, 4, "xyz"),
    "i1": (4, 1, 4, "zxy"),
    "i2": (4, 2, 4, "zxy"),
    "i3": (4, 3, 4, "zxy"),
    "b0": (5, 0, 4, "zyx"),
    "b1": (5, 1, 4, "xyz"),
    "b2": (5, 2, 4, "zyx"),
    "b3": (5, 3, 4, "zyx"),
}
BACK_ITEMS = {
    "q": (0, 0, 1, "yxz"),
    "k": (1, 0, 1, "xyz"),
    "v": (2, 0, 1, "zxy"),
    "o0": (3, 0, 1, "zyx"),
    "i0": (4, 0, 4, "zxy"),
    "i1": (4, 1, 4, "xyz"),
    "i2": (4, 2, 4, "zyx"),
    "i3": (4, 3, 4, "zyx"),
    "b0": (5, 0, 4, "xyz"),
    "b1": (5, 1, 4, "xyz"),
    "b2": (5, 2, 4, "zxy"),
    "b3": (5, 3, 4, "yxz"),
}
FRONT_ORDER = (
    (("q", 0), ("v", 0), ("h1", 0), ("k", 0), ("v", 1), ("q", 1), ("b2", 0), ("k", 1), ("q", 2), ("v", 2), ("h1", 1), ("b2", 1), ("i1", 0), ("i0", 0), ("k", 2), ("i2", 0), ("b1", 0), ("h0", 0), ("h2", 0), ("h3", 0), ("o0", 0), ("i0", 1), ("q", 3), ("b1", 1), ("o0", 1), ("k", 3), ("v", 3), ("b3", 0), ("b2", 2), ("i1", 1), ("h0", 1), ("i2", 1), ("q", 4), ("v", 4), ("q", 5), ("h2", 1), ("b3", 1), ("i1", 2), ("i3", 0), ("v", 5), ("i2", 2), ("k", 4), ("b0", 0), ("b3", 2), ("h3", 1),),
    (("k", 5),),
    (),
    (("i1", 3), ("i0", 2), ("i2", 3), ("i3", 1), ("b0", 1), ("b1", 2), ("o0", 2), ("b2", 3),),
    (),
    (("b3", 3),),
    (("i0", 3), ("i3", 2), ("b0", 2), ("b2", 4),),
    (("i1", 4),),
    (("b2", 5),),
    (("i1", 5), ("b3", 4), ("i2", 4), ("b1", 3),),
    (("b3", 5), ("i3", 3), ("b0", 3),),
    (("i2", 5), ("o0", 3),),
    (("i0", 4),),
    (("i3", 4), ("b1", 4), ("i0", 5), ("b0", 4),),
    (("i3", 5), ("o0", 4),),
    (("b1", 5), ("b0", 5), ("o0", 5),),
)
BACK_ORDER = (
    (),
    (),
    (("b0", 0),),
    (("b0", 1),),
    (("i2", 0), ("i0", 0), ("i3", 0), ("b2", 0),),
    (("o0", 0), ("i2", 1), ("i0", 1), ("i3", 1), ("b0", 2), ("b2", 1),),
    (("o0", 1), ("b3", 0), ("i2", 2), ("b0", 3),),
    (("b1", 0), ("i1", 0), ("b3", 1), ("i0", 2), ("i3", 2),),
    (("b1", 1), ("i1", 1), ("o0", 2), ("b2", 2),),
    (("b3", 2),),
    (("b1", 2), ("i2", 3), ("b0", 4),),
    (),
    (("b1", 3), ("i1", 2), ("q", 0), ("b3", 3), ("i2", 4), ("i0", 3), ("i3", 3),),
    (("k", 0), ("q", 1), ("i1", 3), ("sm", 0), ("o0", 3), ("i2", 5), ("i0", 4), ("k", 1), ("sm", 1), ("i3", 4),),
    (("v", 0),),
    (("r2", 0), ("v", 1), ("b1", 4), ("q", 2), ("o0", 4), ("k", 2), ("i1", 4), ("b3", 4), ("sm", 2), ("i0", 5), ("r0", 0), ("i3", 5), ("v", 2), ("r2", 1), ("b2", 3), ("b1", 5), ("q", 3), ("o0", 5), ("r3", 0), ("k", 3), ("i1", 5), ("sm", 3), ("b3", 5), ("r1", 0), ("b0", 5), ("b2", 4),),
    (("r0", 1), ("v", 3), ("q", 4), ("k", 4), ("r3", 1), ("sm", 4), ("v", 4), ("q", 5), ("k", 5), ("r1", 1), ("sm", 5), ("b2", 5), ("v", 5),),
)


def fold_stages(place, part, got, send, recv):
    flip = place.z % 2
    near = jax.tree.map(lambda u, d: u + flip * (d - u), place.up, place.down)
    next_ = jax.tree.map(lambda u, d: d + flip * (u - d), place.up, place.down)
    peers = (place.twin, place.across, place.beside, near, next_)
    copies = [remote(part, got.at[i], send.at[i], recv.at[i], peer) for i, peer in enumerate(peers)]
    def stage(i):
        def run():
            if i > 0:
                copies[i - 1].wait()
                part[...] = part[...] + got[i - 1]
            if i < 5:
                copies[i].start()
        return run
    return [stage(i) for i in range(6)]


def swap(away, into, send, recv, peer, parts=4):
    size = away.shape[0] // parts
    plans = []
    for i in range(parts):
        r = pl.ds(i * size, size)
        give = remote(away.at[r], into.at[r], send.at[i], recv.at[i], peer)
        plans.append([give.start, give.wait])
    return plans


def whole(s):
    return pl.BlockSpec(s, lambda i: (0,) * len(s), pipeline_mode=pl.Buffered(1))


def forward_pair(bq, hook, len_ref, q_ref, k_ref, v_ref, o_ref, lse_ref):
    rows = q_ref.shape[0]
    n = len_ref[0]
    lane = lax.broadcasted_iota(jnp.int32, (1, 128), 1)
    krow = lax.broadcasted_iota(jnp.int32, (rows, 1), 0)
    kbias = jnp.where((krow + len_ref[1]) % rows < n, 0.0, -1e9)
    first = lane < DH
    for i in range(rows // bq):
        if i % (rows // bq // 2) == 0:
            hook(i * 2 * bq // rows)
            k = k_ref[...].astype(F32)
            v = v_ref[...]
            kas = []
            for h in range(2):
                own = lane // DH == h
                kas.append(jnp.where(own, k, jnp.where(lane == DH * (1 - h), kbias, 0.0)).astype(BF16))
        place = pl.ds(i * bq, bq)
        q = q_ref[place].astype(F32)
        os_, ls = [], []
        for h in range(2):
            own = lane // DH == h
            qa = jnp.where(own, q, jnp.where(lane == DH * (1 - h), 1.0, 0.0)).astype(BF16)
            s = nt(qa, kas[h])
            m = jnp.max(s, axis=1, keepdims=True)
            p = jnp.exp(s - m)
            l = jnp.sum(p, axis=1, keepdims=True)
            os_.append(nn(p.astype(BF16), v) * (1.0 / l))
            ls.append(m + jnp.log(l))
        o_ref[place] = jnp.where(first, os_[0], os_[1]).astype(BF16)
        lse_ref[place] = jnp.where(first, ls[1], ls[0])


def attend_forward(length, q, k, v, bq=256):
    rows, width = q.shape
    spec = pl.BlockSpec((rows, 128), lambda i: (0, i))
    return pl.pallas_call(
        functools.partial(forward_pair, bq, lambda i: None),
        grid=(width // 128,),
        in_specs=[SMALL, spec, spec, spec],
        out_specs=[spec, spec],
        out_shape=[S((rows, width), BF16), S((rows, width), F32)],
        compiler_params=pltpu.CompilerParams(vmem_limit_bytes=56 << 20),
        name="attend_forward",
    )(length, q, k, v)


def run(plans, events):
    for name, stage in events:
        plans[name][stage]()


def front(length, hidden, shards, b_query, b_value, bq=256):
    n = len(shards)
    rows, width = 2 * hidden.shape[1], hidden.shape[2]
    half, pairs = width // 2, width // 128
    items = [(name, w, shards[w].shape[1] // parts * i, shards[w].shape[1] // parts, order) for name, (w, i, parts, order) in FRONT_ITEMS.items()]

    def kernel(*refs):
        len_ref, pair_ref, given, bq_ref, bv_ref = refs[0], refs[1], refs[2 : 2 + n], refs[2 + n], refs[3 + n]
        refs = refs[4 + n :]
        o_ref, lse_ref, outs = refs[0], refs[1], refs[2 : 6 + n]
        refs = refs[6 + n :]
        rows_s, q_s, k_s, v_s, near, (send, recv, out_sem), sems = refs[0], refs[1], refs[2], refs[3], refs[4:7], refs[7:10], refs[10:]
        step = pl.program_id(0)
        place = Place()
        fulls = list(near) + list(outs[7:])
        local = rows // 2
        keep = pltpu.make_async_copy(pair_ref.at[place.t], rows_s.at[pl.ds(0, local)], out_sem.at[7])
        plans = {
            f"h{i}": plan
            for i, plan in enumerate(swap(pair_ref.at[1 - place.t], rows_s.at[pl.ds(local, local)], send, recv, place.beside))
        }
        for i, (name, w, at, count, order) in enumerate(items):
            plans[name] = gather_stages(place, order, given[w], fulls[w], at, count, *sems[3 * i : 3 * i + 3])
        stores = [pltpu.make_async_copy(src, dst, out_sem.at[i]) for i, (src, dst) in enumerate(zip((rows_s, q_s, k_s, v_s) + tuple(near), outs))]

        def project(full, dst, bias, scale):
            def block(i, _):
                r = pl.ds(pl.multiple_of(i * 256, 256), 256)
                for t in range(2):
                    v = nn(rows_s[r], full[t].reshape(width, half))
                    if bias is not None:
                        v = v + bias[:, t * half : (t + 1) * half]
                    dst[r, t * half : (t + 1) * half] = (v * scale).astype(BF16)
                return 0
            lax.fori_loop(0, rows // 256, block, 0)

        @pl.when(step == 0)
        def _():
            keep.start()
            place.greet()
            run(plans, FRONT_ORDER[0])
            keep.wait()
            project(near[0], q_s, bq_ref, 0.125)
            run(plans, FRONT_ORDER[1])
            project(near[1], k_s, None, 1.0)
            run(plans, FRONT_ORDER[2])
            project(near[2], v_s, bv_ref, 1.0)
            for store in stores:
                store.start()

        def hook(part):
            for i in range(pairs):
                @pl.when(step == 1 + i)
                def _():
                    run(plans, FRONT_ORDER[3 + 2 * i + part])

        @pl.when(step > 0)
        def _():
            cols = pl.ds(pl.multiple_of((step - 1) * 128, 128), 128)
            forward_pair(bq, hook, len_ref, q_s.at[:, cols], k_s.at[:, cols], v_s.at[:, cols], o_ref, lse_ref)

        @pl.when(step == pairs)
        def _():
            run(plans, FRONT_ORDER[3 + 2 * pairs])
            for store in stores:
                store.wait()

    spec = pl.BlockSpec((rows, 128), lambda i: (0, jnp.maximum(i - 1, 0)))
    flat = S((rows, width), BF16)
    full = [S((2, 4, 2, 2) + s.shape, BF16) for s in shards]
    V = pltpu.VMEM
    return pl.pallas_call(
        kernel,
        grid=(1 + pairs,),
        in_specs=[SMALL, HBM] + [HBM] * n + [whole((1, width))] * 2,
        out_specs=[spec, spec] + [HBM] * (4 + n),
        out_shape=[flat, S((rows, width), F32), flat, flat, flat, flat] + full,
        scratch_shapes=[V((rows, width), BF16)] * 4 + [V(f.shape, BF16) for f in full[:3]] + [DMA((4,)), DMA((4,)), DMA((8,))]
        + [s for _ in items for s in (DMA((7,)), DMA((7,)), DMA)],
        cost_estimate=pl.CostEstimate(flops=10 * rows * rows * width, bytes_accessed=40 << 20, transcendentals=rows * rows * 12),
        compiler_params=pltpu.CompilerParams(collective_id=1, has_side_effects=True, vmem_limit_bytes=56 << 20),
        name="front",
    )(length, hidden, *shards, b_query, b_value)


def backward_pair(bk, hook, len_ref, q_ref, k_ref, v_ref, d_ref, o_ref, lse_ref, dq_ref, dk_ref, dv_ref, qa_s, ka_s, va_s, da_s, acc):
    rows = q_ref.shape[0]
    n = len_ref[0]
    lane = lax.broadcasted_iota(jnp.int32, (1, 128), 1)
    krow = lax.broadcasted_iota(jnp.int32, (rows, 1), 0)
    kbias = jnp.where((krow + len_ref[1]) % rows < n, 0.0, -1e9)
    d = d_ref[...].astype(F32)
    prod = d * o_ref[...].astype(F32)
    hi, mid, lo = split3(-lse_ref[...])
    for h in range(2):
        own = lane // DH == h
        sp = DH * (1 - h)
        def pick(a, b, c, e):
            return jnp.where(lane == sp, a, jnp.where(lane == sp + 1, b, jnp.where(lane == sp + 2, c, jnp.where(lane == sp + 3, e, 0.0))))
        dh, dm, dl = split3(-jnp.sum(jnp.where(own, prod, 0.0), axis=1, keepdims=True))
        qa_s[h] = jnp.where(own, q_ref[...].astype(F32), pick(hi, mid, lo, 1.0)).astype(BF16)
        ka_s[h] = jnp.where(own, k_ref[...].astype(F32), pick(1.0, 1.0, 1.0, kbias)).astype(BF16)
        da_s[h] = jnp.where(own, d, pick(dh, dm, dl, 0.0)).astype(BF16)
        va_s[h] = jnp.where(own, v_ref[...].astype(F32), pick(1.0, 1.0, 1.0, 0.0)).astype(BF16)
    first = lane < DH
    upper = lax.broadcasted_iota(jnp.int32, (128, 1), 0) < DH
    for kb in range(0, rows, bk):
        if kb % (rows // 2) == 0:
            hook(kb * 2 // rows)
        dks, dvs, dqs = [], [], []
        for h in range(2):
            p = jnp.exp(nt(ka_s[h, kb : kb + bk], qa_s[h]))
            ds = (p * nt(va_s[h, kb : kb + bk], da_s[h])).astype(BF16)
            dvs.append(nn(p.astype(BF16), d_ref[...]))
            dks.append(nn(ds, q_ref[...]))
            dqs.append(tn(k_ref[kb : kb + bk], ds))
        dk_ref[kb : kb + bk] = jnp.where(first, dks[0], dks[1]).astype(BF16)
        dv_ref[kb : kb + bk] = jnp.where(first, dvs[0], dvs[1]).astype(BF16)
        dq = jnp.where(upper, dqs[0], dqs[1])
        if kb == 0:
            acc[...] = dq
        else:
            acc[...] += dq
    dq_ref[...] = (acc[...].T * 0.125).astype(BF16)


def pair_scratch(rows):
    aug = pltpu.VMEM((2, rows, 128), BF16)
    return [aug, aug, aug, aug, pltpu.VMEM((128, rows), F32)]


def attend_backward(length, q, k, v, d, o, lse, bk=256):
    rows, width = q.shape
    spec = pl.BlockSpec((rows, 128), lambda i: (0, i))
    return pl.pallas_call(
        functools.partial(backward_pair, bk, lambda i: None),
        grid=(width // 128,),
        in_specs=[SMALL] + [spec] * 6,
        out_specs=[spec] * 3,
        out_shape=[S((rows, width), BF16)] * 3,
        scratch_shapes=pair_scratch(rows),
        compiler_params=pltpu.CompilerParams(vmem_limit_bytes=56 << 20),
        name="attend_backward",
    )(length, q, k, v, d, o, lse)


def back(length, q, k, v, d, o, lse, rows_in, fulls, grad_one, small, grads, bk=256):
    n = len(grads)
    rows, width = q.shape
    half, pairs = width // 2, width // 128
    shards = [(grads[0].shape[4], half)] * 3 + [g.shape[4:] for g in grads]
    items = [(name, w, shards[w][1] // parts * i, shards[w][1] // parts, order) for name, (w, i, parts, order) in BACK_ITEMS.items()]
    vb = small.shape[0] - 4

    def kernel(*refs):
        main_in, rows_ref, full, one_ref, small_ref, given = refs[:7], refs[7], refs[8:11], refs[11], refs[12], refs[13 : 13 + n]
        refs = refs[13 + n :]
        pair_ref, sum_ref, outs = refs[0], refs[1], refs[2 : 5 + n]
        refs = refs[5 + n :]
        dq_s, dk_s, dv_s, rT, gr_s = refs[:5]
        own, part, got, fold_send, fold_recv, (send, recv, local_sem) = refs[5:8], refs[8], refs[9], refs[10], refs[11], refs[12:15]
        main_scratch, scratch = refs[15:20], refs[20:]
        step = pl.program_id(0)
        place = Place()
        local = rows // 2
        keep = pltpu.make_async_copy(gr_s.at[pl.ds(0, local)], pair_ref.at[place.t], local_sem)
        plans = {
            f"r{i}": plan
            for i, plan in enumerate(swap(gr_s.at[pl.ds(local, local)], pair_ref.at[place.t], send, recv, place.beside))
        }
        plans["sm"] = fold_stages(place, part, got, fold_send, fold_recv)
        sources = list(own) + list(given)
        for i, (name, w, at, count, order) in enumerate(items):
            plans[name] = reduce_stages(place, order, sources[w], at, count, outs[w], scratch[9 * i : 9 * i + 9])

        @pl.when(step == 0)
        def _():
            place.greet()

        def hook(j):
            for i in range(pairs):
                @pl.when(step == i)
                def _():
                    run(plans, BACK_ORDER[2 * i + j])

        @pl.when(step < pairs)
        def _():
            cols = pl.ds(pl.multiple_of(step * 128, 128), 128)
            backward_pair(bk, hook, *main_in, dq_s.at[:, cols], dk_s.at[:, cols], dv_s.at[:, cols], *main_scratch)

        @pl.when(step == pairs)
        def _():
            at = 2 * pairs
            rT[...] = rows_ref[...].T
            part[...] = small_ref[...]
            for i, d_s in enumerate((dq_s, dk_s, dv_s)):
                for t in range(2):
                    own[i][t] = nn(rT[...], d_s[:, t * half : (t + 1) * half]).astype(BF16).reshape(own[i].shape[1:])
                if i == 0:
                    part[vb : vb + 1] = colsum(dq_s[...].astype(F32))
                    part[vb + 1 : vb + 2] = colsum(dv_s[...].astype(F32))
                run(plans, BACK_ORDER[at + i])
            for j in (1, 0):
                def block(i, _):
                    r = pl.ds(pl.multiple_of(i * 256, 256), 256)
                    total = one_ref[r]
                    for d_s, w in zip((dq_s, dk_s, dv_s), full):
                        for t in range(2):
                            total = total + nt(d_s[r, t * half : (t + 1) * half], w[t])
                    gr_s[r] = total.astype(BF16)
                    return 0
                lax.fori_loop(j * (rows // 512), (j + 1) * (rows // 512), block, 0)
                if j == 0:
                    keep.start()
                run(plans, BACK_ORDER[at + 4 - j])
            keep.wait()
            sum_ref[...] = part[...]

    spec = pl.BlockSpec((rows, 128), lambda i: (0, jnp.minimum(i, pairs - 1)))
    V = pltpu.VMEM
    flat = V((rows, width), BF16)
    outs = [S(s, F32) for s in shards]
    return pl.pallas_call(
        kernel,
        grid=(pairs + 1,),
        in_specs=[SMALL] + [spec] * 6 + [whole((rows, width))] + [whole(f.shape) for f in fulls] + [whole((rows, width)), whole(small.shape)] + [HBM] * n,
        out_specs=[HBM, whole(small.shape)] + [whole(s) for s in shards],
        out_shape=[S((2, rows // 2, width), BF16), S(small.shape, F32)] + outs,
        scratch_shapes=[flat, flat, flat, V((width, rows), BF16), flat]
        + [V((2, 4, 2, 2) + shards[0], BF16)] * 3
        + [V(small.shape, F32), V((5,) + small.shape, F32), DMA((5,)), DMA((5,)), DMA((4,)), DMA((4,)), DMA]
        + pair_scratch(rows)
        + [s for _, w, f, c, o in items for s in reduce_scratch(o, shards[w][0], c)],
        cost_estimate=pl.CostEstimate(flops=20 * rows * rows * width, bytes_accessed=60 << 20, transcendentals=rows * rows * 12),
        compiler_params=pltpu.CompilerParams(collective_id=2, has_side_effects=True, vmem_limit_bytes=63 << 20),
        name="back",
    )(length, q, k, v, d, o, lse, rows_in, *fulls, grad_one, small, *grads)


def norm_parts(v):
    c = v - jnp.mean(v, axis=-1, keepdims=True)
    r = lax.rsqrt(jnp.mean(c * c, axis=-1, keepdims=True) + 1e-5)
    return c * r, r


def norm_back(n, r, dyg):
    return r * (dyg - jnp.mean(dyg, axis=-1, keepdims=True) - n * jnp.mean(dyg * n, axis=-1, keepdims=True))


def colsum(v):
    return jnp.sum(v, axis=0, keepdims=True)


def mlp_up_kernel(chunk, a_ref, h_ref, wo_ref, wi_ref, wb_ref, vec_ref, bi_ref, out_ref, mid_ref, v1_ref, v2_ref, act, gp, b2):
    half, inner = wo_ref.shape[2], wi_ref.shape[2]
    b_out, b_back, gain_one, shift_one, gain_two, shift_two = [vec_ref[i : i + 1] for i in range(6)]
    v1 = h_ref[...].astype(F32) + (nt(a_ref[:, :half], wo_ref[0]) + nt(a_ref[:, half:], wo_ref[1])) + b_out
    v1_ref[...] = v1
    n1, r1 = norm_parts(v1)
    normed = n1 * gain_one + shift_one
    mid = normed.astype(BF16)
    mid_ref[...] = mid
    b2[...] = normed + b_back

    def up(i, _):
        t = i // (inner // chunk)
        cols = pl.ds(pl.multiple_of(i % (inner // chunk) * chunk, chunk), chunk)
        hp = nn(mid, wi_ref[t, :, cols]) + bi_ref[t, :, cols]
        half_up = 0.5 + 0.5 * lax.erf(hp * math.sqrt(0.5))
        a = (hp * half_up).astype(BF16)
        act[t, :, cols] = a
        gp[t, :, cols] = (half_up + hp * (jnp.exp(hp * hp * -0.5) * (1.0 / math.sqrt(2 * math.pi)))).astype(BF16)
        b2[...] += nt(a, wb_ref[t, :, cols])
        return 0

    lax.fori_loop(0, 2 * inner // chunk, up, 0)
    v2_ref[...] = b2[...]
    n2, r2 = norm_parts(b2[...])
    out_ref[...] = (n2 * gain_two + shift_two).astype(BF16)


def mlp_up(a, h, wo, wi, wb, vec, bi, rows=256, chunk=768):
    total, width = a.shape
    inner = wi.shape[2]
    row = pl.BlockSpec((rows, width), lambda i: (i, 0))
    wide = pl.BlockSpec((2, rows, inner), lambda i: (0, i, 0))
    return pl.pallas_call(
        functools.partial(mlp_up_kernel, chunk),
        grid=(total // rows,),
        in_specs=[row, row] + [whole(s.shape) for s in (wo, wi, wb, vec, bi)],
        out_specs=[row, row, row, row, wide, wide],
        out_shape=[S((total, width), BF16), S((total, width), BF16), S((total, width), F32), S((total, width), F32), S((2, total, inner), BF16), S((2, total, inner), BF16)],
        scratch_shapes=[pltpu.VMEM((rows, width), F32)],
        cost_estimate=pl.CostEstimate(flops=total * width * (8 * inner + 2 * width), bytes_accessed=40 << 20, transcendentals=4 * total * inner),
        compiler_params=pltpu.CompilerParams(vmem_limit_bytes=60 << 20),
        name="mlp_up",
    )(a, h, wo, wi, wb, vec, bi)


def mlp_down_kernel(len_ref, a_ref, mid_ref, near_ref, far_ref, v1_ref, v2_ref, wo_ref, vec_ref, wi_ref, wb_ref, act_ref, gp_ref,
                    g1_ref, ga_ref, gwo_ref, gwi_ref, gwb_ref, small_ref, gbi_ref, back, btT, midT, gn):
    step = pl.program_id(0)
    rows, half, block = a_ref.shape[0], wo_ref.shape[2], 256
    b_out, b_back, gain_one, shift_one, gain_two, shift_two = [vec_ref[i : i + 1] for i in range(6)]

    @pl.when(step == 0)
    def _():
        small_ref[...] = jnp.zeros_like(small_ref)
        midT[...] = mid_ref[...].T
        for b in range(rows // block):
            r = slice(b * block, (b + 1) * block)
            n2, r2 = norm_parts(v2_ref[r])
            place = (b * block + lax.broadcasted_iota(jnp.int32, (block, 1), 0) + len_ref[1]) % rows
            c = (near_ref if b < rows // block // 2 else far_ref)[(b * block) % (rows // 2) : (b * block) % (rows // 2) + block]
            go = c.astype(F32) * jnp.where(place < len_ref[0], 1.0, 0.0)
            grad_two = norm_back(n2, r2, go * gain_two)
            bt = grad_two.astype(BF16)
            back[r] = bt
            btT[:, r] = bt.T
            gn[r] = grad_two
            small_ref[1:2] += colsum(grad_two)
            small_ref[4:5] += colsum(go * n2)
            small_ref[5:6] += colsum(go)

    gb = (nn(back[...], wb_ref[0]) * gp_ref[0].astype(F32)).astype(BF16)
    gbi_ref[0] = colsum(gb.astype(F32))
    gwb_ref[0] = nn(btT[...], act_ref[0]).astype(BF16)
    gwi_ref[0] = nn(midT[...], gb).astype(BF16)
    gn[...] += nt(gb, wi_ref[0])

    @pl.when(step == pl.num_programs(0) - 1)
    def _():
        for b in range(rows // block):
            r = slice(b * block, (b + 1) * block)
            g = gn[r]
            n1, r1 = norm_parts(v1_ref[r])
            grad_one = norm_back(n1, r1, g * gain_one)
            bo = grad_one.astype(BF16)
            back[r] = bo
            g1_ref[r] = grad_one
            small_ref[0:1] += colsum(grad_one)
            small_ref[2:3] += colsum(g * n1)
            small_ref[3:4] += colsum(g)
            for t in range(2):
                ga_ref[r, t * half : (t + 1) * half] = nn(bo, wo_ref[t]).astype(BF16)
        btT[...] = back[...].T
        for t in range(2):
            gwo_ref[t] = nn(btT[...], a_ref[:, t * half : (t + 1) * half]).astype(BF16)


def mlp_down(length, a, mid, near, far, v1, v2, wo, wi, wb, act, gp, vec, bi, chunk=512):
    rows, width = a.shape
    inner = wi.shape[2]
    m = inner // chunk
    tall = pl.BlockSpec((1, rows, chunk), lambda i: (i // m, 0, i % m))
    weight = pl.BlockSpec((1, width, chunk), lambda i: (i // m, 0, i % m))
    thin = pl.BlockSpec((1, 1, chunk), lambda i: (i // m, 0, i % m))
    V = pltpu.VMEM
    return pl.pallas_call(
        mlp_down_kernel,
        grid=(2 * m,),
        in_specs=[SMALL] + [whole(s.shape) for s in (a, mid, near, far, v1, v2, wo, vec)] + [weight, weight, tall, tall],
        out_specs=[whole((rows, width)), whole((rows, width)), whole(wo.shape), weight, weight, whole(vec.shape), thin],
        out_shape=[S((rows, width), F32), S((rows, width), BF16), S(wo.shape, BF16), S(wi.shape, BF16), S(wb.shape, BF16), S(vec.shape, F32), S(bi.shape, F32)],
        scratch_shapes=[V((rows, width), BF16), V((width, rows), BF16), V((width, rows), BF16), V((rows, width), F32)],
        cost_estimate=pl.CostEstimate(flops=rows * width * (16 * inner + 4 * width), bytes_accessed=60 << 20, transcendentals=0),
        compiler_params=pltpu.CompilerParams(vmem_limit_bytes=60 << 20),
        name="mlp_down",
    )(length, a, mid, near, far, v1, v2, wo, vec, wi, wb, act, gp)


def per_device(
    hidden, lengths, cotangent, w_query, w_key, w_value, w_out, w_in, w_back,
    b_query, b_value, b_out, b_in, b_back, gain_one, shift_one, gain_two, shift_two,
):
    t = lax.axis_index("tensor")
    local = hidden.shape[1]
    width = b_query.shape[0]
    inner = b_in.shape[0]
    own_kernels = lax.axis_size("dp") == 16 and lax.axis_size("tensor") == 2
    flip = [(0, 1), (1, 0)]

    def mine(a):
        return lax.dynamic_index_in_dim(a, t, 0, keepdims=False)

    def take(a):
        other = lax.dynamic_index_in_dim(a, 1 - t, 0, keepdims=False)
        return jnp.concatenate([mine(a), lax.ppermute(other, "tensor", flip)], 0)

    def give(a):
        got = lax.ppermute(a[local:], "tensor", flip)
        first = t == 0
        return jnp.stack([jnp.where(first, a[:local], got), jnp.where(first, got, a[:local])], 0)

    def gather(w):
        return lax.all_gather(lax.all_gather(w, "dp", axis=0, tiled=True), "tensor", axis=0)

    def scatter(g):
        g = lax.psum_scatter(g, "dp", scatter_dimension=1, tiled=True)
        return lax.psum_scatter(g, "tensor", scatter_dimension=0, tiled=False).astype(F32)

    def flat(w):
        return w.reshape(2, width, -1)

    length = jnp.stack([mine(lengths)[0], t * local]).astype(jnp.int32)
    shards = (w_query, w_key, w_value, w_out, w_in, w_back)
    if own_kernels:
        attended, lse, rows, query, key, value, *fulls = front(length, hidden, shards, b_query[None], b_value[None])
        fulls = [flat(w) for w in fulls]
        cotangent = lax.optimization_barrier((cotangent, attended))[0]
    else:
        rows = take(hidden)
        fulls = [gather(w) for w in shards]

        def project(w):
            return jnp.concatenate([nn(rows, w[0]), nn(rows, w[1])], 1)

        query = ((project(fulls[0]) + b_query) * 0.125).astype(BF16)
        key = project(fulls[1]).astype(BF16)
        value = (project(fulls[2]) + b_value).astype(BF16)
        attended, lse = attend_forward(length, query, key, value)
    full_query, full_key, full_value, full_out, full_in, full_back = fulls
    vec = jnp.stack([b_out, b_back, gain_one, shift_one, gain_two, shift_two, b_out, b_out])
    bi = b_in.reshape(2, 1, inner // 2)
    near_cot = mine(cotangent)
    far_cot = lax.ppermute(lax.dynamic_index_in_dim(cotangent, 1 - t, 0, keepdims=False), "tensor", flip)
    out, mid, v1, v2, act, gp = mlp_up(attended, rows, full_out, full_in, full_back, vec, bi)
    output = give(out)
    grad_one, grad_attended, g_out, g_in, g_back, small, g_b_in = mlp_down(
        length, attended, mid, near_cot, far_cot, v1, v2, full_out, full_in, full_back, act, gp, vec, bi
    )
    small = jnp.concatenate([small, g_b_in.reshape(-1, width), jnp.zeros((4, width), F32)])
    def split(g):
        return g.reshape(2, 4, 2, 2, -1, g.shape[-1])
    vb = 8 + inner // width
    if own_kernels:
        grad_hidden, small, *owned = back(
            length, query, key, value, grad_attended, attended, lse, rows, fulls[:3], grad_one, small, [split(g) for g in (g_out, g_in, g_back)]
        )
    else:
        d_query, d_key, d_value = attend_backward(length, query, key, value, grad_attended, attended, lse)
        total = grad_one
        grads = []
        for d, w in ((d_query, full_query), (d_key, full_key), (d_value, full_value)):
            total = total + nt(d, jnp.concatenate([w[0], w[1]], 1))
            g = tn(rows, d).astype(BF16)
            grads.append(jnp.stack([g[:, : width // 2], g[:, width // 2 :]]))
        small = small.at[vb].set(jnp.sum(d_query.astype(F32), 0)).at[vb + 1].set(jnp.sum(d_value.astype(F32), 0))
        grad_hidden = give(total.astype(BF16))
        owned = [scatter(g) for g in grads + [g_out, g_in, g_back]]
        small = lax.psum(small, ("dp", "tensor"))
    return (
        output, grad_hidden, *owned,
        small[vb], small[vb + 1], small[0], small[8:vb].reshape(inner), small[1], small[2], small[3], small[4], small[5],
    )


def solution(mesh):
    rows = P(None, ("dp", "tensor"), None)
    weight = P("dp", "tensor")
    return jax.shard_map(
        per_device,
        mesh=mesh,
        in_specs=(rows, P(None, "dp"), rows) + (weight,) * 6 + (P(),) * 9,
        out_specs=(rows, rows) + (weight,) * 6 + (P(),) * 9,
        check_vma=False,
    )
```

time: 381 us -> 292 us (0.77)
  Pallas kernels: 333 us -> 265 us
  matrix products: 19 us -> 0 us
    pallas_call x5 -> x4, Pallas kernels: 333 us -> 265 us  [the longest x1 117 us: back(): pl.pallas_call(kernel, grid=(pairs + 1,), in_specs=[SMALL] + [spec] * 6 +...]
    dot_general x12 -> x0, matrix products: 19 us -> none  [the longest x3 7.39 us: nt(): lax.dot_general(a, b, (((1,), (1,)), ((), ())), preferred_element_type=F32)]
    unnamed x72 -> x41, local copies, waits for them, and re-layouts: 9.97 us -> 6.75 us
  transfers between devices with their start and end apart: 0 -> 2, of which waited for: 0 -> 0; matrix products, arithmetic and copies ran while one was open for 0% -> 2% of each run, Pallas kernels for 0% -> 64%
where the time goes in v3:
time: 292 us; the launch traced here: 290 us
  Pallas kernels  265 us (91%)
  local copies, waits for them, and re-layouts  15.8 us (5%)
  other arithmetic  6.16 us (2%)
    pallas_call x1, Pallas kernels, back(): pl.pallas_call(kernel, grid=(pairs + 1,), in_specs=[SMALL] + [spec] * 6 +...  117 us
    pallas_call x1, Pallas kernels, front(): pl.pallas_call(kernel, grid=(1 + pairs,), in_specs=[SMALL, HBM] + [HBM] *...  80.5 us
    pallas_call x1, Pallas kernels, mlp_down(): pl.pallas_call(mlp_down_kernel, grid=(2 * m,), in_specs=[SMALL] + [whole(...  39 us
    pallas_call x1, Pallas kernels, mlp_up(): pl.pallas_call(functools.partial(mlp_up_kernel, chunk), grid=(total // ro...  28.3 us
    unnamed x41, local copies, waits for them, and re-layouts  6.75 us
  transfers between devices with their start and end apart: 2, of which 0 were waited for; matrix products, arithmetic and copies ran while one was open for 2% of the time, Pallas kernels for 64%

profile of v3, /device:TPU:0, one launch (start us, length us, event | category | flops | bytes accessed | tf_op | source)
XLA Modules:
  0.0 289.9 jit_solution(1118379537419608500)
XLA Ops:
  0.7 1.3 broadcast_in_dim.9.refs_8_
  1.9 1.3 broadcast_in_dim.10.refs_9_
  3.8 1.2 pad_add_fusion.refs_0_.len_ref
  5.0 80.5 %front.1 = (bf16[1024,768]{1,0:T(8,128)(2,1)}, f32[1024,768]{1,0:T(8,128)}, bf16[1024,768]{1,0:T(8,128)(2,1)}, bf16[1024,768]{1,0:T(8,128)(2,1)}, bf16[1024,768]...) custom-call(s32[2]{0:T(128)} %pad_add_fusion.refs_0_.len_ref, ...), custom_call_target="tpu_custom_call" | custom-call | flops 8053063680 | bytes 41943040 | tf_op jit(solution)/shard_map/front/pallas_call | solution.py:405
  85.6 1.0 dynamic-slice_bitcast_fusion
  86.7 0.8 collective-permute-start.1
  87.5 0.7 stack.46.vec_ref
  88.2 28.3 %mlp_up.1 = (bf16[1024,768]{1,0:T(8,128)(2,1)}, bf16[1024,768]{1,0:T(8,128)(2,1)}, f32[1024,768]{1,0:T(8,128)}, f32[1024,768]{1,0:T(8,128)}, bf16[2,1024,1536]{2...) custom-call(bf16[1024,768]{1,0:T(8,128)(2,1)} %get-tuple-element.51.a_ref.refs_5_, ...), custom_call_target="tpu_custom_call" | custom-call | flops 10871635968 | bytes 41943040 | tf_op jit(solution)/shard_map/mlp_up/pallas_call | solution.py:620
  116.5 1.2 slice.35
  117.7 1.3 collective-permute-start
  119.1 0.9 copy-done.16
  120.0 39.0 %mlp_down.1 = (f32[1024,768]{1,0:T(8,128)}, bf16[1024,768]{1,0:T(8,128)(2,1)}, bf16[2,768,384]{2,1,0:T(8,128)(2,1)}, bf16[2,768,1536]{2,1,0:T(8,128)(2,1)}, bf16...) custom-call(s32[2]{0:T(128)} %pad_add_fusion.refs_0_.len_ref, ...), custom_call_target="tpu_custom_call" | custom-call | flops 21743271936 | bytes 62914560 | tf_op jit(solution)/shard_map/mlp_down/pallas_call | solution.py:692
  159.0 0.7 reduce
  159.8 1.4 maximum_maximum_fusion.refs_12_
  161.2 116.9 %back.1 = (bf16[2,512,768]{2,1,0:T(8,128)(2,1)}, f32[16,768]{1,0:T(8,128)}, f32[48,384]{1,0:T(8,128)}, f32[48,384]{1,0:T(8,128)}, f32[48,384]{1,0:T(8,128)}, /*i...) custom-call(s32[2]{0:T(128)} %pad_add_fusion.refs_0_.len_ref, ...), custom_call_target="tpu_custom_call" | custom-call | flops 16106127360 | bytes 62914560 | tf_op jit(solution)/shard_map/back/pallas_call | solution.py:556
  278.1 0.7 slice.39
  279.5 1.6 slice_reduce_fusion
  281.1 1.5 select_bitcast_fusion.1
  282.6 1.3 pad_maximum_fusion
  283.9 0.7 copy-done.3
  284.6 1.1 copy.42
  285.8 0.6 copy.43
  288.3 0.7 copy.47
  289.0 0.7 copy.48
  (48 shorter events, 3.3 us)
Async XLA Ops:
  0.7 2.6 copy-start
  5.0 80.5 %copy-start.2 = (bf16[2,512,768]{2,1,0:T(8,128)(2,1)S(1)}, bf16[2,512,768]{2,1,0:T(8,128)(2,1)}, u32[]{:S(2)}) copy-start(bf16[2,512,768]{2,1,0:T(8,128)(2,1)} %param.20) | copy-start | bytes 4718596
  85.6 1.9 copy-start.10
  85.6 1.9 copy-start.11
  85.6 1.9 copy-start.12
  85.6 1.9 copy-start.13
  85.6 1.9 copy-start.14
  85.6 1.9 copy-start.15
  86.7 32.4 %collective-permute-start.1 = (bf16[512,768]{1,0:T(8,128)(2,1)S(1)}, bf16[512,768]{1,0:T(8,128)(2,1)S(1)}, u32[]{:S(2)}, u32[]{:S(2)}) collective-permute-start(bf16[512,768]{1,0:T(8,128)(2,1)S(1)} %get-tuple-element.95), channel_id=1, source_target_pairs={{0,1},{1,0},{2,3},{3,2},{4,5},{5,4},{6,7},{7,6},{8,9},{9,8},{10,11... | collective-permute-start | bytes 2359304 | tf_op jit(solution)/shard_map/ppermute | solution.py:759
  117.7 163.5 %collective-permute-start = (bf16[512,768]{1,0:T(8,128)(2,1)S(1)}, bf16[512,768]{1,0:T(8,128)(2,1)}, u32[]{:S(2)}, u32[]{:S(2)}) collective-permute-start(bf16[512,768]{1,0:T(8,128)(2,1)S(1)} %slice.35), channel_id=1, source_target_pairs={{0,1},{1,0},{2,3},{3,2},{4,5},{5,4},{6,7},{7,6},{8,9},{9,8},{10,11... | collective-permute-start | bytes 2359304 | tf_op jit(solution)/shard_map/ppermute | solution.py:724
  119.1 0.9 copy-start.16
  282.6 2.0 copy-start.3
  284.6 1.2 copy-start.9
  284.6 1.8 copy-start.8
  284.6 2.5 copy-start.7
  284.6 3.1 %copy-start.6 = (f32[48,384]{1,0:T(8,128)S(1)}, f32[48,384]{1,0:T(8,128)}, u32[]{:S(2)}) copy-start(f32[48,384]{1,0:T(8,128)} %get-tuple-element.119) | copy-start | bytes 221188
  284.6 3.7 %copy-start.5 = (f32[48,1536]{1,0:T(8,128)S(1)}, f32[48,1536]{1,0:T(8,128)}, u32[]{:S(2)}) copy-start(f32[48,1536]{1,0:T(8,128)} %get-tuple-element.120) | copy-start | bytes 884740
  284.6 4.4 %copy-start.4 = (f32[48,1536]{1,0:T(8,128)S(1)}, f32[48,1536]{1,0:T(8,128)}, u32[]{:S(2)}) copy-start(f32[48,1536]{1,0:T(8,128)} %get-tuple-element.121) | copy-start | bytes 884740
  284.6 5.1 %copy-start.1 = (s32[2,1]{0,1:T(1,128)S(1)}, s32[2,1]{0,1:T(1,128)}, u32[]{:S(2)}) copy-start(s32[2,1]{0,1:T(1,128)} %param.19) | copy-start | bytes 28

commit v4 on v3

--- a/solution.py
+++ b/solution.py
@@ -125,7 +125,10 @@
     z, x, c, t = place.z, place.x, place.c, place.t
     lanes = pl.ds(first, count)
     part = count // 256 * 128
-    low, high = pl.ds(0, part), pl.ds(part, count - part)
+    if part:
+        low, high = (slice(None), pl.ds(0, part)), (slice(None), pl.ds(part, count - part))
+    else:
+        low, high = (pl.ds(0, 16), slice(None)), (pl.ds(16, held.shape[3] - 16), slice(None))
     load = pltpu.make_async_copy(grad.at[:, :, :, c, :, lanes], held, local)
     def move(i, src, dst, peer):
         return remote(src, dst, send.at[i], recv.at[i], peer)
@@ -140,18 +143,18 @@
             c1, c2 = move(1, held.at[:, :, 1 - x], r1, place.across), move(2, held.at[1 - t, :, x], r2, place.beside)
             def add1(): add_blocks(8, lambda i: held.at[i // 4, i % 4, x], lambda i: r1.at[i // 4, i % 4])
         mine = lambda k: held.at[t, k, x]
-        c3 = move(3, held.at[t, place.far, x, :, low], r3.at[:, low], place.up)
-        c4 = move(4, held.at[t, place.far, x, :, high], r3.at[:, high], place.down)
+        c3 = move(3, held.at[(t, place.far, x) + low], r3.at[low], place.up)
+        c4 = move(4, held.at[(t, place.far, x) + high], r3.at[high], place.down)
         c5, c6 = move(5, mine(place.above), r4.at[0], place.up), move(6, mine(place.below), r4.at[1], place.down)
         def s1(): load.wait(); c0.wait_recv(); add_blocks(16, at3(held), at3(r0)); c1.start()
         def s2(): c1.wait_recv(); add1(); c2.start()
         def s3(): c2.wait_recv(); add_blocks(4, mine, lambda k: r2.at[k]); c3.start(); c4.start()
         def s4():
             c3.wait_recv()
-            v = held.at[t, place.above, x, :, low]; v[...] = (v[...].astype(F32) + r3[:, low].astype(F32)).astype(BF16)
+            v = held.at[(t, place.above, x) + low]; v[...] = (v[...].astype(F32) + r3[low].astype(F32)).astype(BF16)
             c5.start()
             c4.wait_recv()
-            v = held.at[t, place.below, x, :, high]; v[...] = (v[...].astype(F32) + r3[:, high].astype(F32)).astype(BF16)
+            v = held.at[(t, place.below, x) + high]; v[...] = (v[...].astype(F32) + r3[high].astype(F32)).astype(BF16)
             c6.start()
         def s5():
             c5.wait_recv(); c6.wait_recv()
@@ -187,65 +190,61 @@
     "k": (1, 0, 1, "zyx"),
     "v": (2, 0, 1, "yxz"),
     "o0": (3, 0, 1, "xyz"),
-    "i0": (4, 0, 4, "xyz"),
-    "i1": (4, 1, 4, "zxy"),
-    "i2": (4, 2, 4, "zxy"),
-    "i3": (4, 3, 4, "zxy"),
+    "i0": (4, 0, 2, "zxy"),
+    "i1": (4, 1, 2, "xyz"),
     "b0": (5, 0, 4, "zyx"),
-    "b1": (5, 1, 4, "xyz"),
+    "b1": (5, 1, 4, "zxy"),
     "b2": (5, 2, 4, "zyx"),
     "b3": (5, 3, 4, "zyx"),
 }
 BACK_ITEMS = {
-    "q": (0, 0, 1, "yxz"),
-    "k": (1, 0, 1, "xyz"),
-    "v": (2, 0, 1, "zxy"),
-    "o0": (3, 0, 1, "zyx"),
-    "i0": (4, 0, 4, "zxy"),
-    "i1": (4, 1, 4, "xyz"),
-    "i2": (4, 2, 4, "zyx"),
-    "i3": (4, 3, 4, "zyx"),
-    "b0": (5, 0, 4, "xyz"),
-    "b1": (5, 1, 4, "xyz"),
-    "b2": (5, 2, 4, "zxy"),
-    "b3": (5, 3, 4, "yxz"),
+    "m0": (0, 0, 1, "yxz"),
+    "m1": (1, 0, 1, "yxz"),
+    "mq": (2, 0, 3, "zyx"),
+    "mk": (2, 1, 3, "xyz"),
+    "mv": (2, 2, 3, "zyx"),
+    "o0": (3, 0, 1, "xyz"),
+    "i0": (4, 0, 2, "zxy"),
+    "i1": (4, 1, 2, "yxz"),
+    "b0": (5, 0, 2, "zxy"),
+    "b1": (5, 1, 2, "xyz"),
 }
 FRONT_ORDER = (
-    (("q", 0), ("v", 0), ("h1", 0), ("k", 0), ("v", 1), ("q", 1), ("b2", 0), ("k", 1), ("q", 2), ("v", 2), ("h1", 1), ("b2", 1), ("i1", 0), ("i0", 0), ("k", 2), ("i2", 0), ("b1", 0), ("h0", 0), ("h2", 0), ("h3", 0), ("o0", 0), ("i0", 1), ("q", 3), ("b1", 1), ("o0", 1), ("k", 3), ("v", 3), ("b3", 0), ("b2", 2), ("i1", 1), ("h0", 1), ("i2", 1), ("q", 4), ("v", 4), ("q", 5), ("h2", 1), ("b3", 1), ("i1", 2), ("i3", 0), ("v", 5), ("i2", 2), ("k", 4), ("b0", 0), ("b3", 2), ("h3", 1),),
-    (("k", 5),),
+    (("v", 0), ("q", 0), ("h1", 0), ("k", 0), ("b0", 0), ("v", 1), ("q", 1), ("k", 1), ("v", 2), ("b0", 1), ("i0", 0), ("q", 2), ("k", 2), ("h0", 0), ("i1", 0), ("b1", 0), ("o0", 0), ("h1", 1), ("b2", 0), ("b3", 0), ("q", 3), ("i1", 1), ("v", 3), ("o0", 1), ("b0", 2), ("k", 3), ("i0", 1), ("b1", 1), ("b2", 1), ("q", 4), ("b3", 1), ("h0", 1), ("q", 5),),
+    (("v", 4), ("i0", 2), ("i1", 2), ("k", 4), ("b1", 2), ("b2", 2), ("o0", 2), ("b3", 2), ("v", 5), ("k", 5),),
     (),
-    (("i1", 3), ("i0", 2), ("i2", 3), ("i3", 1), ("b0", 1), ("b1", 2), ("o0", 2), ("b2", 3),),
+    (("b0", 3),),
+    (("b2", 3), ("i0", 3),),
+    (("b1", 3), ("b3", 3),),
+    (("i1", 3),),
     (),
-    (("b3", 3),),
-    (("i0", 3), ("i3", 2), ("b0", 2), ("b2", 4),),
+    (("b0", 4),),
+    (("o0", 3),),
+    (("b2", 4), ("b0", 5), ("i0", 4),),
     (("i1", 4),),
-    (("b2", 5),),
-    (("i1", 5), ("b3", 4), ("i2", 4), ("b1", 3),),
-    (("b3", 5), ("i3", 3), ("b0", 3),),
-    (("i2", 5), ("o0", 3),),
-    (("i0", 4),),
-    (("i3", 4), ("b1", 4), ("i0", 5), ("b0", 4),),
-    (("i3", 5), ("o0", 4),),
-    (("b1", 5), ("b0", 5), ("o0", 5),),
+    (("b2", 5), ("i0", 5), ("b3", 4), ("o0", 4),),
+    (("i1", 5), ("b1", 4),),
+    (("o0", 5), ("b3", 5),),
+    (("b1", 5),),
 )
 BACK_ORDER = (
+    (("b0", 0),),
     (),
+    (("b0", 1),),
+    (("i1", 0),),
+    (("b0", 2), ("m0", 0), ("i1", 1), ("b1", 0), ("o0", 0),),
+    (("m0", 1),),
+    (("b1", 1), ("i0", 0), ("o0", 1),),
     (),
-    (("b0", 0),),
-    (("b0", 1),),
-    (("i2", 0), ("i0", 0), ("i3", 0), ("b2", 0),),
-    (("o0", 0), ("i2", 1), ("i0", 1), ("i3", 1), ("b0", 2), ("b2", 1),),
-    (("o0", 1), ("b3", 0), ("i2", 2), ("b0", 3),),
-    (("b1", 0), ("i1", 0), ("b3", 1), ("i0", 2), ("i3", 2),),
-    (("b1", 1), ("i1", 1), ("o0", 2), ("b2", 2),),
-    (("b3", 2),),
-    (("b1", 2), ("i2", 3), ("b0", 4),),
+    (("b0", 3), ("i1", 2), ("i0", 1),),
+    (("m0", 2), ("b1", 2), ("m1", 0),),
+    (("i0", 2),),
+    (("m1", 1), ("o0", 2), ("b0", 4), ("b1", 3),),
     (),
-    (("b1", 3), ("i1", 2), ("q", 0), ("b3", 3), ("i2", 4), ("i0", 3), ("i3", 3),),
-    (("k", 0), ("q", 1), ("i1", 3), ("sm", 0), ("o0", 3), ("i2", 5), ("i0", 4), ("k", 1), ("sm", 1), ("i3", 4),),
-    (("v", 0),),
-    (("r2", 0), ("v", 1), ("b1", 4), ("q", 2), ("o0", 4), ("k", 2), ("i1", 4), ("b3", 4), ("sm", 2), ("i0", 5), ("r0", 0), ("i3", 5), ("v", 2), ("r2", 1), ("b2", 3), ("b1", 5), ("q", 3), ("o0", 5), ("r3", 0), ("k", 3), ("i1", 5), ("sm", 3), ("b3", 5), ("r1", 0), ("b0", 5), ("b2", 4),),
-    (("r0", 1), ("v", 3), ("q", 4), ("k", 4), ("r3", 1), ("sm", 4), ("v", 4), ("q", 5), ("k", 5), ("r1", 1), ("sm", 5), ("b2", 5), ("v", 5),),
+    (("i1", 3), ("m1", 2),),
+    (("r1", 0), ("b0", 5), ("m0", 3), ("r0", 0), ("i1", 4), ("b1", 4), ("i0", 3), ("o0", 3), ("m1", 3),),
+    (("mq", 0), ("m0", 4), ("mv", 0), ("i1", 5), ("mk", 0),),
+    (("sm", 0), ("mq", 1), ("i0", 4), ("mv", 1), ("b1", 5), ("r1", 1), ("o0", 4), ("sm", 1), ("mk", 1), ("m1", 4), ("m0", 5), ("mq", 2), ("sm", 2), ("mv", 2), ("mk", 2), ("o0", 5), ("m1", 5), ("r0", 1), ("mq", 3), ("i0", 5), ("sm", 3), ("mv", 3), ("mk", 3), ("mq", 4), ("sm", 4), ("mk", 4), ("mv", 4), ("mq", 5), ("mv", 5), ("sm", 5), ("mk", 5),),
 )
 
 
@@ -266,7 +265,7 @@
     return [stage(i) for i in range(6)]
 
 
-def swap(away, into, send, recv, peer, parts=4):
+def swap(away, into, send, recv, peer, parts=2):
     size = away.shape[0] // parts
     plans = []
     for i in range(parts):
@@ -280,29 +279,29 @@
     return pl.BlockSpec(s, lambda i: (0,) * len(s), pipeline_mode=pl.Buffered(1))
 
 
+def live_rows(len_ref, rows):
+    t = lax.axis_index("tensor")
+    place = lax.broadcasted_iota(jnp.int32, (rows, 1), 0)
+    return (place + t * (rows // 2)) % rows < len_ref[t, 0]
+
+
 def forward_pair(bq, hook, len_ref, q_ref, k_ref, v_ref, o_ref, lse_ref):
     rows = q_ref.shape[0]
-    n = len_ref[0]
     lane = lax.broadcasted_iota(jnp.int32, (1, 128), 1)
-    krow = lax.broadcasted_iota(jnp.int32, (rows, 1), 0)
-    kbias = jnp.where((krow + len_ref[1]) % rows < n, 0.0, -1e9)
+    kbias = jnp.where(live_rows(len_ref, rows), 0.0, -1e9)
     first = lane < DH
-    for i in range(rows // bq):
-        if i % (rows // bq // 2) == 0:
-            hook(i * 2 * bq // rows)
-            k = k_ref[...].astype(F32)
-            v = v_ref[...]
-            kas = []
-            for h in range(2):
-                own = lane // DH == h
-                kas.append(jnp.where(own, k, jnp.where(lane == DH * (1 - h), kbias, 0.0)).astype(BF16))
-        place = pl.ds(i * bq, bq)
+
+    def block(i, _):
+        hook(i, rows // bq)
+        place = pl.ds(pl.multiple_of(i * bq, bq), bq)
         q = q_ref[place].astype(F32)
+        k, v = k_ref[...].astype(F32), v_ref[...]
         os_, ls = [], []
         for h in range(2):
-            own = lane // DH == h
-            qa = jnp.where(own, q, jnp.where(lane == DH * (1 - h), 1.0, 0.0)).astype(BF16)
-            s = nt(qa, kas[h])
+            own, spare = lane // DH == h, lane == DH * (1 - h)
+            qa = jnp.where(own, q, jnp.where(spare, 1.0, 0.0)).astype(BF16)
+            ka = jnp.where(own, k, jnp.where(spare, kbias, 0.0)).astype(BF16)
+            s = nt(qa, ka)
             m = jnp.max(s, axis=1, keepdims=True)
             p = jnp.exp(s - m)
             l = jnp.sum(p, axis=1, keepdims=True)
@@ -310,13 +309,16 @@
             ls.append(m + jnp.log(l))
         o_ref[place] = jnp.where(first, os_[0], os_[1]).astype(BF16)
         lse_ref[place] = jnp.where(first, ls[1], ls[0])
-
-
-def attend_forward(length, q, k, v, bq=256):
+        return 0
+
+    lax.fori_loop(0, rows // bq, block, 0)
+
+
+def attend_forward(length, q, k, v, bq=512):
     rows, width = q.shape
     spec = pl.BlockSpec((rows, 128), lambda i: (0, i))
     return pl.pallas_call(
-        functools.partial(forward_pair, bq, lambda i: None),
+        functools.partial(forward_pair, bq, lambda i, n: None),
         grid=(width // 128,),
         in_specs=[SMALL, spec, spec, spec],
         out_specs=[spec, spec],
@@ -331,30 +333,37 @@
         plans[name][stage]()
 
 
-def front(length, hidden, shards, b_query, b_value, bq=256):
+def front(length, hidden, shards, vec, bq=512):
     n = len(shards)
     rows, width = 2 * hidden.shape[1], hidden.shape[2]
     half, pairs = width // 2, width // 128
     items = [(name, w, shards[w].shape[1] // parts * i, shards[w].shape[1] // parts, order) for name, (w, i, parts, order) in FRONT_ITEMS.items()]
 
     def kernel(*refs):
-        len_ref, pair_ref, given, bq_ref, bv_ref = refs[0], refs[1], refs[2 : 2 + n], refs[2 + n], refs[3 + n]
+        len_ref, pair_ref, given, vec_ref = refs[0], refs[1], refs[2 : 2 + n], refs[2 + n]
+        refs = refs[3 + n :]
+        o_ref, lse_ref, outs, far_outs, mixed = refs[0], refs[1], refs[2:6], refs[6 : 3 + n], refs[3 + n]
         refs = refs[4 + n :]
-        o_ref, lse_ref, outs = refs[0], refs[1], refs[2 : 6 + n]
-        refs = refs[6 + n :]
-        rows_s, q_s, k_s, v_s, near, (send, recv, out_sem), sems = refs[0], refs[1], refs[2], refs[3], refs[4:7], refs[7:10], refs[10:]
+        rows_s, q_s, k_s, v_s, near, mix_s, (send, recv, out_sem), sems = refs[0], refs[1], refs[2], refs[3], refs[4:7], refs[7], refs[8:11], refs[11:]
         step = pl.program_id(0)
         place = Place()
-        fulls = list(near) + list(outs[7:])
+        fulls = list(near) + list(far_outs)
         local = rows // 2
-        keep = pltpu.make_async_copy(pair_ref.at[place.t], rows_s.at[pl.ds(0, local)], out_sem.at[7])
+        keep = pltpu.make_async_copy(pair_ref.at[place.t], rows_s.at[pl.ds(0, local)], out_sem.at[4])
         plans = {
             f"h{i}": plan
             for i, plan in enumerate(swap(pair_ref.at[1 - place.t], rows_s.at[pl.ds(local, local)], send, recv, place.beside))
         }
         for i, (name, w, at, count, order) in enumerate(items):
             plans[name] = gather_stages(place, order, given[w], fulls[w], at, count, *sems[3 * i : 3 * i + 3])
-        stores = [pltpu.make_async_copy(src, dst, out_sem.at[i]) for i, (src, dst) in enumerate(zip((rows_s, q_s, k_s, v_s) + tuple(near), outs))]
+        stores = [pltpu.make_async_copy(src, dst, out_sem.at[i]) for i, (src, dst) in enumerate(zip((rows_s, q_s, k_s, v_s), outs))]
+        stores.append(pltpu.make_async_copy(mix_s, mixed, out_sem.at[5]))
+
+        def turn(i):
+            for t in range(2):
+                w = near[i][t].reshape(width, half).T
+                for j in range(pairs // 2):
+                    mix_s[j, t, i * 128 : (i + 1) * 128] = w[j * 128 : (j + 1) * 128]
 
         def project(full, dst, bias, scale):
             def block(i, _):
@@ -373,19 +382,23 @@
             place.greet()
             run(plans, FRONT_ORDER[0])
             keep.wait()
-            project(near[0], q_s, bq_ref, 0.125)
+            project(near[0], q_s, vec_ref[6:7], 0.125)
             run(plans, FRONT_ORDER[1])
             project(near[1], k_s, None, 1.0)
             run(plans, FRONT_ORDER[2])
-            project(near[2], v_s, bv_ref, 1.0)
+            project(near[2], v_s, vec_ref[7:8], 1.0)
+            for i in range(3):
+                turn(i)
             for store in stores:
                 store.start()
 
-        def hook(part):
+        def hook(block, blocks):
             for i in range(pairs):
-                @pl.when(step == 1 + i)
-                def _():
-                    run(plans, FRONT_ORDER[3 + 2 * i + part])
+                for part in range(2):
+                    if FRONT_ORDER[3 + 2 * i + part]:
+                        @pl.when((step == 1 + i) & (block == part * (blocks // 2)))
+                        def _():
+                            run(plans, FRONT_ORDER[3 + 2 * i + part])
 
         @pl.when(step > 0)
         def _():
@@ -405,23 +418,21 @@
     return pl.pallas_call(
         kernel,
         grid=(1 + pairs,),
-        in_specs=[SMALL, HBM] + [HBM] * n + [whole((1, width))] * 2,
-        out_specs=[spec, spec] + [HBM] * (4 + n),
-        out_shape=[flat, S((rows, width), F32), flat, flat, flat, flat] + full,
-        scratch_shapes=[V((rows, width), BF16)] * 4 + [V(f.shape, BF16) for f in full[:3]] + [DMA((4,)), DMA((4,)), DMA((8,))]
+        in_specs=[SMALL, HBM] + [HBM] * n + [whole(vec.shape)],
+        out_specs=[spec, spec] + [HBM] * (2 + n),
+        out_shape=[flat, S((rows, width), F32), flat, flat, flat, flat] + full[3:] + [S((pairs // 2, 2, half, width), BF16)],
+        scratch_shapes=[V((rows, width), BF16)] * 4 + [V(f.shape, BF16) for f in full[:3]] + [V((pairs // 2, 2, half, width), BF16), DMA((4,)), DMA((4,)), DMA((6,))]
         + [s for _ in items for s in (DMA((7,)), DMA((7,)), DMA)],
         cost_estimate=pl.CostEstimate(flops=10 * rows * rows * width, bytes_accessed=40 << 20, transcendentals=rows * rows * 12),
         compiler_params=pltpu.CompilerParams(collective_id=1, has_side_effects=True, vmem_limit_bytes=56 << 20),
         name="front",
-    )(length, hidden, *shards, b_query, b_value)
+    )(length, hidden, *shards, vec)
 
 
 def backward_pair(bk, hook, len_ref, q_ref, k_ref, v_ref, d_ref, o_ref, lse_ref, dq_ref, dk_ref, dv_ref, qa_s, ka_s, va_s, da_s, acc):
     rows = q_ref.shape[0]
-    n = len_ref[0]
     lane = lax.broadcasted_iota(jnp.int32, (1, 128), 1)
-    krow = lax.broadcasted_iota(jnp.int32, (rows, 1), 0)
-    kbias = jnp.where((krow + len_ref[1]) % rows < n, 0.0, -1e9)
+    kbias = jnp.where(live_rows(len_ref, rows), 0.0, -1e9)
     d = d_ref[...].astype(F32)
     prod = d * o_ref[...].astype(F32)
     hi, mid, lo = split3(-lse_ref[...])
@@ -437,23 +448,25 @@
         va_s[h] = jnp.where(own, v_ref[...].astype(F32), pick(1.0, 1.0, 1.0, 0.0)).astype(BF16)
     first = lane < DH
     upper = lax.broadcasted_iota(jnp.int32, (128, 1), 0) < DH
-    for kb in range(0, rows, bk):
-        if kb % (rows // 2) == 0:
-            hook(kb * 2 // rows)
+    acc[...] = jnp.zeros_like(acc)
+
+    def block(b, _):
+        hook(b, rows // bk)
+        r = pl.ds(b * bk, bk)
         dks, dvs, dqs = [], [], []
         for h in range(2):
-            p = jnp.exp(nt(ka_s[h, kb : kb + bk], qa_s[h]))
-            ds = (p * nt(va_s[h, kb : kb + bk], da_s[h])).astype(BF16)
+            p = jnp.exp(nt(ka_s[h, r], qa_s[h]))
+            ds = (p * nt(va_s[h, r], da_s[h])).astype(BF16)
             dvs.append(nn(p.astype(BF16), d_ref[...]))
             dks.append(nn(ds, q_ref[...]))
-            dqs.append(tn(k_ref[kb : kb + bk], ds))
-        dk_ref[kb : kb + bk] = jnp.where(first, dks[0], dks[1]).astype(BF16)
-        dv_ref[kb : kb + bk] = jnp.where(first, dvs[0], dvs[1]).astype(BF16)
-        dq = jnp.where(upper, dqs[0], dqs[1])
-        if kb == 0:
-            acc[...] = dq
-        else:
-            acc[...] += dq
+            dqs.append(tn(k_ref[r], ds))
+        dk_ref[r] = jnp.where(first, dks[0], dks[1]).astype(BF16)
+        dv_ref[r] = jnp.where(first, dvs[0], dvs[1]).astype(BF16)
+        acc[...] += jnp.where(upper, dqs[0], dqs[1])
+        return 0
+
+    for b in range(rows // bk):
+        block(b, 0)
     dq_ref[...] = (acc[...].T * 0.125).astype(BF16)
 
 
@@ -462,11 +475,11 @@
     return [aug, aug, aug, aug, pltpu.VMEM((128, rows), F32)]
 
 
-def attend_backward(length, q, k, v, d, o, lse, bk=256):
+def attend_backward(length, q, k, v, d, o, lse, bk=512):
     rows, width = q.shape
     spec = pl.BlockSpec((rows, 128), lambda i: (0, i))
     return pl.pallas_call(
-        functools.partial(backward_pair, bk, lambda i: None),
+        functools.partial(backward_pair, bk, lambda i, n: None),
         grid=(width // 128,),
         in_specs=[SMALL] + [spec] * 6,
         out_specs=[spec] * 3,
@@ -477,22 +490,26 @@
     )(length, q, k, v, d, o, lse)
 
 
-def back(length, q, k, v, d, o, lse, rows_in, fulls, grad_one, small, grads, bk=256):
+def back(length, q, k, v, d, o, lse, rows_in, mixed, grad_one, small, grads, bk=512):
     n = len(grads)
     rows, width = q.shape
     half, pairs = width // 2, width // 128
-    shards = [(grads[0].shape[4], half)] * 3 + [g.shape[4:] for g in grads]
-    items = [(name, w, shards[w][1] // parts * i, shards[w][1] // parts, order) for name, (w, i, parts, order) in BACK_ITEMS.items()]
+    pieces = pairs // 2
+    shards = [(grads[0].shape[4], half)] * pieces + [g.shape[4:] for g in grads]
+    items = []
+    for name, (w, i, parts, order) in BACK_ITEMS.items():
+        items.append((name, w, shards[w][1] // parts * i, shards[w][1] // parts, order))
     vb = small.shape[0] - 4
 
     def kernel(*refs):
-        main_in, rows_ref, full, one_ref, small_ref, given = refs[:7], refs[7], refs[8:11], refs[11], refs[12], refs[13 : 13 + n]
-        refs = refs[13 + n :]
-        pair_ref, sum_ref, outs = refs[0], refs[1], refs[2 : 5 + n]
-        refs = refs[5 + n :]
-        dq_s, dk_s, dv_s, rT, gr_s = refs[:5]
-        own, part, got, fold_send, fold_recv, (send, recv, local_sem) = refs[5:8], refs[8], refs[9], refs[10], refs[11], refs[12:15]
-        main_scratch, scratch = refs[15:20], refs[20:]
+        main_in, rows_ref, mixed_ref, one_ref, small_ref, given = refs[:7], refs[7], refs[8], refs[9], refs[10], refs[11 : 11 + n]
+        refs = refs[11 + n :]
+        pair_ref, sum_ref, outs = refs[0], refs[1], refs[2 : 2 + pieces + n]
+        refs = refs[2 + pieces + n :]
+        cat, rT, total, gr_s, own = refs[:5]
+        refs = refs[5:]
+        part, got, fold_send, fold_recv, send, recv, local_sem = refs[:7]
+        main_scratch, scratch = refs[7:12], refs[12:]
         step = pl.program_id(0)
         place = Place()
         local = rows // 2
@@ -502,72 +519,121 @@
             for i, plan in enumerate(swap(gr_s.at[pl.ds(local, local)], pair_ref.at[place.t], send, recv, place.beside))
         }
         plans["sm"] = fold_stages(place, part, got, fold_send, fold_recv)
-        sources = list(own) + list(given)
+        sources = [own.at[p] for p in range(pieces)] + list(given)
         for i, (name, w, at, count, order) in enumerate(items):
             plans[name] = reduce_stages(place, order, sources[w], at, count, outs[w], scratch[9 * i : 9 * i + 9])
 
         @pl.when(step == 0)
         def _():
             place.greet()
-
-        def hook(j):
+            part[...] = small_ref[...]
+            total[...] = one_ref[...]
+            rT[...] = rows_ref[...].T
+
+        def at(i, j):
+            return 2 * i + j + i // 2
+
+        def hook(block, blocks):
             for i in range(pairs):
-                @pl.when(step == i)
+                for j in range(2):
+                    if BACK_ORDER[at(i, j)]:
+                        if block == j * (blocks // 2):
+                            @pl.when(step == i)
+                            def _():
+                                run(plans, BACK_ORDER[at(i, j)])
+
+        t = step % 2
+        backward_pair(bk, hook, *main_in, cat.at[t, :, pl.ds(0, 128)], cat.at[t, :, pl.ds(128, 128)], cat.at[t, :, pl.ds(256, 128)], *main_scratch)
+
+        def gather_rows(p, first):
+            r = slice(first, first + local)
+            v = total[r] + (nn(cat[0, r], mixed_ref[p, 0]) + nn(cat[1, r], mixed_ref[p, 1]))
+            total[r] = v
+            gr_s[r] = v.astype(BF16)
+
+        @pl.when(step % 2 == 1)
+        def _():
+            p = step // 2
+            last = step == pairs - 1
+            gather_rows(p, local)
+
+            @pl.when(last)
+            def _():
+                run(plans, BACK_ORDER[-3])
+
+            def weigh(t, _):
+                own[p, t] = nn(rT[...], cat[t]).astype(BF16).reshape(own.shape[2:])
+                sums = colsum(cat[t].astype(F32))
+                lanes = pl.ds(pl.multiple_of(t * half + p * 128, 128), 128)
+                part[vb : vb + 1, lanes] = sums[:, :128]
+                part[vb + 1 : vb + 2, lanes] = sums[:, 256:]
+                return 0
+            weigh(0, 0)
+            weigh(1, 0)
+            for i in range(pieces - 1):
+                @pl.when(step == 2 * i + 1)
                 def _():
-                    run(plans, BACK_ORDER[2 * i + j])
-
-        @pl.when(step < pairs)
+                    run(plans, BACK_ORDER[at(2 * i + 1, 2)])
+
+            @pl.when(last)
+            def _():
+                run(plans, BACK_ORDER[-2])
+            gather_rows(p, 0)
+
+        @pl.when(step == pairs - 1)
         def _():
-            cols = pl.ds(pl.multiple_of(step * 128, 128), 128)
-            backward_pair(bk, hook, *main_in, dq_s.at[:, cols], dk_s.at[:, cols], dv_s.at[:, cols], *main_scratch)
-
-        @pl.when(step == pairs)
-        def _():
-            at = 2 * pairs
-            rT[...] = rows_ref[...].T
-            part[...] = small_ref[...]
-            for i, d_s in enumerate((dq_s, dk_s, dv_s)):
-                for t in range(2):
-                    own[i][t] = nn(rT[...], d_s[:, t * half : (t + 1) * half]).astype(BF16).reshape(own[i].shape[1:])
-                if i == 0:
-                    part[vb : vb + 1] = colsum(dq_s[...].astype(F32))
-                    part[vb + 1 : vb + 2] = colsum(dv_s[...].astype(F32))
-                run(plans, BACK_ORDER[at + i])
-            for j in (1, 0):
-                def block(i, _):
-                    r = pl.ds(pl.multiple_of(i * 256, 256), 256)
-                    total = one_ref[r]
-                    for d_s, w in zip((dq_s, dk_s, dv_s), full):
-                        for t in range(2):
-                            total = total + nt(d_s[r, t * half : (t + 1) * half], w[t])
-                    gr_s[r] = total.astype(BF16)
-                    return 0
-                lax.fori_loop(j * (rows // 512), (j + 1) * (rows // 512), block, 0)
-                if j == 0:
-                    keep.start()
-                run(plans, BACK_ORDER[at + 4 - j])
+            keep.start()
+            run(plans, BACK_ORDER[-1])
+            sum_ref[...] = part[...]
             keep.wait()
-            sum_ref[...] = part[...]
-
-    spec = pl.BlockSpec((rows, 128), lambda i: (0, jnp.minimum(i, pairs - 1)))
+
+    spec = pl.BlockSpec((rows, 128), lambda i: (0, i % 2 * (pairs // 2) + i // 2))
     V = pltpu.VMEM
-    flat = V((rows, width), BF16)
     outs = [S(s, F32) for s in shards]
     return pl.pallas_call(
         kernel,
-        grid=(pairs + 1,),
-        in_specs=[SMALL] + [spec] * 6 + [whole((rows, width))] + [whole(f.shape) for f in fulls] + [whole((rows, width)), whole(small.shape)] + [HBM] * n,
+        grid=(pairs,),
+        in_specs=[SMALL] + [spec] * 6 + [whole((rows, width)), whole(mixed.shape), whole((rows, width)), whole(small.shape)] + [HBM] * n,
         out_specs=[HBM, whole(small.shape)] + [whole(s) for s in shards],
         out_shape=[S((2, rows // 2, width), BF16), S(small.shape, F32)] + outs,
-        scratch_shapes=[flat, flat, flat, V((width, rows), BF16), flat]
-        + [V((2, 4, 2, 2) + shards[0], BF16)] * 3
+        scratch_shapes=[V((2, rows, half), BF16), V((width, rows), BF16), V((rows, width), F32), V((rows, width), BF16)]
+        + [V((pieces, 2, 4, 2, 2) + shards[0], BF16)]
         + [V(small.shape, F32), V((5,) + small.shape, F32), DMA((5,)), DMA((5,)), DMA((4,)), DMA((4,)), DMA]
         + pair_scratch(rows)
         + [s for _, w, f, c, o in items for s in reduce_scratch(o, shards[w][0], c)],
         cost_estimate=pl.CostEstimate(flops=20 * rows * rows * width, bytes_accessed=60 << 20, transcendentals=rows * rows * 12),
         compiler_params=pltpu.CompilerParams(collective_id=2, has_side_effects=True, vmem_limit_bytes=63 << 20),
         name="back",
-    )(length, q, k, v, d, o, lse, rows_in, *fulls, grad_one, small, *grads)
+    )(length, q, k, v, d, o, lse, rows_in, mixed, grad_one, small, *grads)
+
+
+def finish(near_out, came_out, grad_hidden, owned):
+    local, width = near_out.shape
+    pieces = 3
+
+    def kernel(*refs):
+        near_ref, came_ref, grad_ref = refs[:3]
+        given, (out_ref, hid_ref), outs, sem = refs[3:9], refs[9:11], refs[11:17], refs[17]
+        t = lax.axis_index("tensor")
+        moves = [(near_ref, out_ref.at[t]), (came_ref, out_ref.at[1 - t]), (grad_ref, hid_ref)]
+        moves += list(zip(given[pieces:], outs[3:]))
+        for i in range(3):
+            for p in range(pieces):
+                moves.append((given[p].at[:, pl.ds(i * 128, 128)], outs[i].at[:, pl.ds(p * 128, 128)]))
+        copies = [pltpu.make_async_copy(a, b, sem.at[i]) for i, (a, b) in enumerate(moves)]
+        for copy in copies:
+            copy.start()
+        for copy in copies:
+            copy.wait()
+
+    return pl.pallas_call(
+        kernel,
+        in_specs=[pl.BlockSpec(memory_space=pltpu.VMEM)] * 9,
+        out_specs=[HBM] * 8,
+        out_shape=[S((2, local, width), BF16)] * 2 + [S(o.shape, F32) for o in owned],
+        scratch_shapes=[DMA((15,))],
+        name="finish",
+    )(near_out, came_out, grad_hidden, *owned)
 
 
 def norm_parts(v):
@@ -584,7 +650,7 @@
     return jnp.sum(v, axis=0, keepdims=True)
 
 
-def mlp_up_kernel(chunk, a_ref, h_ref, wo_ref, wi_ref, wb_ref, vec_ref, bi_ref, out_ref, mid_ref, v1_ref, v2_ref, act, gp, b2):
+def mlp_up_kernel(chunk, a_ref, h_ref, wo_ref, wi_ref, wb_ref, vec_ref, bi_ref, near_ref, far_ref, mid_ref, v1_ref, v2_ref, act, gp, b2):
     half, inner = wo_ref.shape[2], wi_ref.shape[2]
     b_out, b_back, gain_one, shift_one, gain_two, shift_two = [vec_ref[i : i + 1] for i in range(6)]
     v1 = h_ref[...].astype(F32) + (nt(a_ref[:, :half], wo_ref[0]) + nt(a_ref[:, half:], wo_ref[1])) + b_out
@@ -609,10 +675,19 @@
     lax.fori_loop(0, 2 * inner // chunk, up, 0)
     v2_ref[...] = b2[...]
     n2, r2 = norm_parts(b2[...])
-    out_ref[...] = (n2 * gain_two + shift_two).astype(BF16)
-
-
-def mlp_up(a, h, wo, wi, wb, vec, bi, rows=256, chunk=768):
+    out = (n2 * gain_two + shift_two).astype(BF16)
+    step, steps = pl.program_id(0), pl.num_programs(0)
+
+    @pl.when(step < steps // 2)
+    def _():
+        near_ref[...] = out
+
+    @pl.when(step >= steps // 2)
+    def _():
+        far_ref[...] = out
+
+
+def mlp_up(a, h, wo, wi, wb, vec, bi, rows=256, chunk=1536):
     total, width = a.shape
     inner = wi.shape[2]
     row = pl.BlockSpec((rows, width), lambda i: (i, 0))
@@ -621,8 +696,12 @@
         functools.partial(mlp_up_kernel, chunk),
         grid=(total // rows,),
         in_specs=[row, row] + [whole(s.shape) for s in (wo, wi, wb, vec, bi)],
-        out_specs=[row, row, row, row, wide, wide],
-        out_shape=[S((total, width), BF16), S((total, width), BF16), S((total, width), F32), S((total, width), F32), S((2, total, inner), BF16), S((2, total, inner), BF16)],
+        out_specs=[
+            pl.BlockSpec((rows, width), lambda i: (jnp.minimum(i, total // rows // 2 - 1), 0)),
+            pl.BlockSpec((rows, width), lambda i: (jnp.maximum(i - total // rows // 2, 0), 0)),
+            row, row, row, wide, wide,
+        ],
+        out_shape=[S((total // 2, width), BF16), S((total // 2, width), BF16), S((total, width), BF16), S((total, width), F32), S((total, width), F32), S((2, total, inner), BF16), S((2, total, inner), BF16)],
         scratch_shapes=[pltpu.VMEM((rows, width), F32)],
         cost_estimate=pl.CostEstimate(flops=total * width * (8 * inner + 2 * width), bytes_accessed=40 << 20, transcendentals=4 * total * inner),
         compiler_params=pltpu.CompilerParams(vmem_limit_bytes=60 << 20),
@@ -630,22 +709,24 @@
     )(a, h, wo, wi, wb, vec, bi)
 
 
-def mlp_down_kernel(len_ref, a_ref, mid_ref, near_ref, far_ref, v1_ref, v2_ref, wo_ref, vec_ref, wi_ref, wb_ref, act_ref, gp_ref,
-                    g1_ref, ga_ref, gwo_ref, gwi_ref, gwb_ref, small_ref, gbi_ref, back, btT, midT, gn):
+def mlp_down_kernel(len_ref, a_ref, mid_ref, cot_ref, far_ref, v1_ref, v2_ref, wo_ref, vec_ref, wi_ref, wb_ref, act_ref, gp_ref,
+                    g1_ref, ga_ref, gwo_ref, gwi_ref, gwb_ref, small_ref, back, btT, midT, gn, sums_s):
     step = pl.program_id(0)
-    rows, half, block = a_ref.shape[0], wo_ref.shape[2], 256
+    rows, half, chunk, block = a_ref.shape[0], wo_ref.shape[2], wi_ref.shape[2], 256
+    width = a_ref.shape[1]
     b_out, b_back, gain_one, shift_one, gain_two, shift_two = [vec_ref[i : i + 1] for i in range(6)]
 
     @pl.when(step == 0)
     def _():
         small_ref[...] = jnp.zeros_like(small_ref)
         midT[...] = mid_ref[...].T
+        live = jnp.where(live_rows(len_ref, rows), 1.0, 0.0)
+        near = cot_ref.at[lax.axis_index("tensor")]
         for b in range(rows // block):
             r = slice(b * block, (b + 1) * block)
             n2, r2 = norm_parts(v2_ref[r])
-            place = (b * block + lax.broadcasted_iota(jnp.int32, (block, 1), 0) + len_ref[1]) % rows
-            c = (near_ref if b < rows // block // 2 else far_ref)[(b * block) % (rows // 2) : (b * block) % (rows // 2) + block]
-            go = c.astype(F32) * jnp.where(place < len_ref[0], 1.0, 0.0)
+            at = (b * block) % (rows // 2)
+            go = (near if b < rows // block // 2 else far_ref)[at : at + block].astype(F32) * live[r]
             grad_two = norm_back(n2, r2, go * gain_two)
             bt = grad_two.astype(BF16)
             back[r] = bt
@@ -656,10 +737,16 @@
             small_ref[5:6] += colsum(go)
 
     gb = (nn(back[...], wb_ref[0]) * gp_ref[0].astype(F32)).astype(BF16)
-    gbi_ref[0] = colsum(gb.astype(F32))
+    sums = colsum(gb.astype(F32))
     gwb_ref[0] = nn(btT[...], act_ref[0]).astype(BF16)
     gwi_ref[0] = nn(midT[...], gb).astype(BF16)
     gn[...] += nt(gb, wi_ref[0])
+    sums_s[...] = sums
+    for j in range(half * 8 // chunk):
+        @pl.when(step == j)
+        def _():
+            for at in range(j * chunk, (j + 1) * chunk, 128):
+                small_ref[8 + at // width : 9 + at // width, at % width : at % width + 128] = sums_s[:, at - j * chunk : at - j * chunk + 128]
 
     @pl.when(step == pl.num_programs(0) - 1)
     def _():
@@ -681,25 +768,25 @@
             gwo_ref[t] = nn(btT[...], a_ref[:, t * half : (t + 1) * half]).astype(BF16)
 
 
-def mlp_down(length, a, mid, near, far, v1, v2, wo, wi, wb, act, gp, vec, bi, chunk=512):
+def mlp_down(length, a, mid, cot, far, v1, v2, wo, wi, wb, act, gp, vec, chunk=512):
     rows, width = a.shape
     inner = wi.shape[2]
     m = inner // chunk
     tall = pl.BlockSpec((1, rows, chunk), lambda i: (i // m, 0, i % m))
     weight = pl.BlockSpec((1, width, chunk), lambda i: (i // m, 0, i % m))
-    thin = pl.BlockSpec((1, 1, chunk), lambda i: (i // m, 0, i % m))
     V = pltpu.VMEM
+    small = (12 + 2 * inner // width, width)
     return pl.pallas_call(
         mlp_down_kernel,
         grid=(2 * m,),
-        in_specs=[SMALL] + [whole(s.shape) for s in (a, mid, near, far, v1, v2, wo, vec)] + [weight, weight, tall, tall],
-        out_specs=[whole((rows, width)), whole((rows, width)), whole(wo.shape), weight, weight, whole(vec.shape), thin],
-        out_shape=[S((rows, width), F32), S((rows, width), BF16), S(wo.shape, BF16), S(wi.shape, BF16), S(wb.shape, BF16), S(vec.shape, F32), S(bi.shape, F32)],
-        scratch_shapes=[V((rows, width), BF16), V((width, rows), BF16), V((width, rows), BF16), V((rows, width), F32)],
+        in_specs=[SMALL] + [whole(s.shape) for s in (a, mid, cot, far, v1, v2, wo, vec)] + [weight, weight, tall, tall],
+        out_specs=[whole((rows, width)), whole((rows, width)), whole(wo.shape), weight, weight, whole(small)],
+        out_shape=[S((rows, width), F32), S((rows, width), BF16), S(wo.shape, BF16), S(wi.shape, BF16), S(wb.shape, BF16), S(small, F32)],
+        scratch_shapes=[V((rows, width), BF16), V((width, rows), BF16), V((width, rows), BF16), V((rows, width), F32), V((1, chunk), F32)],
         cost_estimate=pl.CostEstimate(flops=rows * width * (16 * inner + 4 * width), bytes_accessed=60 << 20, transcendentals=0),
-        compiler_params=pltpu.CompilerParams(vmem_limit_bytes=60 << 20),
+        compiler_params=pltpu.CompilerParams(vmem_limit_bytes=62 << 20),
         name="mlp_down",
-    )(length, a, mid, near, far, v1, v2, wo, vec, wi, wb, act, gp)
+    )(length, a, mid, cot, far, v1, v2, wo, vec, wi, wb, act, gp)
 
 
 def per_device(
@@ -735,43 +822,41 @@
     def flat(w):
         return w.reshape(2, width, -1)
 
-    length = jnp.stack([mine(lengths)[0], t * local]).astype(jnp.int32)
+    vec = jnp.stack([b_out, b_back, gain_one, shift_one, gain_two, shift_two, b_query, b_value])
     shards = (w_query, w_key, w_value, w_out, w_in, w_back)
     if own_kernels:
-        attended, lse, rows, query, key, value, *fulls = front(length, hidden, shards, b_query[None], b_value[None])
-        fulls = [flat(w) for w in fulls]
-        cotangent = lax.optimization_barrier((cotangent, attended))[0]
+        attended, lse, rows, query, key, value, full_out, full_in, full_back, mixed = front(lengths, hidden, shards, vec)
+        full_out, full_in, full_back = flat(full_out), flat(full_in), flat(full_back)
+        late_cotangent = lax.optimization_barrier((cotangent, attended))[0]
     else:
+        late_cotangent = cotangent
         rows = take(hidden)
-        fulls = [gather(w) for w in shards]
+        full_query, full_key, full_value, full_out, full_in, full_back = [gather(w) for w in shards]
 
         def project(w):
             return jnp.concatenate([nn(rows, w[0]), nn(rows, w[1])], 1)
 
-        query = ((project(fulls[0]) + b_query) * 0.125).astype(BF16)
-        key = project(fulls[1]).astype(BF16)
-        value = (project(fulls[2]) + b_value).astype(BF16)
-        attended, lse = attend_forward(length, query, key, value)
-    full_query, full_key, full_value, full_out, full_in, full_back = fulls
-    vec = jnp.stack([b_out, b_back, gain_one, shift_one, gain_two, shift_two, b_out, b_out])
+        query = ((project(full_query) + b_query) * 0.125).astype(BF16)
+        key = project(full_key).astype(BF16)
+        value = (project(full_value) + b_value).astype(BF16)
+        attended, lse = attend_forward(lengths, query, key, value)
     bi = b_in.reshape(2, 1, inner // 2)
-    near_cot = mine(cotangent)
-    far_cot = lax.ppermute(lax.dynamic_index_in_dim(cotangent, 1 - t, 0, keepdims=False), "tensor", flip)
-    out, mid, v1, v2, act, gp = mlp_up(attended, rows, full_out, full_in, full_back, vec, bi)
-    output = give(out)
-    grad_one, grad_attended, g_out, g_in, g_back, small, g_b_in = mlp_down(
-        length, attended, mid, near_cot, far_cot, v1, v2, full_out, full_in, full_back, act, gp, vec, bi
+    far_cot = lax.ppermute(lax.dynamic_index_in_dim(late_cotangent, 1 - t, 0, keepdims=False), "tensor", flip)
+    near_out, far_out, mid, v1, v2, act, gp = mlp_up(attended, rows, full_out, full_in, full_back, vec, bi)
+    came_out = lax.ppermute(far_out, "tensor", flip)
+    grad_one, grad_attended, g_out, g_in, g_back, small = mlp_down(
+        lengths, attended, mid, cotangent, far_cot, v1, v2, full_out, full_in, full_back, act, gp, vec
     )
-    small = jnp.concatenate([small, g_b_in.reshape(-1, width), jnp.zeros((4, width), F32)])
     def split(g):
         return g.reshape(2, 4, 2, 2, -1, g.shape[-1])
     vb = 8 + inner // width
     if own_kernels:
         grad_hidden, small, *owned = back(
-            length, query, key, value, grad_attended, attended, lse, rows, fulls[:3], grad_one, small, [split(g) for g in (g_out, g_in, g_back)]
+            lengths, query, key, value, grad_attended, attended, lse, rows, mixed, grad_one, small, [split(g) for g in (g_out, g_in, g_back)]
         )
+        output, grad_hidden, *owned = finish(near_out, came_out, grad_hidden, owned)
     else:
-        d_query, d_key, d_value = attend_backward(length, query, key, value, grad_attended, attended, lse)
+        d_query, d_key, d_value = attend_backward(lengths, query, key, value, grad_attended, attended, lse)
         total = grad_one
         grads = []
         for d, w in ((d_query, full_query), (d_key, full_key), (d_value, full_value)):
@@ -779,6 +864,8 @@
             g = tn(rows, d).astype(BF16)
             grads.append(jnp.stack([g[:, : width // 2], g[:, width // 2 :]]))
         small = small.at[vb].set(jnp.sum(d_query.astype(F32), 0)).at[vb + 1].set(jnp.sum(d_value.astype(F32), 0))
+        first = t == 0
+        output = jnp.stack([jnp.where(first, near_out, came_out), jnp.where(first, came_out, near_out)], 0)
         grad_hidden = give(total.astype(BF16))
         owned = [scatter(g) for g in grads + [g_out, g_in, g_back]]
         small = lax.psum(small, ("dp", "tensor"))

time: 292 us -> 260 us (0.89)
  Pallas kernels: 265 us -> 244 us
  other arithmetic: 6.16 us -> 0 us
  local copies, waits for them, and re-layouts: 15.8 us -> 12.3 us
    pallas_call x1 -> x2, Pallas kernels: 117 us -> 104 us  [the longest x1 99.8 us: back(): pl.pallas_call(kernel, grid=(pairs,), in_specs=[SMALL] + [spec] * 6 + [wh...]
    another operation x7 -> x9, local copies, waits for them, and re-layouts: 0.68 us -> 6.16 us  [per_device(): jnp.stack([b_out, b_back, gain_one, shift_one, gain_two, shift_two, b_que...]
    pallas_call x1, Pallas kernels: 80.5 us -> 75.6 us  [front(): pl.pallas_call(kernel, grid=(1 + pairs,), in_specs=[SMALL, HBM] + [HBM] *...]
    another operation x3 -> x0, other arithmetic: 3.99 us -> none  [the longest x2 2.76 us: give(): jnp.stack([jnp.where(first, a[:local], got), jnp.where(first, got, a[:loc...]
    unnamed x41 -> x7, local copies, waits for them, and re-layouts: 6.75 us -> 3.09 us
  transfers between devices with their start and end apart: 2 -> 2, of which waited for: 0 -> 0; matrix products, arithmetic and copies ran while one was open for 2% -> 1% of each run, Pallas kernels for 64% -> 63%
where the time goes in v4:
time: 260 us
  Pallas kernels  244 us (94%)
  local copies, waits for them, and re-layouts  12.3 us (5%)
    pallas_call x1, Pallas kernels, back(): pl.pallas_call(kernel, grid=(pairs,), in_specs=[SMALL] + [spec] * 6 + [wh...  99.8 us
    pallas_call x1, Pallas kernels, front(): pl.pallas_call(kernel, grid=(1 + pairs,), in_specs=[SMALL, HBM] + [HBM] *...  75.6 us
    pallas_call x1, Pallas kernels, mlp_down(): pl.pallas_call(mlp_down_kernel, grid=(2 * m,), in_specs=[SMALL] + [whole(...  39.3 us
    pallas_call x1, Pallas kernels, mlp_up(): pl.pallas_call(functools.partial(mlp_up_kernel, chunk), grid=(total // ro...  25.6 us
    another operation x9, local copies, waits for them, and re-layouts, per_device(): jnp.stack([b_out, b_back, gain_one, shift_one, gain_two, shift_two, b_que...  6.16 us
  transfers between devices with their start and end apart: 2, of which 0 were waited for; matrix products, arithmetic and copies ran while one was open for 1% of the time, Pallas kernels for 63%

profile of v4, /device:TPU:0, one launch (start us, length us, event | category | flops | bytes accessed | tf_op | source)
XLA Modules:
  0.0 259.7 jit_solution(8957965287877689878)
XLA Ops:
  0.7 1.3 copy.35.refs_0_.len_ref
  2.0 0.7 stack.33
  2.6 0.7 stack.34
  3.3 0.7 stack.27
  4.0 0.7 stack.28
  4.7 0.7 stack.29
  5.4 0.7 stack.30
  6.1 0.7 stack.31
  6.8 0.7 stack.32
  7.5 0.6 stack.35.refs_8_.vec_ref
  8.1 75.6 %front.1 = (bf16[1024,768]{1,0:T(8,128)(2,1)}, f32[1024,768]{1,0:T(8,128)}, bf16[1024,768]{1,0:T(8,128)(2,1)}, bf16[1024,768]{1,0:T(8,128)(2,1)}, bf16[1024,768]...) custom-call(s32[2,1]{1,0:T(2,128)} %copy.35.refs_0_.len_ref, ...), custom_call_target="tpu_custom_call" | custom-call | flops 8053063680 | bytes 41943040 | tf_op jit(solution)/shard_map/front/pallas_call | solution.py:418
  83.7 0.1 dynamic-slice_bitcast_fusion
  83.8 1.5 collective-permute-start.1
  85.3 25.6 %mlp_up.1 = (bf16[512,768]{1,0:T(8,128)(2,1)}, bf16[512,768]{1,0:T(8,128)(2,1)}, bf16[1024,768]{1,0:T(8,128)(2,1)}, f32[1024,768]{1,0:T(8,128)}, f32[1024,768]{1...) custom-call(bf16[1024,768]{1,0:T(8,128)(2,1)} %get-tuple-element.57.a_ref.refs_5_, ...), custom_call_target="tpu_custom_call" | custom-call | flops 10871635968 | bytes 41943040 | tf_op jit(solution)/shard_map/mlp_up/pallas_call | solution.py:695
  110.9 0.6 collective-permute-start
  111.5 0.9 copy-done.2
  112.4 39.3 %mlp_down.1 = (f32[1024,768]{1,0:T(8,128)}, bf16[1024,768]{1,0:T(8,128)(2,1)}, bf16[2,768,384]{2,1,0:T(8,128)(2,1)}, bf16[2,768,1536]{2,1,0:T(8,128)(2,1)}, bf16...) custom-call(s32[2,1]{1,0:T(2,128)} %copy.35.refs_0_.len_ref, bf16[1024,768]{1,0:T(8,128)(2,1)} %get-tuple-element.57.a_ref.refs_5_, ...), custom_call_target="tpu_custom_call" | custom-call | flops 21743271936 | bytes 62914560 | tf_op jit(solution)/shard_map/mlp_down/pallas_call | solution.py:779
  151.7 99.8 %back.1 = (bf16[2,512,768]{2,1,0:T(8,128)(2,1)}, f32[16,768]{1,0:T(8,128)}, f32[48,384]{1,0:T(8,128)}, f32[48,384]{1,0:T(8,128)}, f32[48,384]{1,0:T(8,128)}, /*i...) custom-call(s32[2,1]{1,0:T(2,128)} %copy.35.refs_0_.len_ref, bf16[1024,768]{1,0:T(8,128)(2,1)} %get-tuple-element.64.refs_1_, ...), custom_call_target="tpu_custom_call" | custom-call | flops 16106127360 | bytes 62914560 | tf_op jit(solution)/shard_map/back/pallas_call | solution.py:593
  251.5 0.7 slice.30
  252.2 0.6 reshape.65
  252.9 1.6 slice_reduce_fusion
  254.5 0.0 collective-permute-done.refs_1_
  254.5 0.9 copy-done
  255.4 4.1 %finish.1 = (bf16[2,512,768]{2,1,0:T(8,128)(2,1)}, bf16[2,512,768]{2,1,0:T(8,128)(2,1)}, f32[48,384]{1,0:T(8,128)}, f32[48,384]{1,0:T(8,128)}, f32[48,384]{1,0:T...) custom-call(bf16[512,768]{1,0:T(8,128)(2,1)} %get-tuple-element.62.refs_0_, ...), custom_call_target="tpu_custom_call" | custom-call | tf_op jit(solution)/shard_map/finish/pallas_call | solution.py:629
  (5 shorter events, 0.0 us)
Async XLA Ops:
  8.1 75.6 %copy-start.1 = (bf16[2,512,768]{2,1,0:T(8,128)(2,1)S(1)}, bf16[2,512,768]{2,1,0:T(8,128)(2,1)}, u32[]{:S(2)}) copy-start(bf16[2,512,768]{2,1,0:T(8,128)(2,1)} %cot_ref.1) | copy-start | bytes 4718596
  83.8 27.7 %collective-permute-start.1 = (bf16[512,768]{1,0:T(8,128)(2,1)S(1)}, bf16[512,768]{1,0:T(8,128)(2,1)S(1)}, u32[]{:S(2)}, u32[]{:S(2)}) collective-permute-start(bf16[512,768]{1,0:T(8,128)(2,1)S(1)} %dynamic-slice_bitcast_fusion), channel_id=1, source_target_pairs={{0,1},{1,0},{2,3},{3,2},{4,5},{5,4},{6,7},{7,6},{8,9},{9,8},{10,11... | collective-permute-start | bytes 2359304 | tf_op jit(solution)/shard_map/ppermute | solution.py:844
  110.9 143.7 %collective-permute-start = (bf16[512,768]{1,0:T(8,128)(2,1)}, bf16[512,768]{1,0:T(8,128)(2,1)S(1)}, u32[]{:S(2)}, u32[]{:S(2)}) collective-permute-start(bf16[512,768]{1,0:T(8,128)(2,1)} %get-tuple-element.63), channel_id=1, source_target_pairs={{0,1},{1,0},{2,3},{3,2},{4,5},{5,4},{6,7},{7,6},{8,9},{9,8},{10,11... | collective-permute-start | bytes 2359304 | tf_op jit(solution)/shard_map/ppermute | solution.py:846
  111.5 0.9 copy-start.2
  254.5 0.9 copy-start

commit v5 on v4

--- a/solution.py
+++ b/solution.py
@@ -12,7 +12,7 @@
 DH = 64
 S = jax.ShapeDtypeStruct
 HBM = pl.BlockSpec(memory_space=pl.ANY)
-SMALL = pl.BlockSpec(memory_space=pltpu.SMEM)
+LENGTHS = pl.BlockSpec(memory_space=pltpu.VMEM)
 DMA = pltpu.SemaphoreType.DMA
 
 
@@ -44,12 +44,14 @@
         at = lambda z, x, c, t: ((z * 2 + x) * 2 + c, t)
         self.up, self.down = at(self.above, x, c, t), at(self.below, x, c, t)
         self.across, self.beside, self.twin = at(z, 1 - x, c, t), at(z, x, c, 1 - t), at(z, x, 1 - c, t)
-
-    def greet(self):
+        self.corner, self.opposite = at(z, 1 - x, c, 1 - t), at(self.far, x, c, t)
+        self.near = (self.up, self.down, self.across, self.beside, self.twin)
+
+    def greet(self, peers):
         barrier = pltpu.get_barrier_semaphore()
-        for peer in (self.up, self.down, self.across, self.beside, self.twin):
+        for peer in peers:
             pl.semaphore_signal(barrier, inc=1, device_id=peer, device_id_type=pl.DeviceIdType.MESH)
-        pl.semaphore_wait(barrier, 5)
+        pl.semaphore_wait(barrier, len(peers))
 
 
 def remote(src, dst, send, recv, peer):
@@ -114,10 +116,39 @@
 def reduce_scratch(order, rows, lanes):
     V = lambda *s: pltpu.VMEM(s + (rows, lanes), BF16)
     base = [V(2, 4, 2), V(2, 4, 2)]
-    if order == "yxz": base += [V(4, 2), V(4), V(), V(2)]
+    if order == "wide": base += [V(3, 4), V(3), V(), V()]
+    elif order == "yxz": base += [V(4, 2), V(4), V(), V(2)]
     elif order == "xyz": base += [V(2, 4), V(4), V(), V(2)]
     else: base += [V(2, 2), V(2, 2, 2), V(2), V()]
     return base + [pltpu.SemaphoreType.DMA((7,)), pltpu.SemaphoreType.DMA((7,)), pltpu.SemaphoreType.DMA]
+
+
+def wide_stages(place, load, c0, held, r0, r1, r2, out, lanes, move):
+    z, x, t = place.z, place.x, place.t
+    flat = [
+        move(1, held.at[t, :, 1 - x], r1.at[0], place.across),
+        move(2, held.at[1 - t, :, x], r1.at[1], place.beside),
+        move(3, held.at[1 - t, :, 1 - x], r1.at[2], place.corner),
+    ]
+    tall = [
+        move(4, held.at[t, place.above, x], r2.at[0], place.up),
+        move(5, held.at[t, place.below, x], r2.at[1], place.down),
+        move(6, held.at[t, place.far, x], r2.at[2], place.opposite),
+    ]
+    def block(ref): return lambda i: ref.at[i // 8, (i // 2) % 4, i % 2]
+    def s0(): load.start(); c0.start()
+    def s1():
+        load.wait(); c0.wait_recv(); add_blocks(16, block(held), block(r0))
+        for copy in flat: copy.start()
+    def s2():
+        for copy in flat: copy.wait_recv()
+        add_blocks(4, lambda k: held.at[t, k, x], *[lambda k, i=i: r1.at[i, k] for i in range(3)])
+        for copy in tall: copy.start()
+    def s3():
+        for copy in tall: copy.wait_recv()
+        out[:, lanes] = (held[t, z, x].astype(F32) + r2[2].astype(F32)) + (r2[0].astype(F32) + r2[1].astype(F32))
+        for copy in [c0] + flat + tall: copy.wait_send()
+    return [s0, s1, s2, s3]
 
 
 def reduce_stages(place, order, grad, first, count, out, scratch):
@@ -133,6 +164,8 @@
     def move(i, src, dst, peer):
         return remote(src, dst, send.at[i], recv.at[i], peer)
     c0 = move(0, grad.at[:, :, :, 1 - c, :, lanes], r0, place.twin)
+    if order == "wide":
+        return wide_stages(place, load, c0, held, r0, r1, r2, out, lanes, move)
     at3 = lambda ref: (lambda i: ref.at[i // 8, (i // 2) % 4, i % 2])
     def s0(): load.start(); c0.start()
     if order[0] != "z":
@@ -198,15 +231,15 @@
     "b3": (5, 3, 4, "zyx"),
 }
 BACK_ITEMS = {
-    "m0": (0, 0, 1, "yxz"),
+    "m0": (0, 0, 1, "xyz"),
     "m1": (1, 0, 1, "yxz"),
-    "mq": (2, 0, 3, "zyx"),
-    "mk": (2, 1, 3, "xyz"),
-    "mv": (2, 2, 3, "zyx"),
-    "o0": (3, 0, 1, "xyz"),
+    "mq": (2, 0, 3, "zxy"),
+    "mk": (2, 1, 3, "zxy"),
+    "mv": (2, 2, 3, "yxz"),
+    "o0": (3, 0, 1, "zxy"),
     "i0": (4, 0, 2, "zxy"),
-    "i1": (4, 1, 2, "yxz"),
-    "b0": (5, 0, 2, "zxy"),
+    "i1": (4, 1, 2, "xyz"),
+    "b0": (5, 0, 2, "yxz"),
     "b1": (5, 1, 2, "xyz"),
 }
 FRONT_ORDER = (
@@ -228,44 +261,39 @@
     (("b1", 5),),
 )
 BACK_ORDER = (
+    (("i0", 0), ("i1", 0), ("b1", 0),),
     (("b0", 0),),
+    (("i0", 1), ("i1", 1),),
+    (("b0", 1), ("b1", 1),),
+    (("i0", 2), ("m0", 0),),
     (),
-    (("b0", 1),),
-    (("i1", 0),),
-    (("b0", 2), ("m0", 0), ("i1", 1), ("b1", 0), ("o0", 0),),
-    (("m0", 1),),
-    (("b1", 1), ("i0", 0), ("o0", 1),),
+    (("i1", 2), ("m0", 1),),
+    (("b0", 2), ("o0", 0),),
     (),
-    (("b0", 3), ("i1", 2), ("i0", 1),),
-    (("m0", 2), ("b1", 2), ("m1", 0),),
-    (("i0", 2),),
-    (("m1", 1), ("o0", 2), ("b0", 4), ("b1", 3),),
+    (("o0", 1), ("i1", 3), ("i0", 3), ("b1", 2), ("m1", 0),),
     (),
-    (("i1", 3), ("m1", 2),),
-    (("r1", 0), ("b0", 5), ("m0", 3), ("r0", 0), ("i1", 4), ("b1", 4), ("i0", 3), ("o0", 3), ("m1", 3),),
-    (("mq", 0), ("m0", 4), ("mv", 0), ("i1", 5), ("mk", 0),),
-    (("sm", 0), ("mq", 1), ("i0", 4), ("mv", 1), ("b1", 5), ("r1", 1), ("o0", 4), ("sm", 1), ("mk", 1), ("m1", 4), ("m0", 5), ("mq", 2), ("sm", 2), ("mv", 2), ("mk", 2), ("o0", 5), ("m1", 5), ("r0", 1), ("mq", 3), ("i0", 5), ("sm", 3), ("mv", 3), ("mk", 3), ("mq", 4), ("sm", 4), ("mk", 4), ("mv", 4), ("mq", 5), ("mv", 5), ("sm", 5), ("mk", 5),),
+    (("o0", 2), ("m1", 1), ("m0", 2),),
+    (("b0", 3), ("i1", 4), ("b1", 3),),
+    (("i0", 4),),
+    (("b0", 4), ("r2", 0), ("o0", 3), ("i1", 5), ("m1", 2), ("m0", 3),),
+    (("mv", 0), ("i0", 5), ("b1", 4), ("mq", 0), ("mk", 0), ("o0", 4),),
+    (("b0", 5), ("m0", 4), ("mv", 1), ("r2", 1), ("sm", 0), ("mq", 1), ("mk", 1), ("m1", 3), ("r0", 0), ("o0", 5), ("b1", 5), ("sm", 1), ("m0", 5), ("mv", 2), ("mq", 2), ("r1", 0), ("r3", 0), ("mk", 2), ("m1", 4), ("r0", 1), ("mv", 3), ("mq", 3), ("sm", 2), ("mk", 3), ("mq", 4), ("m1", 5), ("mv", 4), ("r1", 1), ("mk", 4), ("sm", 3), ("mv", 5), ("r3", 1), ("mq", 5), ("mk", 5),),
 )
 
 
 def fold_stages(place, part, got, send, recv):
-    flip = place.z % 2
-    near = jax.tree.map(lambda u, d: u + flip * (d - u), place.up, place.down)
-    next_ = jax.tree.map(lambda u, d: d + flip * (u - d), place.up, place.down)
-    peers = (place.twin, place.across, place.beside, near, next_)
+    peers = (place.twin, place.across, place.beside, place.corner, place.up, place.down, place.opposite)
     copies = [remote(part, got.at[i], send.at[i], recv.at[i], peer) for i, peer in enumerate(peers)]
-    def stage(i):
-        def run():
-            if i > 0:
-                copies[i - 1].wait()
-                part[...] = part[...] + got[i - 1]
-            if i < 5:
-                copies[i].start()
-        return run
-    return [stage(i) for i in range(6)]
-
-
-def swap(away, into, send, recv, peer, parts=2):
+    def hop(first, last, old):
+        for copy in copies[old:first]: copy.wait()
+        if first == 1: part[...] = part[...] + got[0]
+        elif first == 4: part[...] = (part[...] + got[1]) + (got[2] + got[3])
+        elif first == 7: part[...] = (part[...] + got[6]) + (got[4] + got[5])
+        for copy in copies[first:last]: copy.start()
+    return [lambda: hop(0, 1, 0), lambda: hop(1, 4, 0), lambda: hop(4, 7, 1), lambda: hop(7, 7, 4)]
+
+
+def swap(away, into, send, recv, peer, parts):
     size = away.shape[0] // parts
     plans = []
     for i in range(parts):
@@ -282,7 +310,8 @@
 def live_rows(len_ref, rows):
     t = lax.axis_index("tensor")
     place = lax.broadcasted_iota(jnp.int32, (rows, 1), 0)
-    return (place + t * (rows // 2)) % rows < len_ref[t, 0]
+    length = jnp.where(t == 0, len_ref[0:1], len_ref[1:2])
+    return (place + t * (rows // 2)) % rows < length
 
 
 def forward_pair(bq, hook, len_ref, q_ref, k_ref, v_ref, o_ref, lse_ref):
@@ -320,7 +349,7 @@
     return pl.pallas_call(
         functools.partial(forward_pair, bq, lambda i, n: None),
         grid=(width // 128,),
-        in_specs=[SMALL, spec, spec, spec],
+        in_specs=[LENGTHS, spec, spec, spec],
         out_specs=[spec, spec],
         out_shape=[S((rows, width), BF16), S((rows, width), F32)],
         compiler_params=pltpu.CompilerParams(vmem_limit_bytes=56 << 20),
@@ -328,20 +357,24 @@
     )(length, q, k, v)
 
 
+def pieces_of(order, letter):
+    return len({name for phase in order for name, _ in phase if name[0] == letter})
+
+
 def run(plans, events):
     for name, stage in events:
         plans[name][stage]()
 
 
-def front(length, hidden, shards, vec, bq=512):
+def front(length, hidden, shards, b_query, b_value, bq=512):
     n = len(shards)
     rows, width = 2 * hidden.shape[1], hidden.shape[2]
     half, pairs = width // 2, width // 128
     items = [(name, w, shards[w].shape[1] // parts * i, shards[w].shape[1] // parts, order) for name, (w, i, parts, order) in FRONT_ITEMS.items()]
 
     def kernel(*refs):
-        len_ref, pair_ref, given, vec_ref = refs[0], refs[1], refs[2 : 2 + n], refs[2 + n]
-        refs = refs[3 + n :]
+        len_ref, pair_ref, given, bq_ref, bv_ref = refs[0], refs[1], refs[2 : 2 + n], refs[2 + n], refs[3 + n]
+        refs = refs[4 + n :]
         o_ref, lse_ref, outs, far_outs, mixed = refs[0], refs[1], refs[2:6], refs[6 : 3 + n], refs[3 + n]
         refs = refs[4 + n :]
         rows_s, q_s, k_s, v_s, near, mix_s, (send, recv, out_sem), sems = refs[0], refs[1], refs[2], refs[3], refs[4:7], refs[7], refs[8:11], refs[11:]
@@ -352,7 +385,7 @@
         keep = pltpu.make_async_copy(pair_ref.at[place.t], rows_s.at[pl.ds(0, local)], out_sem.at[4])
         plans = {
             f"h{i}": plan
-            for i, plan in enumerate(swap(pair_ref.at[1 - place.t], rows_s.at[pl.ds(local, local)], send, recv, place.beside))
+            for i, plan in enumerate(swap(pair_ref.at[1 - place.t], rows_s.at[pl.ds(local, local)], send, recv, place.beside, pieces_of(FRONT_ORDER, "h")))
         }
         for i, (name, w, at, count, order) in enumerate(items):
             plans[name] = gather_stages(place, order, given[w], fulls[w], at, count, *sems[3 * i : 3 * i + 3])
@@ -379,14 +412,14 @@
         @pl.when(step == 0)
         def _():
             keep.start()
-            place.greet()
+            place.greet(place.near)
             run(plans, FRONT_ORDER[0])
             keep.wait()
-            project(near[0], q_s, vec_ref[6:7], 0.125)
+            project(near[0], q_s, bq_ref[...].reshape(1, width), 0.125)
             run(plans, FRONT_ORDER[1])
             project(near[1], k_s, None, 1.0)
             run(plans, FRONT_ORDER[2])
-            project(near[2], v_s, vec_ref[7:8], 1.0)
+            project(near[2], v_s, bv_ref[...].reshape(1, width), 1.0)
             for i in range(3):
                 turn(i)
             for store in stores:
@@ -418,7 +451,7 @@
     return pl.pallas_call(
         kernel,
         grid=(1 + pairs,),
-        in_specs=[SMALL, HBM] + [HBM] * n + [whole(vec.shape)],
+        in_specs=[LENGTHS, HBM] + [HBM] * n + [whole((width,))] * 2,
         out_specs=[spec, spec] + [HBM] * (2 + n),
         out_shape=[flat, S((rows, width), F32), flat, flat, flat, flat] + full[3:] + [S((pairs // 2, 2, half, width), BF16)],
         scratch_shapes=[V((rows, width), BF16)] * 4 + [V(f.shape, BF16) for f in full[:3]] + [V((pairs // 2, 2, half, width), BF16), DMA((4,)), DMA((4,)), DMA((6,))]
@@ -426,7 +459,7 @@
         cost_estimate=pl.CostEstimate(flops=10 * rows * rows * width, bytes_accessed=40 << 20, transcendentals=rows * rows * 12),
         compiler_params=pltpu.CompilerParams(collective_id=1, has_side_effects=True, vmem_limit_bytes=56 << 20),
         name="front",
-    )(length, hidden, *shards, vec)
+    )(length, hidden, *shards, b_query, b_value)
 
 
 def backward_pair(bk, hook, len_ref, q_ref, k_ref, v_ref, d_ref, o_ref, lse_ref, dq_ref, dk_ref, dv_ref, qa_s, ka_s, va_s, da_s, acc):
@@ -481,7 +514,7 @@
     return pl.pallas_call(
         functools.partial(backward_pair, bk, lambda i, n: None),
         grid=(width // 128,),
-        in_specs=[SMALL] + [spec] * 6,
+        in_specs=[LENGTHS] + [spec] * 6,
         out_specs=[spec] * 3,
         out_shape=[S((rows, width), BF16)] * 3,
         scratch_shapes=pair_scratch(rows),
@@ -516,7 +549,7 @@
         keep = pltpu.make_async_copy(gr_s.at[pl.ds(0, local)], pair_ref.at[place.t], local_sem)
         plans = {
             f"r{i}": plan
-            for i, plan in enumerate(swap(gr_s.at[pl.ds(local, local)], pair_ref.at[place.t], send, recv, place.beside))
+            for i, plan in enumerate(swap(gr_s.at[pl.ds(local, local)], pair_ref.at[place.t], send, recv, place.beside, pieces_of(BACK_ORDER, "r")))
         }
         plans["sm"] = fold_stages(place, part, got, fold_send, fold_recv)
         sources = [own.at[p] for p in range(pieces)] + list(given)
@@ -525,7 +558,7 @@
 
         @pl.when(step == 0)
         def _():
-            place.greet()
+            place.greet(place.near + (place.corner, place.opposite))
             part[...] = small_ref[...]
             total[...] = one_ref[...]
             rT[...] = rows_ref[...].T
@@ -593,12 +626,12 @@
     return pl.pallas_call(
         kernel,
         grid=(pairs,),
-        in_specs=[SMALL] + [spec] * 6 + [whole((rows, width)), whole(mixed.shape), whole((rows, width)), whole(small.shape)] + [HBM] * n,
+        in_specs=[LENGTHS] + [spec] * 6 + [whole((rows, width)), whole(mixed.shape), whole((rows, width)), whole(small.shape)] + [HBM] * n,
         out_specs=[HBM, whole(small.shape)] + [whole(s) for s in shards],
         out_shape=[S((2, rows // 2, width), BF16), S(small.shape, F32)] + outs,
         scratch_shapes=[V((2, rows, half), BF16), V((width, rows), BF16), V((rows, width), F32), V((rows, width), BF16)]
         + [V((pieces, 2, 4, 2, 2) + shards[0], BF16)]
-        + [V(small.shape, F32), V((5,) + small.shape, F32), DMA((5,)), DMA((5,)), DMA((4,)), DMA((4,)), DMA]
+        + [V(small.shape, F32), V((7,) + small.shape, F32), DMA((7,)), DMA((7,)), DMA((4,)), DMA((4,)), DMA]
         + pair_scratch(rows)
         + [s for _, w, f, c, o in items for s in reduce_scratch(o, shards[w][0], c)],
         cost_estimate=pl.CostEstimate(flops=20 * rows * rows * width, bytes_accessed=60 << 20, transcendentals=rows * rows * 12),
@@ -650,9 +683,10 @@
     return jnp.sum(v, axis=0, keepdims=True)
 
 
-def mlp_up_kernel(chunk, a_ref, h_ref, wo_ref, wi_ref, wb_ref, vec_ref, bi_ref, near_ref, far_ref, mid_ref, v1_ref, v2_ref, act, gp, b2):
+def mlp_up_kernel(chunk, a_ref, h_ref, wo_ref, wi_ref, wb_ref, *refs):
+    vec_refs, (bi_ref, near_ref, far_ref, mid_ref, v1_ref, v2_ref, act, gp, b2) = refs[:6], refs[6:]
     half, inner = wo_ref.shape[2], wi_ref.shape[2]
-    b_out, b_back, gain_one, shift_one, gain_two, shift_two = [vec_ref[i : i + 1] for i in range(6)]
+    b_out, b_back, gain_one, shift_one, gain_two, shift_two = [ref[...].reshape(1, -1) for ref in vec_refs]
     v1 = h_ref[...].astype(F32) + (nt(a_ref[:, :half], wo_ref[0]) + nt(a_ref[:, half:], wo_ref[1])) + b_out
     v1_ref[...] = v1
     n1, r1 = norm_parts(v1)
@@ -695,7 +729,7 @@
     return pl.pallas_call(
         functools.partial(mlp_up_kernel, chunk),
         grid=(total // rows,),
-        in_specs=[row, row] + [whole(s.shape) for s in (wo, wi, wb, vec, bi)],
+        in_specs=[row, row] + [whole(s.shape) for s in (wo, wi, wb, *vec, bi)],
         out_specs=[
             pl.BlockSpec((rows, width), lambda i: (jnp.minimum(i, total // rows // 2 - 1), 0)),
             pl.BlockSpec((rows, width), lambda i: (jnp.maximum(i - total // rows // 2, 0), 0)),
@@ -706,15 +740,16 @@
         cost_estimate=pl.CostEstimate(flops=total * width * (8 * inner + 2 * width), bytes_accessed=40 << 20, transcendentals=4 * total * inner),
         compiler_params=pltpu.CompilerParams(vmem_limit_bytes=60 << 20),
         name="mlp_up",
-    )(a, h, wo, wi, wb, vec, bi)
-
-
-def mlp_down_kernel(len_ref, a_ref, mid_ref, cot_ref, far_ref, v1_ref, v2_ref, wo_ref, vec_ref, wi_ref, wb_ref, act_ref, gp_ref,
-                    g1_ref, ga_ref, gwo_ref, gwi_ref, gwb_ref, small_ref, back, btT, midT, gn, sums_s):
+    )(a, h, wo, wi, wb, *vec, bi)
+
+
+def mlp_down_kernel(len_ref, a_ref, mid_ref, cot_ref, far_ref, v1_ref, v2_ref, wo_ref, *refs):
+    vec_refs, (wi_ref, wb_ref, act_ref, gp_ref) = refs[:6], refs[6:10]
+    g1_ref, ga_ref, gwo_ref, gwi_ref, gwb_ref, small_ref, back, btT, midT, gn, sums_s = refs[10:]
     step = pl.program_id(0)
     rows, half, chunk, block = a_ref.shape[0], wo_ref.shape[2], wi_ref.shape[2], 256
     width = a_ref.shape[1]
-    b_out, b_back, gain_one, shift_one, gain_two, shift_two = [vec_ref[i : i + 1] for i in range(6)]
+    b_out, b_back, gain_one, shift_one, gain_two, shift_two = [ref[...].reshape(1, -1) for ref in vec_refs]
 
     @pl.when(step == 0)
     def _():
@@ -779,14 +814,14 @@
     return pl.pallas_call(
         mlp_down_kernel,
         grid=(2 * m,),
-        in_specs=[SMALL] + [whole(s.shape) for s in (a, mid, cot, far, v1, v2, wo, vec)] + [weight, weight, tall, tall],
+        in_specs=[LENGTHS] + [whole(s.shape) for s in (a, mid, cot, far, v1, v2, wo, *vec)] + [weight, weight, tall, tall],
         out_specs=[whole((rows, width)), whole((rows, width)), whole(wo.shape), weight, weight, whole(small)],
         out_shape=[S((rows, width), F32), S((rows, width), BF16), S(wo.shape, BF16), S(wi.shape, BF16), S(wb.shape, BF16), S(small, F32)],
         scratch_shapes=[V((rows, width), BF16), V((width, rows), BF16), V((width, rows), BF16), V((rows, width), F32), V((1, chunk), F32)],
         cost_estimate=pl.CostEstimate(flops=rows * width * (16 * inner + 4 * width), bytes_accessed=60 << 20, transcendentals=0),
         compiler_params=pltpu.CompilerParams(vmem_limit_bytes=62 << 20),
         name="mlp_down",
-    )(length, a, mid, cot, far, v1, v2, wo, vec, wi, wb, act, gp)
+    )(length, a, mid, cot, far, v1, v2, wo, *vec, wi, wb, act, gp)
 
 
 def per_device(
@@ -822,10 +857,10 @@
     def flat(w):
         return w.reshape(2, width, -1)
 
-    vec = jnp.stack([b_out, b_back, gain_one, shift_one, gain_two, shift_two, b_query, b_value])
+    vec = (b_out, b_back, gain_one, shift_one, gain_two, shift_two)
     shards = (w_query, w_key, w_value, w_out, w_in, w_back)
     if own_kernels:
-        attended, lse, rows, query, key, value, full_out, full_in, full_back, mixed = front(lengths, hidden, shards, vec)
+        attended, lse, rows, query, key, value, full_out, full_in, full_back, mixed = front(lengths, hidden, shards, b_query, b_value)
         full_out, full_in, full_back = flat(full_out), flat(full_in), flat(full_back)
         late_cotangent = lax.optimization_barrier((cotangent, attended))[0]
     else:

time: 260 us -> 250 us (0.962)
  local copies, waits for them, and re-layouts: 12.3 us -> 6.15 us
  Pallas kernels: 244 us -> 240 us
    another operation x9 -> x0, local copies, waits for them, and re-layouts: 6.16 us -> none  [per_device(): jnp.stack([b_out, b_back, gain_one, shift_one, gain_two, shift_two, b_que...]
    pallas_call x3, Pallas kernels: 215 us -> 211 us  [the longest x1 94.4 us: back(): pl.pallas_call(kernel, grid=(pairs,), in_specs=[LENGTHS] + [spec] * 6 + [...]
  transfers between devices with their start and end apart: 2 -> 2, of which waited for: 0 -> 0; matrix products, arithmetic and copies ran while one was open for 1% -> 1% of each run, Pallas kernels for 63% -> 64%
where the time goes in v5:
time: 250 us
  Pallas kernels  240 us (96%)
  local copies, waits for them, and re-layouts  6.15 us (2%)
    pallas_call x1, Pallas kernels, back(): pl.pallas_call(kernel, grid=(pairs,), in_specs=[LENGTHS] + [spec] * 6 + [...  94.4 us
    pallas_call x1, Pallas kernels, front(): pl.pallas_call(kernel, grid=(1 + pairs,), in_specs=[LENGTHS, HBM] + [HBM]...  76.6 us
    pallas_call x1, Pallas kernels, mlp_down(): pl.pallas_call(mlp_down_kernel, grid=(2 * m,), in_specs=[LENGTHS] + [whol...  39.5 us
    pallas_call x1, Pallas kernels, mlp_up(): pl.pallas_call(functools.partial(mlp_up_kernel, chunk), grid=(total // ro...  25.7 us
  transfers between devices with their start and end apart: 2, of which 0 were waited for; matrix products, arithmetic and copies ran while one was open for 1% of the time, Pallas kernels for 64%

profile of v5, /device:TPU:0, one launch (start us, length us, event | category | flops | bytes accessed | tf_op | source)
XLA Modules:
  0.0 249.6 jit_solution(13627713264849918654)
XLA Ops:
  0.7 1.3 copy.35.refs_0_.len_ref
  2.0 0.0 copy-start.1
  2.0 76.6 %front.1 = (bf16[1024,768]{1,0:T(8,128)(2,1)}, f32[1024,768]{1,0:T(8,128)}, bf16[1024,768]{1,0:T(8,128)(2,1)}, bf16[1024,768]{1,0:T(8,128)(2,1)}, bf16[1024,768]...) custom-call(s32[2,1]{1,0:T(2,128)} %copy.35.refs_0_.len_ref, ...), custom_call_target="tpu_custom_call" | custom-call | flops 8053063680 | bytes 41943040 | tf_op jit(solution)/shard_map/front/pallas_call | solution.py:451
  78.6 0.0 copy-done.1
  78.6 0.1 dynamic-slice_bitcast_fusion
  78.7 1.3 collective-permute-start.1
  80.0 25.7 %mlp_up.1 = (bf16[512,768]{1,0:T(8,128)(2,1)}, bf16[512,768]{1,0:T(8,128)(2,1)}, bf16[1024,768]{1,0:T(8,128)(2,1)}, f32[1024,768]{1,0:T(8,128)}, f32[1024,768]{1...) custom-call(bf16[1024,768]{1,0:T(8,128)(2,1)} %get-tuple-element.57.a_ref.refs_5_, ...), custom_call_target="tpu_custom_call" | custom-call | flops 10871635968 | bytes 41943040 | tf_op jit(solution)/shard_map/mlp_up/pallas_call | solution.py:729
  105.6 0.9 collective-permute-start
  106.5 0.0 collective-permute-done.1.far_ref
  106.5 0.0 copy-start.2
  106.5 0.9 copy-done.2
  107.4 39.5 %mlp_down.1 = (f32[1024,768]{1,0:T(8,128)}, bf16[1024,768]{1,0:T(8,128)(2,1)}, bf16[2,768,384]{2,1,0:T(8,128)(2,1)}, bf16[2,768,1536]{2,1,0:T(8,128)(2,1)}, bf16...) custom-call(s32[2,1]{1,0:T(2,128)} %copy.35.refs_0_.len_ref, bf16[1024,768]{1,0:T(8,128)(2,1)} %get-tuple-element.57.a_ref.refs_5_, ...), custom_call_target="tpu_custom_call" | custom-call | flops 21743271936 | bytes 62914560 | tf_op jit(solution)/shard_map/mlp_down/pallas_call | solution.py:814
  147.0 94.4 %back.1 = (bf16[2,512,768]{2,1,0:T(8,128)(2,1)}, f32[16,768]{1,0:T(8,128)}, f32[48,384]{1,0:T(8,128)}, f32[48,384]{1,0:T(8,128)}, f32[48,384]{1,0:T(8,128)}, /*i...) custom-call(s32[2,1]{1,0:T(2,128)} %copy.35.refs_0_.len_ref, bf16[1024,768]{1,0:T(8,128)(2,1)} %get-tuple-element.64.refs_1_, ...), custom_call_target="tpu_custom_call" | custom-call | flops 16106127360 | bytes 62914560 | tf_op jit(solution)/shard_map/back/pallas_call | solution.py:626
  241.4 0.7 slice.30
  242.1 0.6 reshape.65
  242.7 1.6 slice_reduce_fusion
  244.4 0.0 collective-permute-done.refs_1_
  244.4 0.0 copy-start
  244.4 0.9 copy-done
  245.3 4.1 %finish.1 = (bf16[2,512,768]{2,1,0:T(8,128)(2,1)}, bf16[2,512,768]{2,1,0:T(8,128)(2,1)}, f32[48,384]{1,0:T(8,128)}, f32[48,384]{1,0:T(8,128)}, f32[48,384]{1,0:T...) custom-call(bf16[512,768]{1,0:T(8,128)(2,1)} %get-tuple-element.62.refs_0_, ...), custom_call_target="tpu_custom_call" | custom-call | tf_op jit(solution)/shard_map/finish/pallas_call | solution.py:662
Async XLA Ops:
  2.0 76.6 %copy-start.1 = (bf16[2,512,768]{2,1,0:T(8,128)(2,1)S(1)}, bf16[2,512,768]{2,1,0:T(8,128)(2,1)}, u32[]{:S(2)}) copy-start(bf16[2,512,768]{2,1,0:T(8,128)(2,1)} %cot_ref.1) | copy-start | bytes 4718596
  78.7 27.9 %collective-permute-start.1 = (bf16[512,768]{1,0:T(8,128)(2,1)S(1)}, bf16[512,768]{1,0:T(8,128)(2,1)S(1)}, u32[]{:S(2)}, u32[]{:S(2)}) collective-permute-start(bf16[512,768]{1,0:T(8,128)(2,1)S(1)} %dynamic-slice_bitcast_fusion), channel_id=1, source_target_pairs={{0,1},{1,0},{2,3},{3,2},{4,5},{5,4},{6,7},{7,6},{8,9},{9,8},{10,11... | collective-permute-start | bytes 2359304 | tf_op jit(solution)/shard_map/ppermute | solution.py:879
  105.6 138.7 %collective-permute-start = (bf16[512,768]{1,0:T(8,128)(2,1)}, bf16[512,768]{1,0:T(8,128)(2,1)S(1)}, u32[]{:S(2)}, u32[]{:S(2)}) collective-permute-start(bf16[512,768]{1,0:T(8,128)(2,1)} %get-tuple-element.63), channel_id=1, source_target_pairs={{0,1},{1,0},{2,3},{3,2},{4,5},{5,4},{6,7},{7,6},{8,9},{9,8},{10,11... | collective-permute-start | bytes 2359304 | tf_op jit(solution)/shard_map/ppermute | solution.py:881
  106.5 0.9 copy-start.2
  244.4 0.9 copy-start

commit v6 on v5

--- a/solution.py
+++ b/solution.py
@@ -539,13 +539,17 @@
         refs = refs[11 + n :]
         pair_ref, sum_ref, outs = refs[0], refs[1], refs[2 : 2 + pieces + n]
         refs = refs[2 + pieces + n :]
-        cat, rT, total, gr_s, own = refs[:5]
-        refs = refs[5:]
+        cat, rT, total, gr_s, own, rows_s, mix_s, load_sem = refs[:8]
+        refs = refs[8:]
         part, got, fold_send, fold_recv, send, recv, local_sem = refs[:7]
         main_scratch, scratch = refs[7:12], refs[12:]
         step = pl.program_id(0)
         place = Place()
         local = rows // 2
+        loads = [
+            pltpu.make_async_copy(src, dst, load_sem.at[i])
+            for i, (src, dst) in enumerate(((rows_ref, rows_s), (one_ref, total), (mixed_ref, mix_s)))
+        ]
         keep = pltpu.make_async_copy(gr_s.at[pl.ds(0, local)], pair_ref.at[place.t], local_sem)
         plans = {
             f"r{i}": plan
@@ -560,8 +564,8 @@
         def _():
             place.greet(place.near + (place.corner, place.opposite))
             part[...] = small_ref[...]
-            total[...] = one_ref[...]
-            rT[...] = rows_ref[...].T
+            for load in loads:
+                load.start()
 
         def at(i, j):
             return 2 * i + j + i // 2
@@ -580,9 +584,15 @@
 
         def gather_rows(p, first):
             r = slice(first, first + local)
-            v = total[r] + (nn(cat[0, r], mixed_ref[p, 0]) + nn(cat[1, r], mixed_ref[p, 1]))
+            v = total[r] + (nn(cat[0, r], mix_s[p, 0]) + nn(cat[1, r], mix_s[p, 1]))
             total[r] = v
             gr_s[r] = v.astype(BF16)
+
+        @pl.when(step == 1)
+        def _():
+            for load in loads:
+                load.wait()
+            rT[...] = rows_s[...].T
 
         @pl.when(step % 2 == 1)
         def _():
@@ -626,11 +636,11 @@
     return pl.pallas_call(
         kernel,
         grid=(pairs,),
-        in_specs=[LENGTHS] + [spec] * 6 + [whole((rows, width)), whole(mixed.shape), whole((rows, width)), whole(small.shape)] + [HBM] * n,
+        in_specs=[LENGTHS] + [spec] * 6 + [HBM, HBM, HBM, whole(small.shape)] + [HBM] * n,
         out_specs=[HBM, whole(small.shape)] + [whole(s) for s in shards],
         out_shape=[S((2, rows // 2, width), BF16), S(small.shape, F32)] + outs,
         scratch_shapes=[V((2, rows, half), BF16), V((width, rows), BF16), V((rows, width), F32), V((rows, width), BF16)]
-        + [V((pieces, 2, 4, 2, 2) + shards[0], BF16)]
+        + [V((pieces, 2, 4, 2, 2) + shards[0], BF16), V((rows, width), BF16), V(mixed.shape, BF16), DMA((3,))]
         + [V(small.shape, F32), V((7,) + small.shape, F32), DMA((7,)), DMA((7,)), DMA((4,)), DMA((4,)), DMA]
         + pair_scratch(rows)
         + [s for _, w, f, c, o in items for s in reduce_scratch(o, shards[w][0], c)],
@@ -743,9 +753,10 @@
     )(a, h, wo, wi, wb, *vec, bi)
 
 
-def mlp_down_kernel(len_ref, a_ref, mid_ref, cot_ref, far_ref, v1_ref, v2_ref, wo_ref, *refs):
+def mlp_down_kernel(len_ref, a_hbm, mid_ref, cot_ref, far_ref, v1_hbm, v2_ref, wo_hbm, *refs):
     vec_refs, (wi_ref, wb_ref, act_ref, gp_ref) = refs[:6], refs[6:10]
-    g1_ref, ga_ref, gwo_ref, gwi_ref, gwb_ref, small_ref, back, btT, midT, gn, sums_s = refs[10:]
+    g1_ref, ga_ref, gwo_ref, gwi_ref, gwb_ref, small_ref, back, btT, midT, gn, sums_s, a_ref, v1_ref, wo_ref, load_sem = refs[10:]
+    loads = [pltpu.make_async_copy(src, dst, load_sem.at[i]) for i, (src, dst) in enumerate(((a_hbm, a_ref), (v1_hbm, v1_ref), (wo_hbm, wo_ref)))]
     step = pl.program_id(0)
     rows, half, chunk, block = a_ref.shape[0], wo_ref.shape[2], wi_ref.shape[2], 256
     width = a_ref.shape[1]
@@ -753,6 +764,8 @@
 
     @pl.when(step == 0)
     def _():
+        for load in loads:
+            load.start()
         small_ref[...] = jnp.zeros_like(small_ref)
         midT[...] = mid_ref[...].T
         live = jnp.where(live_rows(len_ref, rows), 1.0, 0.0)
@@ -785,6 +798,8 @@
 
     @pl.when(step == pl.num_programs(0) - 1)
     def _():
+        for load in loads:
+            load.wait()
         for b in range(rows // block):
             r = slice(b * block, (b + 1) * block)
             g = gn[r]
@@ -814,10 +829,11 @@
     return pl.pallas_call(
         mlp_down_kernel,
         grid=(2 * m,),
-        in_specs=[LENGTHS] + [whole(s.shape) for s in (a, mid, cot, far, v1, v2, wo, *vec)] + [weight, weight, tall, tall],
+        in_specs=[LENGTHS, HBM] + [whole(s.shape) for s in (mid, cot, far)] + [HBM, whole(v2.shape), HBM] + [whole(s.shape) for s in vec] + [weight, weight, tall, tall],
         out_specs=[whole((rows, width)), whole((rows, width)), whole(wo.shape), weight, weight, whole(small)],
         out_shape=[S((rows, width), F32), S((rows, width), BF16), S(wo.shape, BF16), S(wi.shape, BF16), S(wb.shape, BF16), S(small, F32)],
-        scratch_shapes=[V((rows, width), BF16), V((width, rows), BF16), V((width, rows), BF16), V((rows, width), F32), V((1, chunk), F32)],
+        scratch_shapes=[V((rows, width), BF16), V((width, rows), BF16), V((width, rows), BF16), V((rows, width), F32), V((1, chunk), F32)]
+        + [V(a.shape, BF16), V(v1.shape, F32), V(wo.shape, BF16), DMA((3,))],
         cost_estimate=pl.CostEstimate(flops=rows * width * (16 * inner + 4 * width), bytes_accessed=60 << 20, transcendentals=0),
         compiler_params=pltpu.CompilerParams(vmem_limit_bytes=62 << 20),
         name="mlp_down",

time: 250 us -> 246 us (0.984)
  Pallas kernels: 240 us -> 236 us
    pallas_call x1, Pallas kernels: 94.4 us -> 91.7 us  [back(): pl.pallas_call(kernel, grid=(pairs,), in_specs=[LENGTHS] + [spec] * 6 + [...]
  transfers between devices with their start and end apart: 2 -> 2, of which waited for: 0 -> 0; matrix products, arithmetic and copies ran while one was open for 1% -> 1% of each run, Pallas kernels for 64% -> 63%
where the time goes in v6:
time: 246 us; the launch traced here: 245 us
  Pallas kernels  236 us (96%)
  local copies, waits for them, and re-layouts  6.15 us (2%)
    pallas_call x1, Pallas kernels, back(): pl.pallas_call(kernel, grid=(pairs,), in_specs=[LENGTHS] + [spec] * 6 + [...  91.7 us
    pallas_call x1, Pallas kernels, front(): pl.pallas_call(kernel, grid=(1 + pairs,), in_specs=[LENGTHS, HBM] + [HBM]...  76.6 us
    pallas_call x1, Pallas kernels, mlp_down(): pl.pallas_call(mlp_down_kernel, grid=(2 * m,), in_specs=[LENGTHS, HBM] +...  37.8 us
    pallas_call x1, Pallas kernels, mlp_up(): pl.pallas_call(functools.partial(mlp_up_kernel, chunk), grid=(total // ro...  25.7 us
  transfers between devices with their start and end apart: 2, of which 0 were waited for; matrix products, arithmetic and copies ran while one was open for 1% of the time, Pallas kernels for 63%

profile of v6, /device:TPU:0, one launch (start us, length us, event | category | flops | bytes accessed | tf_op | source)
XLA Modules:
  0.0 245.3 jit_solution(5572654138216487882)
XLA Ops:
  0.7 1.3 copy.35.refs_0_.len_ref
  2.0 0.0 copy-start.1
  2.0 76.6 %front.1 = (bf16[1024,768]{1,0:T(8,128)(2,1)}, f32[1024,768]{1,0:T(8,128)}, bf16[1024,768]{1,0:T(8,128)(2,1)}, bf16[1024,768]{1,0:T(8,128)(2,1)}, bf16[1024,768]...) custom-call(s32[2,1]{1,0:T(2,128)} %copy.35.refs_0_.len_ref, ...), custom_call_target="tpu_custom_call" | custom-call | flops 8053063680 | bytes 41943040 | tf_op jit(solution)/shard_map/front/pallas_call | solution.py:451
  78.6 0.0 copy-done.1
  78.6 0.1 dynamic-slice_bitcast_fusion
  78.7 1.3 collective-permute-start.1
  80.0 25.7 %mlp_up.1 = (bf16[512,768]{1,0:T(8,128)(2,1)}, bf16[512,768]{1,0:T(8,128)(2,1)}, bf16[1024,768]{1,0:T(8,128)(2,1)}, f32[1024,768]{1,0:T(8,128)}, f32[1024,768]{1...) custom-call(bf16[1024,768]{1,0:T(8,128)(2,1)} %get-tuple-element.57.a_ref.a_hbm.refs_5_, ...), custom_call_target="tpu_custom_call" | custom-call | flops 10871635968 | bytes 41943040 | tf_op jit(solution)/shard_map/mlp_up/pallas_call | solution.py:739
  105.6 0.9 collective-permute-start
  106.5 0.0 collective-permute-done.1.far_ref
  106.5 0.0 copy-start.2
  106.5 0.9 copy-done.2
  107.4 37.8 %mlp_down.1 = (f32[1024,768]{1,0:T(8,128)}, bf16[1024,768]{1,0:T(8,128)(2,1)}, bf16[2,768,384]{2,1,0:T(8,128)(2,1)}, bf16[2,768,1536]{2,1,0:T(8,128)(2,1)}, bf16...) custom-call(s32[2,1]{1,0:T(2,128)} %copy.35.refs_0_.len_ref, bf16[1024,768]{1,0:T(8,128)(2,1)} %get-tuple-element.57.a_ref.a_hbm.refs_5_, ...), custom_call_target="tpu_custom_call" | custom-call | flops 21743271936 | bytes 62914560 | tf_op jit(solution)/shard_map/mlp_down/pallas_call | solution.py:829
  145.3 91.7 %back.1 = (bf16[2,512,768]{2,1,0:T(8,128)(2,1)}, f32[16,768]{1,0:T(8,128)}, f32[48,384]{1,0:T(8,128)}, f32[48,384]{1,0:T(8,128)}, f32[48,384]{1,0:T(8,128)}, /*i...) custom-call(s32[2,1]{1,0:T(2,128)} %copy.35.refs_0_.len_ref, bf16[1024,768]{1,0:T(8,128)(2,1)} %get-tuple-element.64.refs_1_, ...), custom_call_target="tpu_custom_call" | custom-call | flops 16106127360 | bytes 62914560 | tf_op jit(solution)/shard_map/back/pallas_call | solution.py:636
  237.0 0.7 slice.30
  237.8 0.6 reshape.65
  238.4 1.6 slice_reduce_fusion
  240.0 0.0 collective-permute-done.refs_1_
  240.0 0.0 copy-start
  240.0 0.9 copy-done
  240.9 4.1 %finish.1 = (bf16[2,512,768]{2,1,0:T(8,128)(2,1)}, bf16[2,512,768]{2,1,0:T(8,128)(2,1)}, f32[48,384]{1,0:T(8,128)}, f32[48,384]{1,0:T(8,128)}, f32[48,384]{1,0:T...) custom-call(bf16[512,768]{1,0:T(8,128)(2,1)} %get-tuple-element.62.refs_0_, ...), custom_call_target="tpu_custom_call" | custom-call | tf_op jit(solution)/shard_map/finish/pallas_call | solution.py:672
Async XLA Ops:
  2.0 76.6 %copy-start.1 = (bf16[2,512,768]{2,1,0:T(8,128)(2,1)S(1)}, bf16[2,512,768]{2,1,0:T(8,128)(2,1)}, u32[]{:S(2)}) copy-start(bf16[2,512,768]{2,1,0:T(8,128)(2,1)} %cot_ref.1) | copy-start | bytes 4718596
  78.7 27.9 %collective-permute-start.1 = (bf16[512,768]{1,0:T(8,128)(2,1)S(1)}, bf16[512,768]{1,0:T(8,128)(2,1)S(1)}, u32[]{:S(2)}, u32[]{:S(2)}) collective-permute-start(bf16[512,768]{1,0:T(8,128)(2,1)S(1)} %dynamic-slice_bitcast_fusion), channel_id=1, source_target_pairs={{0,1},{1,0},{2,3},{3,2},{4,5},{5,4},{6,7},{7,6},{8,9},{9,8},{10,11... | collective-permute-start | bytes 2359304 | tf_op jit(solution)/shard_map/ppermute | solution.py:895
  105.6 134.4 %collective-permute-start = (bf16[512,768]{1,0:T(8,128)(2,1)}, bf16[512,768]{1,0:T(8,128)(2,1)S(1)}, u32[]{:S(2)}, u32[]{:S(2)}) collective-permute-start(bf16[512,768]{1,0:T(8,128)(2,1)} %get-tuple-element.63), channel_id=1, source_target_pairs={{0,1},{1,0},{2,3},{3,2},{4,5},{5,4},{6,7},{7,6},{8,9},{9,8},{10,11... | collective-permute-start | bytes 2359304 | tf_op jit(solution)/shard_map/ppermute | solution.py:897
  106.5 0.9 copy-start.2
  240.0 0.9 copy-start

commit v7 on v6

--- a/solution.py
+++ b/solution.py
@@ -693,8 +693,15 @@
     return jnp.sum(v, axis=0, keepdims=True)
 
 
-def mlp_up_kernel(chunk, a_ref, h_ref, wo_ref, wi_ref, wb_ref, *refs):
-    vec_refs, (bi_ref, near_ref, far_ref, mid_ref, v1_ref, v2_ref, act, gp, b2) = refs[:6], refs[6:]
+def mlp_up_kernel(chunk, a_ref, h_ref, wo_ref, wi_hbm, wb_hbm, *refs):
+    vec_refs, (bi_ref, near_ref, far_ref, mid_ref, v1_ref, v2_ref, act, gp, b2, wi_ref, wb_ref, load_sem) = refs[:6], refs[6:]
+    loads = [pltpu.make_async_copy(src, dst, load_sem.at[i]) for i, (src, dst) in enumerate(((wi_hbm, wi_ref), (wb_hbm, wb_ref)))]
+
+    @pl.when(pl.program_id(0) == 0)
+    def _():
+        for load in loads:
+            load.start()
+
     half, inner = wo_ref.shape[2], wi_ref.shape[2]
     b_out, b_back, gain_one, shift_one, gain_two, shift_two = [ref[...].reshape(1, -1) for ref in vec_refs]
     v1 = h_ref[...].astype(F32) + (nt(a_ref[:, :half], wo_ref[0]) + nt(a_ref[:, half:], wo_ref[1])) + b_out
@@ -704,6 +711,11 @@
     mid = normed.astype(BF16)
     mid_ref[...] = mid
     b2[...] = normed + b_back
+
+    @pl.when(pl.program_id(0) == 0)
+    def _():
+        for load in loads:
+            load.wait()
 
     def up(i, _):
         t = i // (inner // chunk)
@@ -739,14 +751,14 @@
     return pl.pallas_call(
         functools.partial(mlp_up_kernel, chunk),
         grid=(total // rows,),
-        in_specs=[row, row] + [whole(s.shape) for s in (wo, wi, wb, *vec, bi)],
+        in_specs=[row, row, whole(wo.shape), HBM, HBM] + [whole(s.shape) for s in (*vec, bi)],
         out_specs=[
             pl.BlockSpec((rows, width), lambda i: (jnp.minimum(i, total // rows // 2 - 1), 0)),
             pl.BlockSpec((rows, width), lambda i: (jnp.maximum(i - total // rows // 2, 0), 0)),
             row, row, row, wide, wide,
         ],
         out_shape=[S((total // 2, width), BF16), S((total // 2, width), BF16), S((total, width), BF16), S((total, width), F32), S((total, width), F32), S((2, total, inner), BF16), S((2, total, inner), BF16)],
-        scratch_shapes=[pltpu.VMEM((rows, width), F32)],
+        scratch_shapes=[pltpu.VMEM((rows, width), F32), pltpu.VMEM(wi.shape, BF16), pltpu.VMEM(wb.shape, BF16), DMA((2,))],
         cost_estimate=pl.CostEstimate(flops=total * width * (8 * inner + 2 * width), bytes_accessed=40 << 20, transcendentals=4 * total * inner),
         compiler_params=pltpu.CompilerParams(vmem_limit_bytes=60 << 20),
         name="mlp_up",

time: 246 us -> 246 us (level)
  no operation moved by 1% of the time
where the time goes in v7:
time: 246 us; the launch traced here: 245 us
  Pallas kernels  236 us (96%)
  local copies, waits for them, and re-layouts  6.15 us (2%)
    pallas_call x1, Pallas kernels, back(): pl.pallas_call(kernel, grid=(pairs,), in_specs=[LENGTHS] + [spec] * 6 + [...  91.7 us
    pallas_call x1, Pallas kernels, front(): pl.pallas_call(kernel, grid=(1 + pairs,), in_specs=[LENGTHS, HBM] + [HBM]...  76.6 us
    pallas_call x1, Pallas kernels, mlp_down(): pl.pallas_call(mlp_down_kernel, grid=(2 * m,), in_specs=[LENGTHS, HBM] +...  37.9 us
    pallas_call x1, Pallas kernels, mlp_up(): pl.pallas_call(functools.partial(mlp_up_kernel, chunk), grid=(total // ro...  25.8 us
  transfers between devices with their start and end apart: 2, of which 0 were waited for; matrix products, arithmetic and copies ran while one was open for 1% of the time, Pallas kernels for 63%

profile of v7, /device:TPU:0, one launch (start us, length us, event | category | flops | bytes accessed | tf_op | source)
XLA Modules:
  0.0 245.4 jit_solution(14108568675409939297)
XLA Ops:
  0.7 1.3 copy.35.refs_0_.len_ref
  2.0 0.0 copy-start.1
  2.0 76.6 %front.1 = (bf16[1024,768]{1,0:T(8,128)(2,1)}, f32[1024,768]{1,0:T(8,128)}, bf16[1024,768]{1,0:T(8,128)(2,1)}, bf16[1024,768]{1,0:T(8,128)(2,1)}, bf16[1024,768]...) custom-call(s32[2,1]{1,0:T(2,128)} %copy.35.refs_0_.len_ref, ...), custom_call_target="tpu_custom_call" | custom-call | flops 8053063680 | bytes 41943040 | tf_op jit(solution)/shard_map/front/pallas_call | solution.py:451
  78.6 0.0 copy-done.1
  78.6 0.1 dynamic-slice_bitcast_fusion
  78.7 1.3 collective-permute-start.1
  80.0 25.8 %mlp_up.1 = (bf16[512,768]{1,0:T(8,128)(2,1)}, bf16[512,768]{1,0:T(8,128)(2,1)}, bf16[1024,768]{1,0:T(8,128)(2,1)}, f32[1024,768]{1,0:T(8,128)}, f32[1024,768]{1...) custom-call(bf16[1024,768]{1,0:T(8,128)(2,1)} %get-tuple-element.57.a_ref.a_hbm.refs_5_, ...), custom_call_target="tpu_custom_call" | custom-call | flops 10871635968 | bytes 41943040 | tf_op jit(solution)/shard_map/mlp_up/pallas_call | solution.py:751
  105.8 0.9 collective-permute-start
  106.6 0.0 collective-permute-done.1.far_ref
  106.6 0.0 copy-start.2
  106.6 0.9 copy-done.2
  107.5 37.9 %mlp_down.1 = (f32[1024,768]{1,0:T(8,128)}, bf16[1024,768]{1,0:T(8,128)(2,1)}, bf16[2,768,384]{2,1,0:T(8,128)(2,1)}, bf16[2,768,1536]{2,1,0:T(8,128)(2,1)}, bf16...) custom-call(s32[2,1]{1,0:T(2,128)} %copy.35.refs_0_.len_ref, bf16[1024,768]{1,0:T(8,128)(2,1)} %get-tuple-element.57.a_ref.a_hbm.refs_5_, ...), custom_call_target="tpu_custom_call" | custom-call | flops 21743271936 | bytes 62914560 | tf_op jit(solution)/shard_map/mlp_down/pallas_call | solution.py:841
  145.4 91.7 %back.1 = (bf16[2,512,768]{2,1,0:T(8,128)(2,1)}, f32[16,768]{1,0:T(8,128)}, f32[48,384]{1,0:T(8,128)}, f32[48,384]{1,0:T(8,128)}, f32[48,384]{1,0:T(8,128)}, /*i...) custom-call(s32[2,1]{1,0:T(2,128)} %copy.35.refs_0_.len_ref, bf16[1024,768]{1,0:T(8,128)(2,1)} %get-tuple-element.64.refs_1_, ...), custom_call_target="tpu_custom_call" | custom-call | flops 16106127360 | bytes 62914560 | tf_op jit(solution)/shard_map/back/pallas_call | solution.py:636
  237.1 0.7 slice.30
  237.9 0.6 reshape.65
  238.5 1.6 slice_reduce_fusion
  240.1 0.0 collective-permute-done.refs_1_
  240.1 0.0 copy-start
  240.1 0.9 copy-done
  241.0 4.1 %finish.1 = (bf16[2,512,768]{2,1,0:T(8,128)(2,1)}, bf16[2,512,768]{2,1,0:T(8,128)(2,1)}, f32[48,384]{1,0:T(8,128)}, f32[48,384]{1,0:T(8,128)}, f32[48,384]{1,0:T...) custom-call(bf16[512,768]{1,0:T(8,128)(2,1)} %get-tuple-element.62.refs_0_, ...), custom_call_target="tpu_custom_call" | custom-call | tf_op jit(solution)/shard_map/finish/pallas_call | solution.py:672
Async XLA Ops:
  2.0 76.6 %copy-start.1 = (bf16[2,512,768]{2,1,0:T(8,128)(2,1)S(1)}, bf16[2,512,768]{2,1,0:T(8,128)(2,1)}, u32[]{:S(2)}) copy-start(bf16[2,512,768]{2,1,0:T(8,128)(2,1)} %cot_ref.1) | copy-start | bytes 4718596
  78.7 28.0 %collective-permute-start.1 = (bf16[512,768]{1,0:T(8,128)(2,1)S(1)}, bf16[512,768]{1,0:T(8,128)(2,1)S(1)}, u32[]{:S(2)}, u32[]{:S(2)}) collective-permute-start(bf16[512,768]{1,0:T(8,128)(2,1)S(1)} %dynamic-slice_bitcast_fusion), channel_id=1, source_target_pairs={{0,1},{1,0},{2,3},{3,2},{4,5},{5,4},{6,7},{7,6},{8,9},{9,8},{10,11... | collective-permute-start | bytes 2359304 | tf_op jit(solution)/shard_map/ppermute | solution.py:907
  105.8 134.4 %collective-permute-start = (bf16[512,768]{1,0:T(8,128)(2,1)}, bf16[512,768]{1,0:T(8,128)(2,1)S(1)}, u32[]{:S(2)}, u32[]{:S(2)}) collective-permute-start(bf16[512,768]{1,0:T(8,128)(2,1)} %get-tuple-element.63), channel_id=1, source_target_pairs={{0,1},{1,0},{2,3},{3,2},{4,5},{5,4},{6,7},{7,6},{8,9},{9,8},{10,11... | collective-permute-start | bytes 2359304 | tf_op jit(solution)/shard_map/ppermute | solution.py:909
  106.6 0.9 copy-start.2
  240.1 0.9 copy-start
